TPU v7x, 128 devices: a whole 4x4x4 slice. The times are simulated.
128 devices in a mesh: row: 8 (over y, core), col: 16 (over x, z).
Axes of the slice: x: 4, y: 4, z: 4, core: 2. Of those that a mesh axis runs over, the one named last changes fastest.
Arguments:
- tokens: bfloat16 [2048, 8192], P('col', 'row'), may hold values from -6 to 6
- gate_weight: bfloat16 [8192, 28672], P('row', 'col'), may hold values from -0.109375 to 0.109375
- up_weight: bfloat16 [8192, 28672], P('row', 'col'), may hold values from -0.109375 to 0.109375
- down_weight: bfloat16 [28672, 8192], P('col', 'row'), may hold values from -0.0546875 to 0.0546875
- gate_keep: int32 [224, 48], P('col'), may hold values from 0 to 63, as said below
- gate_count: int32 [224], P('col'), may hold values from 5 to 48, as said below
- up_keep: int32 [224, 48], P('col'), may hold values from 0 to 63, as said below
- up_count: int32 [224], P('col'), may hold values from 5 to 48, as said below
- down_keep: int32 [64, 176], P('row'), may hold values from 0 to 223, as said below
- down_count: int32 [64], P('row'), may hold values from 15 to 176, as said below
Outputs:
- output_rows: bfloat16 [2048, 8192], P('col', 'row')
Inputs may be any that keep to these rules, and one draw needn't show every extreme that they name: `gate_keep`: each row holds distinct block indices of the model features. `gate_count`: some block column uses all 48 slots. `up_keep`: each row holds distinct block indices of the model features. `up_count`: some block column uses all 48 slots. `down_keep`: each row holds distinct block indices of the hidden units. `down_count`: some block column uses all 176 slots.
All inputs are finite; a program needn't handle non-finite values.
Results may differ from a plain program's by a relative error of at most 0.028.
Values may be sent and summed in bfloat16 or wider, within the bound.
A program may use at most 128 MiB of HBM per device.

v0:
```python
import jax
import jax.numpy as jnp
from jax import lax
from jax.sharding import PartitionSpec as P

BLOCK = 128
CHUNKS = 1
COL_A2A = True
COL_RING = False


def local_mask(keep_list, keep_count, offset, blocks):
    position = jnp.arange(keep_list.shape[1], dtype=jnp.int32)
    active_slot = position[None, :] < keep_count[:, None]
    local_index = keep_list - offset
    matches = (
        local_index[:, :, None] == jnp.arange(blocks, dtype=jnp.int32)[None, None, :]
    ) & active_slot[:, :, None]
    return jnp.any(matches, axis=1)


def apply_mask(weight, block_mask, block_size):
    block_rows, block_cols = block_mask.shape
    shaped = weight.reshape(block_rows, block_size, block_cols, block_size)
    masked = jnp.where(block_mask[:, None, :, None], shaped, jnp.zeros((), weight.dtype))
    return masked.reshape(weight.shape)


def row_perm(n_row, step):
    n_y = n_row // 2
    return [(y * 2 + c, ((y + step) % n_y) * 2 + c) for y in range(n_y) for c in range(2)]


def row_reduce_scatter(tokens, weights, n_row, after):
    n_y = n_row // 2
    r = lax.axis_index("row")
    y = r // 2
    core = r % 2
    rows = tokens.shape[0]
    width = weights.shape[1]
    halves = tokens.reshape(2, rows // 2, tokens.shape[1])
    send = lax.dynamic_index_in_dim(halves, 1 - core, 0, keepdims=False)
    keep = lax.dynamic_index_in_dim(halves, core, 0, keepdims=False)
    send = jnp.dot(send, weights, preferred_element_type=jnp.float32).astype(jnp.bfloat16)
    swap = [(i, i ^ 1) for i in range(n_row)]
    got = lax.ppermute(send, "row", swap)
    keep = jnp.dot(keep, weights, preferred_element_type=jnp.float32).astype(jnp.bfloat16)
    pair = (keep.astype(jnp.float32) + got.astype(jnp.float32)).astype(jnp.bfloat16)
    if after is not None:
        pair, after = lax.optimization_barrier((pair, after))
    chunk = rows // 2 // n_y
    pair = pair.reshape(n_y, chunk, width)
    results = []
    for direction, cols in ((1, slice(0, width // 2)), (-1, slice(width // 2, width))):
        own = pair[:, :, cols]
        index = (y - direction) % n_y
        acc = lax.dynamic_index_in_dim(own, index, 0, keepdims=False)
        for step in range(n_y - 1):
            got = lax.ppermute(acc.astype(jnp.bfloat16), "row", row_perm(n_row, direction))
            index = (index - direction) % n_y
            acc = got.astype(jnp.float32) + lax.dynamic_index_in_dim(own, index, 0, keepdims=False)
        results.append(acc)
    return results


def row_all_gather(value, n_row):
    n_y = n_row // 2
    r = lax.axis_index("row")
    y = r // 2
    core = r % 2
    chunk, width = value.shape
    parts = []
    for direction, cols in ((1, slice(0, width // 2)), (-1, slice(width // 2, width))):
        held = value[:, cols]
        full = jnp.zeros((n_y, chunk, width // 2), value.dtype)
        full = lax.dynamic_update_index_in_dim(full, held, y, 0)
        for step in range(n_y - 1):
            held = lax.ppermute(held, "row", row_perm(n_row, direction))
            full = lax.dynamic_update_index_in_dim(full, held, (y - direction * (step + 1)) % n_y, 0)
        parts.append(full)
    half = jnp.concatenate(parts, axis=2).reshape(n_y * chunk, width)
    swap = [(i, i ^ 1) for i in range(n_row)]
    other = lax.ppermute(half, "row", swap)
    both = jnp.zeros((2, n_y * chunk, width), value.dtype)
    both = lax.dynamic_update_index_in_dim(both, half, core, 0)
    both = lax.dynamic_update_index_in_dim(both, other, 1 - core, 0)
    return both.reshape(2 * n_y * chunk, width)


def ring_reduce_scatter(own, pos, n, perm_of):
    width = own.shape[2]
    halves = []
    for direction, cols in ((1, slice(0, width // 2)), (-1, slice(width // 2, width))):
        part = own[:, :, cols]
        index = (pos - direction) % n
        acc = lax.dynamic_index_in_dim(part, index, 0, keepdims=False).astype(jnp.float32)
        for step in range(n - 1):
            got = lax.ppermute(acc.astype(jnp.bfloat16), "col", perm_of(direction))
            index = (index - direction) % n
            acc = got.astype(jnp.float32) + lax.dynamic_index_in_dim(part, index, 0, keepdims=False)
        halves.append(acc)
    return jnp.concatenate(halves, axis=1)


def ring_all_gather(value, pos, n, perm_of):
    chunk, width = value.shape
    parts = []
    for direction, cols in ((1, slice(0, width // 2)), (-1, slice(width // 2, width))):
        held = value[:, cols]
        full = jnp.zeros((n, chunk, width // 2), value.dtype)
        full = lax.dynamic_update_index_in_dim(full, held, pos, 0)
        for step in range(n - 1):
            held = lax.ppermute(held, "col", perm_of(direction))
            full = lax.dynamic_update_index_in_dim(full, held, (pos - direction * (step + 1)) % n, 0)
        parts.append(full)
    return jnp.concatenate(parts, axis=2)


def col_axes(n_col):
    n_z = 4 if n_col % 4 == 0 else 1
    n_x = n_col // n_z
    c = lax.axis_index("col")

    def x_perm(d):
        return [(i * n_z + j, ((i + d) % n_x) * n_z + j) for i in range(n_x) for j in range(n_z)]

    def z_perm(d):
        return [(i * n_z + j, i * n_z + (j + d) % n_z) for i in range(n_x) for j in range(n_z)]

    return n_x, n_z, c // n_z, c % n_z, x_perm, z_perm


def col_all_gather(value, n_col):
    n_x, n_z, x, z, x_perm, z_perm = col_axes(n_col)
    rows, width = value.shape
    part = ring_all_gather(value, z, n_z, z_perm).reshape(n_z * rows, width)
    return ring_all_gather(part, x, n_x, x_perm).reshape(n_x * n_z * rows, width)


def col_reduce_scatter(terms, n_col):
    n_z = 4 if n_col % 4 == 0 else 1
    n_x = n_col // n_z
    c = lax.axis_index("col")
    x = c // n_z
    z = c % n_z
    rows, width = terms.shape

    def x_perm(d):
        return [(i * n_z + j, ((i + d) % n_x) * n_z + j) for i in range(n_x) for j in range(n_z)]

    def z_perm(d):
        return [(i * n_z + j, i * n_z + (j + d) % n_z) for i in range(n_x) for j in range(n_z)]

    part = ring_reduce_scatter(terms.reshape(n_x, rows // n_x, width), x, n_x, x_perm)
    part = part.astype(jnp.bfloat16).reshape(n_z, rows // n_x // n_z, width)
    return ring_reduce_scatter(part, z, n_z, z_perm).astype(jnp.bfloat16)


def on_device(
    tokens,
    gate_weight,
    up_weight,
    down_weight,
    gate_keep,
    gate_count,
    up_keep,
    up_count,
    down_keep,
    down_count,
):
    model_blocks = gate_weight.shape[0] // BLOCK
    hidden_blocks = gate_weight.shape[1] // BLOCK
    n_col = lax.axis_size("col")
    n_row = lax.axis_size("row")
    row_offset = lax.axis_index("row") * model_blocks
    col_offset = lax.axis_index("col") * hidden_blocks
    gate_pruned = apply_mask(
        gate_weight, local_mask(gate_keep, gate_count, row_offset, model_blocks).T, BLOCK
    )
    up_pruned = apply_mask(
        up_weight, local_mask(up_keep, up_count, row_offset, model_blocks).T, BLOCK
    )
    down_pruned = apply_mask(
        down_weight, local_mask(down_keep, down_count, col_offset, hidden_blocks).T, BLOCK
    )
    both_weights = jnp.concatenate([gate_pruned, up_pruned], axis=1)
    rows = tokens.shape[0] // CHUNKS
    gathered = lax.all_gather(tokens, "col", axis=0, tiled=True)
    gathered = gathered.reshape(n_col, CHUNKS, rows, gathered.shape[1])
    outs = []
    previous = None
    for k in range(CHUNKS):
        chunk = gathered[:, k].reshape(n_col * rows, gathered.shape[3])
        gate_sums, up_sums = row_reduce_scatter(chunk, both_weights, n_row, previous)
        hidden = (jax.nn.silu(gate_sums) * up_sums).astype(jnp.bfloat16)
        hidden = row_all_gather(hidden, n_row)
        terms = jnp.dot(hidden, down_pruned, preferred_element_type=jnp.float32).astype(
            jnp.bfloat16
        )
        previous = terms
        if COL_RING:
            outs.append(col_reduce_scatter(terms, n_col))
        elif COL_A2A and k == CHUNKS - 1:
            terms = terms.reshape(n_col, rows, terms.shape[1])
            terms = lax.all_to_all(terms, "col", 0, 0, tiled=False)
            outs.append(jnp.sum(terms.astype(jnp.float32), axis=0).astype(jnp.bfloat16))
        else:
            outs.append(lax.psum_scatter(terms, "col", scatter_dimension=0, tiled=True))
    return jnp.concatenate(outs, axis=0)


def solution(mesh):
    return jax.shard_map(
        on_device,
        mesh=mesh,
        in_specs=(
            P("col", "row"),
            P("row", "col"),
            P("row", "col"),
            P("col", "row"),
            P("col", None),
            P("col"),
            P("col", None),
            P("col"),
            P("row", None),
            P("row"),
        ),
        out_specs=P("col", "row"),
        check_vma=False,
    )
```

profile of v0, /device:TPU:0, one launch (start us, length us, event | category | flops | bytes accessed | tf_op | source)
XLA Modules:
  0.0 307.4 jit_solution(8252012016930296613)
XLA Ops:
  6.5 0.7 all-gather.2.cloned.1.call-update
  7.3 6.0 %copy.14 = bf16[1024,1792]{0,1:T(8,128)(2,1)} copy(bf16[1024,1792]{1,0:T(8,128)(2,1)} %param.12) | data formatting | bytes 7340032 | tf_op args[2]
  13.3 6.0 %copy.13 = bf16[1024,1792]{0,1:T(8,128)(2,1)} copy(bf16[1024,1792]{1,0:T(8,128)(2,1)} %param.11) | data formatting | bytes 7340032 | tf_op args[1]
  19.2 0.1 iota_compare_fusion.4
  19.3 0.3 fusion.16
  19.7 0.1 iota_compare_fusion.5
  19.8 0.3 fusion.14
  20.1 0.5 broadcast_in_dim.93
  20.6 5.2 %bitcast_select_fusion.1 = bf16[1024,1792]{0,1:T(8,128)(2,1)} fusion(bf16[1024,1792]{0,1:T(8,128)(2,1)} %copy.14, pred[224,8,8,128]{3,2,1,0:T(8,128)(4,1)S(1)} %bitcast.77), kind=kLoop, calls=%fused_computation.5 | loop fusion | flops 1835008 | bytes 9175040 | tf_op jit(solution)/shard_map/jit(_where)/select_n | solution.py:25
  25.8 0.5 broadcast_in_dim.90
  26.3 2.8 bitcast_select_fusion.2
  29.2 34.4 %all-gather.2.cloned.1.call-done = bf16[2048,1024]{1,0:T(8,128)(2,1)} async-done(((bf16[128,1024]{1,0:T(8,128)(2,1)}), bf16[2048,1024]{1,0:T(8,128)(2,1)}) %all-gather.2.cloned.1.call-update) | async-done | bytes 4194320 | tf_op jit(solution)/shard_map/all_gather | solution.py:188
  63.6 13.4 %convolution_convert_fusion = bf16[1024,3584]{1,0:T(8,128)(2,1)} fusion(bf16[1024,1792]{0,1:T(8,128)(2,1)} %bitcast_select_fusion.1, bf16[1024,1792]{0,1:T(8,128)(2,1)} %bitcast_select_fusion.2, bf16[2,1024,1024]{2,1,0:T(8,128)(2,1)} %bitcast.84, s32[]{:T(128)S(6)} %select_n.138), kind=kOutput, calls=%fused_computation.1 | convolution fusion | flops 7534542848 | bytes 16777220 | tf_op jit(solution)/shard_map/dot_general | solution.py:44
  77.0 12.0 %collective-permute-done = bf16[1024,3584]{1,0:T(8,128)(2,1)} collective-permute-done((bf16[1024,3584]{1,0:T(8,128)(2,1)}, bf16[1024,3584]{1,0:T(8,128)(2,1)}, u32[]{:S(2)}, u32[]{:S(2)}) %collective-permute-start) | collective-permute-done | bytes 7340064 | tf_op jit(solution)/shard_map/ppermute | solution.py:46
  89.0 14.5 %add_convert_fusion = bf16[1024,3584]{1,0:T(8,128)(2,1)} fusion(bf16[1024,3584]{1,0:T(8,128)(2,1)} %collective-permute-done, bf16[1024,1792]{0,1:T(8,128)(2,1)} %bitcast_select_fusion.1, bf16[1024,1792]{0,1:T(8,128)(2,1)} %bitcast_select_fusion.2, bf16[2,1024,1024]{2,1,0:T(8,128)(2,1)} %bitcast.85, s32[]{:T(128)S(6)} %select_n.135), kind=kOutput, calls=%fused_computation | convolution fusion | flops 7549222912 | bytes 24117252 | tf_op jit(solution)/shard_map/dot_general | solution.py:47
  103.4 5.4 %fusion.22 = (bf16[4,256,1792]{2,1,0:T(8,128)(2,1)S(1)}, bf16[4,256,1792]{2,1,0:T(8,128)(2,1)}) fusion(bf16[4,256,3584]{2,1,0:T(8,128)(2,1)} %bitcast.75), kind=kLoop, calls=%fused_computation.58 | loop fusion | bytes 14680064 | tf_op jit(solution)/shard_map/slice | solution.py:55
  108.9 1.9 copy-done
  110.7 0.1 dynamic-slice_bitcast_fusion.1
  110.8 1.6 collective-permute-start.1
  112.3 2.2 dynamic-slice_bitcast_fusion
  114.5 1.8 collective-permute-start.4
  116.3 18.2 %collective-permute-done.1 = bf16[256,1792]{1,0:T(8,128)(2,1)S(1)} collective-permute-done((bf16[256,1792]{1,0:T(8,128)(2,1)S(1)}, bf16[256,1792]{1,0:T(8,128)(2,1)S(1)}, u32[]{:S(2)}, u32[]{:S(2)}) %collective-permute-start.1) | collective-permute-done | bytes 917536 | tf_op jit(solution)/shard_map/ppermute | solution.py:59
  134.4 1.4 fusion.9
  135.8 0.3 collective-permute-start.2
  136.2 0.7 collective-permute-done.4
  136.9 2.4 fusion.7
  139.2 3.0 collective-permute-start.5
  142.2 16.4 %collective-permute-done.2 = bf16[256,1792]{1,0:T(8,128)(2,1)S(1)} collective-permute-done((bf16[256,1792]{1,0:T(8,128)(2,1)S(1)}, bf16[256,1792]{1,0:T(8,128)(2,1)S(1)}, u32[]{:S(2)}, u32[]{:S(2)}) %collective-permute-start.2) | collective-permute-done | bytes 917536 | tf_op jit(solution)/shard_map/ppermute | solution.py:59
  158.6 1.4 fusion.8
  160.0 0.1 collective-permute-start.3
  160.1 1.2 collective-permute-done.5
  161.3 2.7 fusion.6
  164.0 3.7 %collective-permute-start.6 = (bf16[256,1792]{1,0:T(8,128)(2,1)}, bf16[256,1792]{1,0:T(8,128)(2,1)S(1)}, u32[]{:S(2)}, u32[]{:S(2)}) collective-permute-start(bf16[256,1792]{1,0:T(8,128)(2,1)} %fusion.6), channel_id=1, source_target_pairs={{0,96},{16,112},{32,0},{48,16},{64,32},{80,48},{96,64},{112,80},{1... | collective-permute-start | bytes 2752520 | tf_op jit(solution)/shard_map/ppermute | solution.py:59
  167.6 14.3 %collective-permute-done.3 = bf16[256,1792]{1,0:T(8,128)(2,1)S(1)} collective-permute-done((bf16[256,1792]{1,0:T(8,128)(2,1)S(1)}, bf16[256,1792]{1,0:T(8,128)(2,1)S(1)}, u32[]{:S(2)}, u32[]{:S(2)}) %collective-permute-start.3) | collective-permute-done | bytes 917536 | tf_op jit(solution)/shard_map/ppermute | solution.py:59
  182.0 3.9 %collective-permute-done.6 = bf16[256,1792]{1,0:T(8,128)(2,1)S(1)} collective-permute-done((bf16[256,1792]{1,0:T(8,128)(2,1)}, bf16[256,1792]{1,0:T(8,128)(2,1)S(1)}, u32[]{:S(2)}, u32[]{:S(2)}) %collective-permute-start.6) | collective-permute-done | bytes 917536 | tf_op jit(solution)/shard_map/ppermute | solution.py:59
  185.9 2.2 fusion.5
  188.1 0.1 fusion.23
  188.2 0.1 collective-permute-start.7
  188.2 3.7 %collective-permute-start.10 = (bf16[256,896]{1,0:T(8,128)(2,1)S(1)}, bf16[256,896]{1,0:T(8,128)(2,1)S(1)}, u32[]{:S(2)}, u32[]{:S(2)}) collective-permute-start(bf16[256,896]{1,0:T(8,128)(2,1)S(1)} %get-tuple-element.8), channel_id=1, source_target_pairs={{0,96},{16,112},{32,0},{48,16},{64,32},{80,48},{96,64},{112,80},{1... | collective-permute-start | bytes 1376264 | tf_op jit(solution)/shard_map/ppermute | solution.py:78
  191.9 0.1 broadcast.73.clone.1
  192.0 0.1 bitcast_dynamic-update-slice_fusion.9
  192.1 0.1 broadcast.73.clone
  192.3 0.1 bitcast_dynamic-update-slice_fusion.5
  192.3 7.5 %collective-permute-done.7 = bf16[256,896]{1,0:T(8,128)(2,1)S(1)} collective-permute-done((bf16[256,896]{1,0:T(8,128)(2,1)S(1)}, bf16[256,896]{1,0:T(8,128)(2,1)S(1)}, u32[]{:S(2)}, u32[]{:S(2)}) %collective-permute-start.7) | collective-permute-done | bytes 458784 | tf_op jit(solution)/shard_map/ppermute | solution.py:78
  199.8 3.2 %collective-permute-start.11 = (bf16[256,896]{1,0:T(8,128)(2,1)S(1)}, bf16[256,896]{1,0:T(8,128)(2,1)S(1)}, u32[]{:S(2)}, u32[]{:S(2)}) collective-permute-start(bf16[256,896]{1,0:T(8,128)(2,1)S(1)} %collective-permute-done.10), channel_id=1, source_target_pairs={{0,96},{16,112},{32,0},{48,16},{64,32},{80,48},{96,64},{112,80},{1... | collective-permute-start | bytes 1376264 | tf_op jit(solution)/shard_map/ppermute | solution.py:78
  203.1 0.1 bitcast_dynamic-update-slice_fusion.4
  203.1 7.3 %collective-permute-done.8 = bf16[256,896]{1,0:T(8,128)(2,1)S(1)} collective-permute-done((bf16[256,896]{1,0:T(8,128)(2,1)S(1)}, bf16[256,896]{1,0:T(8,128)(2,1)S(1)}, u32[]{:S(2)}, u32[]{:S(2)}) %collective-permute-start.8) | collective-permute-done | bytes 458784 | tf_op jit(solution)/shard_map/ppermute | solution.py:78
  210.5 3.2 %collective-permute-start.12 = (bf16[256,896]{1,0:T(8,128)(2,1)S(1)}, bf16[256,896]{1,0:T(8,128)(2,1)S(1)}, u32[]{:S(2)}, u32[]{:S(2)}) collective-permute-start(bf16[256,896]{1,0:T(8,128)(2,1)S(1)} %collective-permute-done.11), channel_id=1, source_target_pairs={{0,96},{16,112},{32,0},{48,16},{64,32},{80,48},{96,64},{112,80},{1... | collective-permute-start | bytes 1376264 | tf_op jit(solution)/shard_map/ppermute | solution.py:78
  213.8 0.1 bitcast_dynamic-update-slice_fusion.3
  213.8 6.3 %collective-permute-done.9 = bf16[256,896]{1,0:T(8,128)(2,1)S(1)} collective-permute-done((bf16[256,896]{1,0:T(8,128)(2,1)S(1)}, bf16[256,896]{1,0:T(8,128)(2,1)S(1)}, u32[]{:S(2)}, u32[]{:S(2)}) %collective-permute-start.9) | collective-permute-done | bytes 458784 | tf_op jit(solution)/shard_map/ppermute | solution.py:78
  220.2 0.1 bitcast_dynamic-update-slice_fusion.2
  220.3 0.0 copy-start.7
  220.3 0.0 copy-start.2
  220.3 2.1 pad_maximum_fusion.3
  222.4 0.1 iota_compare_fusion.3
  222.4 0.3 fusion.12
  222.8 0.5 broadcast_in_dim.89
  223.3 2.5 bitcast_dynamic-update-slice_fusion.1
  225.8 3.4 %collective-permute-done.13 = bf16[1024,1792]{1,0:T(8,128)(2,1)} collective-permute-done((bf16[1024,1792]{1,0:T(8,128)(2,1)}, bf16[1024,1792]{1,0:T(8,128)(2,1)}, u32[]{:S(2)}, u32[]{:S(2)}) %collective-permute-start.13) | collective-permute-done | bytes 3670048 | tf_op jit(solution)/shard_map/ppermute | solution.py:83
  229.1 2.5 bitcast_dynamic-update-slice_fusion
  231.6 0.5 broadcast_in_dim.105
  232.1 8.2 %convolution_convert_fusion.2 = bf16[2048,1024]{1,0:T(8,128)(2,1)S(1)} fusion(bf16[2048,1792]{1,0:T(8,128)(2,1)S(1)} %bitcast.76, bf16[1792,1024]{1,0:T(8,128)(2,1)S(1)} %copy-done.8, pred[224,8,8,128]{3,2,1,0:T(8,128)(4,1)S(1)} %bitcast.80), kind=kOutput, calls=%fused_computation.7 | convolution fusion | flops 7520124928 | bytes 17039360 | tf_op jit(solution)/shard_map/dot_general | solution.py:197
  240.4 56.3 %all_to_all.5 = bf16[16,128,1024]{2,1,0:T(8,128)(2,1)} all-to-all(bf16[16,128,1024]{2,1,0:T(8,128)(2,1)S(1)} %bitcast.79), channel_id=1, replica_groups=mesh['row'=8,'col'=16] {'col'}, dimensions={0} | all-to-all | bytes 8388608 | tf_op jit(solution)/shard_map/all_to_all | solution.py:205
  296.7 3.9 %reduce_sum.12 = bf16[128,1024]{1,0:T(8,128)(2,1)} reduce(bf16[16,128,1024]{2,1,0:T(8,128)(2,1)} %all_to_all.5, bf16[]{:T(256)} %constant.162.clone.1), dimensions={0}, to_apply=%region_3.4 | reduce | flops 1966080 | bytes 4456450 | tf_op jit(solution)/shard_map/reduce_sum | solution.py:206
  (28 shorter events, 0.2 us)
Async XLA Ops:
  6.5 57.0 %all-gather.2.cloned.1.call-start = ((), (), s32[]{:S(2)}) async-start(), calls=%async_computation.1 | async-start | bytes 4456448 | tf_op jit(solution)/shard_map/all_gather | solution.py:188
  13.2 6.0 %copy-start.5 = (s32[14]{0:T(128)S(1)}, s32[14]{0:T(128)}, u32[]{:S(2)}) copy-start(s32[14]{0:T(128)} %param.17) | copy-start | bytes 172
  13.2 6.1 %copy-start.3 = (s32[14,48]{1,0:T(8,128)S(1)}, s32[14,48]{1,0:T(8,128)}, u32[]{:S(2)}) copy-start(s32[14,48]{1,0:T(8,128)} %param.16) | copy-start | bytes 8068
  13.2 6.1 %copy-start.4 = (s32[14,48]{1,0:T(8,128)S(1)}, s32[14,48]{1,0:T(8,128)}, u32[]{:S(2)}) copy-start(s32[14,48]{1,0:T(8,128)} %param.14) | copy-start | bytes 8068
  13.2 6.4 %copy-start.6 = (s32[14]{0:T(128)S(1)}, s32[14]{0:T(128)}, u32[]{:S(2)}) copy-start(s32[14]{0:T(128)} %param.15) | copy-start | bytes 172
  20.6 5.7 %copy-start.1 = (bf16[1024,1792]{0,1:T(8,128)(2,1)S(1)}, bf16[1024,1792]{0,1:T(8,128)(2,1)}, u32[]{:S(2)}) copy-start(bf16[1024,1792]{0,1:T(8,128)(2,1)} %copy.13) | copy-start | bytes 11010052
  77.0 12.0 %collective-permute-start = (bf16[1024,3584]{1,0:T(8,128)(2,1)}, bf16[1024,3584]{1,0:T(8,128)(2,1)}, u32[]{:S(2)}, u32[]{:S(2)}) collective-permute-start(bf16[1024,3584]{1,0:T(8,128)(2,1)} %convolution_convert_fusion), channel_id=1, source_target_pairs={{0,16},{16,0},{32,48},{48,32},{64,80},{80,64},{96,112},{112,96},{1... | collective-permute-start | bytes 22020104 | tf_op jit(solution)/shard_map/ppermute | solution.py:46
  108.9 1.9 copy-start
  110.8 23.7 %collective-permute-start.1 = (bf16[256,1792]{1,0:T(8,128)(2,1)S(1)}, bf16[256,1792]{1,0:T(8,128)(2,1)S(1)}, u32[]{:S(2)}, u32[]{:S(2)}) collective-permute-start(bf16[256,1792]{1,0:T(8,128)(2,1)S(1)} %dynamic-slice_bitcast_fusion.1), channel_id=1, source_target_pairs={{0,32},{16,48},{32,64},{48,80},{64,96},{80,112},{96,0},{112,16},{1... | collective-permute-start | bytes 2752520 | tf_op jit(solution)/shard_map/ppermute | solution.py:59
  114.5 22.3 %collective-permute-start.4 = (bf16[256,1792]{1,0:T(8,128)(2,1)}, bf16[256,1792]{1,0:T(8,128)(2,1)S(1)}, u32[]{:S(2)}, u32[]{:S(2)}) collective-permute-start(bf16[256,1792]{1,0:T(8,128)(2,1)} %dynamic-slice_bitcast_fusion), channel_id=1, source_target_pairs={{0,96},{16,112},{32,0},{48,16},{64,32},{80,48},{96,64},{112,80},{1... | collective-permute-start | bytes 2752520 | tf_op jit(solution)/shard_map/ppermute | solution.py:59
  135.8 22.8 %collective-permute-start.2 = (bf16[256,1792]{1,0:T(8,128)(2,1)S(1)}, bf16[256,1792]{1,0:T(8,128)(2,1)S(1)}, u32[]{:S(2)}, u32[]{:S(2)}) collective-permute-start(bf16[256,1792]{1,0:T(8,128)(2,1)S(1)} %fusion.9), channel_id=1, source_target_pairs={{0,32},{16,48},{32,64},{48,80},{64,96},{80,112},{96,0},{112,16},{1... | collective-permute-start | bytes 2752520 | tf_op jit(solution)/shard_map/ppermute | solution.py:59
  139.2 22.0 %collective-permute-start.5 = (bf16[256,1792]{1,0:T(8,128)(2,1)}, bf16[256,1792]{1,0:T(8,128)(2,1)}, u32[]{:S(2)}, u32[]{:S(2)}) collective-permute-start(bf16[256,1792]{1,0:T(8,128)(2,1)} %fusion.7), channel_id=1, source_target_pairs={{0,96},{16,112},{32,0},{48,16},{64,32},{80,48},{96,64},{112,80},{1... | collective-permute-start | bytes 2752520 | tf_op jit(solution)/shard_map/ppermute | solution.py:59
  160.0 22.0 %collective-permute-start.3 = (bf16[256,1792]{1,0:T(8,128)(2,1)S(1)}, bf16[256,1792]{1,0:T(8,128)(2,1)S(1)}, u32[]{:S(2)}, u32[]{:S(2)}) collective-permute-start(bf16[256,1792]{1,0:T(8,128)(2,1)S(1)} %fusion.8), channel_id=1, source_target_pairs={{0,32},{16,48},{32,64},{48,80},{64,96},{80,112},{96,0},{112,16},{1... | collective-permute-start | bytes 2752520 | tf_op jit(solution)/shard_map/ppermute | solution.py:59
  164.0 21.9 %collective-permute-start.6 = (bf16[256,1792]{1,0:T(8,128)(2,1)}, bf16[256,1792]{1,0:T(8,128)(2,1)S(1)}, u32[]{:S(2)}, u32[]{:S(2)}) collective-permute-start(bf16[256,1792]{1,0:T(8,128)(2,1)} %fusion.6), channel_id=1, source_target_pairs={{0,96},{16,112},{32,0},{48,16},{64,32},{80,48},{96,64},{112,80},{1... | collective-permute-start | bytes 2752520 | tf_op jit(solution)/shard_map/ppermute | solution.py:59
  188.2 11.6 %collective-permute-start.7 = (bf16[256,896]{1,0:T(8,128)(2,1)S(1)}, bf16[256,896]{1,0:T(8,128)(2,1)S(1)}, u32[]{:S(2)}, u32[]{:S(2)}) collective-permute-start(bf16[256,896]{1,0:T(8,128)(2,1)S(1)} %get-tuple-element.7), channel_id=1, source_target_pairs={{0,32},{16,48},{32,64},{48,80},{64,96},{80,112},{96,0},{112,16},{1... | collective-permute-start | bytes 1376264 | tf_op jit(solution)/shard_map/ppermute | solution.py:78
  188.2 11.5 %collective-permute-start.10 = (bf16[256,896]{1,0:T(8,128)(2,1)S(1)}, bf16[256,896]{1,0:T(8,128)(2,1)S(1)}, u32[]{:S(2)}, u32[]{:S(2)}) collective-permute-start(bf16[256,896]{1,0:T(8,128)(2,1)S(1)} %get-tuple-element.8), channel_id=1, source_target_pairs={{0,96},{16,112},{32,0},{48,16},{64,32},{80,48},{96,64},{112,80},{1... | collective-permute-start | bytes 1376264 | tf_op jit(solution)/shard_map/ppermute | solution.py:78
  199.8 10.7 %collective-permute-start.8 = (bf16[256,896]{1,0:T(8,128)(2,1)S(1)}, bf16[256,896]{1,0:T(8,128)(2,1)S(1)}, u32[]{:S(2)}, u32[]{:S(2)}) collective-permute-start(bf16[256,896]{1,0:T(8,128)(2,1)S(1)} %collective-permute-done.7), channel_id=1, source_target_pairs={{0,32},{16,48},{32,64},{48,80},{64,96},{80,112},{96,0},{112,16},{1... | collective-permute-start | bytes 1376264 | tf_op jit(solution)/shard_map/ppermute | solution.py:78
  199.8 10.7 %collective-permute-start.11 = (bf16[256,896]{1,0:T(8,128)(2,1)S(1)}, bf16[256,896]{1,0:T(8,128)(2,1)S(1)}, u32[]{:S(2)}, u32[]{:S(2)}) collective-permute-start(bf16[256,896]{1,0:T(8,128)(2,1)S(1)} %collective-permute-done.10), channel_id=1, source_target_pairs={{0,96},{16,112},{32,0},{48,16},{64,32},{80,48},{96,64},{112,80},{1... | collective-permute-start | bytes 1376264 | tf_op jit(solution)/shard_map/ppermute | solution.py:78
  210.5 9.7 %collective-permute-start.9 = (bf16[256,896]{1,0:T(8,128)(2,1)S(1)}, bf16[256,896]{1,0:T(8,128)(2,1)S(1)}, u32[]{:S(2)}, u32[]{:S(2)}) collective-permute-start(bf16[256,896]{1,0:T(8,128)(2,1)S(1)} %collective-permute-done.8), channel_id=1, source_target_pairs={{0,32},{16,48},{32,64},{48,80},{64,96},{80,112},{96,0},{112,16},{1... | collective-permute-start | bytes 1376264 | tf_op jit(solution)/shard_map/ppermute | solution.py:78
  210.5 9.7 %collective-permute-start.12 = (bf16[256,896]{1,0:T(8,128)(2,1)S(1)}, bf16[256,896]{1,0:T(8,128)(2,1)S(1)}, u32[]{:S(2)}, u32[]{:S(2)}) collective-permute-start(bf16[256,896]{1,0:T(8,128)(2,1)S(1)} %collective-permute-done.11), channel_id=1, source_target_pairs={{0,96},{16,112},{32,0},{48,16},{64,32},{80,48},{96,64},{112,80},{1... | collective-permute-start | bytes 1376264 | tf_op jit(solution)/shard_map/ppermute | solution.py:78
  220.3 2.1 copy-start.7
  220.3 2.1 copy-start.2
  222.4 6.8 %collective-permute-start.13 = (bf16[1024,1792]{1,0:T(8,128)(2,1)}, bf16[1024,1792]{1,0:T(8,128)(2,1)}, u32[]{:S(2)}, u32[]{:S(2)}) collective-permute-start(bf16[1024,1792]{1,0:T(8,128)(2,1)} %bitcast.23), channel_id=1, source_target_pairs={{0,16},{16,0},{32,48},{48,32},{64,80},{80,64},{96,112},{112,96},{1... | collective-permute-start | bytes 11010056 | tf_op jit(solution)/shard_map/ppermute | solution.py:83
  225.7 6.4 %copy-start.8 = (bf16[1792,1024]{1,0:T(8,128)(2,1)S(1)}, bf16[1792,1024]{1,0:T(8,128)(2,1)}, u32[]{:S(2)}) copy-start(bf16[1792,1024]{1,0:T(8,128)(2,1)} %param.13) | copy-start | bytes 11010052
Sparse Core Ops, SparseCore 0:
  9.5 54.0 all-gather.1
where the time goes:
time: 308 us; the launch traced here: 307 us
  waiting for transfers between devices  126 us (41%)
  blocking collectives  56.3 us (18%)
  matrix products  36.1 us (12%)
  local copies, waits for them, and re-layouts  29.3 us (10%)
  other arithmetic  25.1 us (8%)
  starting transfers between devices  20.6 us (7%)
  between operations  13.6 us (4%)
    all_to_all x1, blocking collectives, on_device(): terms = lax.all_to_all(terms, 'col', 0, 0, tiled=False)  56.3 us
    ppermute x6, waiting for transfers between devices, row_reduce_scatter(): lax.ppermute(acc.astype(jnp.bfloat16), 'row', row_perm(n_row, direction))  54.7 us
    all_gather x1, waiting for transfers between devices, on_device(): gathered = lax.all_gather(tokens, 'col', axis=0, tiled=True)  34.4 us
    ppermute x6, waiting for transfers between devices, row_all_gather(): held = lax.ppermute(held, 'row', row_perm(n_row, direction))  21.1 us
    dot_general x1, matrix products, row_reduce_scatter(): jnp.dot(keep, weights, preferred_element_type=jnp.float32)  14.5 us
    unnamed x20, local copies, waits for them, and re-layouts  13.8 us
    dot_general x1, matrix products, row_reduce_scatter(): jnp.dot(send, weights, preferred_element_type=jnp.float32)  13.4 us
    ppermute x1, waiting for transfers between devices, row_reduce_scatter(): got = lax.ppermute(send, 'row', swap)  12 us
  transfers between devices with their start and end apart: 15, of which 12 were waited for; matrix products, arithmetic and copies ran while one was open for 12% of the time, Pallas kernels for 0%

commit v1 on v0

--- a/solution.py
+++ b/solution.py
@@ -201,9 +201,12 @@
         if COL_RING:
             outs.append(col_reduce_scatter(terms, n_col))
         elif COL_A2A and k == CHUNKS - 1:
-            terms = terms.reshape(n_col, rows, terms.shape[1])
-            terms = lax.all_to_all(terms, "col", 0, 0, tiled=False)
-            outs.append(jnp.sum(terms.astype(jnp.float32), axis=0).astype(jnp.bfloat16))
+            split = terms.shape[1] // 2
+            left = lax.psum_scatter(terms[:, :split], "col", scatter_dimension=0, tiled=True)
+            right = terms[:, split:].reshape(n_col, rows, terms.shape[1] - split)
+            right = lax.all_to_all(right, "col", 0, 0, tiled=False)
+            right = jnp.sum(right.astype(jnp.float32), axis=0).astype(jnp.bfloat16)
+            outs.append(jnp.concatenate([left, right], axis=1))
         else:
             outs.append(lax.psum_scatter(terms, "col", scatter_dimension=0, tiled=True))
     return jnp.concatenate(outs, axis=0)

time: 308 us -> 337 us (1.094)
  waiting for transfers between devices: 126 us -> 174 us
  blocking collectives: 56.3 us -> 37.1 us
    reduce_scatter x0 -> x1, waiting for transfers between devices: none -> 47.7 us  [on_device(): lax.psum_scatter(terms[:, :split], 'col', scatter_dimension=0, tiled=True)]
    all_to_all x1, blocking collectives: 56.3 us -> 37.1 us  [on_device(): right = lax.all_to_all(right, 'col', 0, 0, tiled=False)]
    reduce_sum x1, other arithmetic: 3.88 us -> 0.29 us  [on_device(): right = jnp.sum(right.astype(jnp.float32), axis=0).astype(jnp.bfloat16)]
  transfers between devices with their start and end apart: 15 -> 16, of which waited for: 12 -> 13; matrix products, arithmetic and copies ran while one was open for 12% -> 11% of each run, Pallas kernels for 0% -> 0%
where the time goes in v1:
time: 337 us; the launch traced here: 336 us
  waiting for transfers between devices  174 us (52%)
  blocking collectives  37.1 us (11%)
  matrix products  36.1 us (11%)
  local copies, waits for them, and re-layouts  31.7 us (9%)
  other arithmetic  23.2 us (7%)
  starting transfers between devices  20.6 us (6%)
  between operations  13.7 us (4%)
    ppermute x6, waiting for transfers between devices, row_reduce_scatter(): lax.ppermute(acc.astype(jnp.bfloat16), 'row', row_perm(n_row, direction))  54.7 us
    reduce_scatter x1, waiting for transfers between devices, on_device(): lax.psum_scatter(terms[:, :split], 'col', scatter_dimension=0, tiled=True)  47.7 us
    all_to_all x1, blocking collectives, on_device(): right = lax.all_to_all(right, 'col', 0, 0, tiled=False)  37.1 us
    all_gather x1, waiting for transfers between devices, on_device(): gathered = lax.all_gather(tokens, 'col', axis=0, tiled=True)  34.3 us
    ppermute x6, waiting for transfers between devices, row_all_gather(): held = lax.ppermute(held, 'row', row_perm(n_row, direction))  21.1 us
    dot_general x1, matrix products, row_reduce_scatter(): jnp.dot(keep, weights, preferred_element_type=jnp.float32)  14.5 us
    unnamed x20, local copies, waits for them, and re-layouts  13.9 us
    dot_general x1, matrix products, row_reduce_scatter(): jnp.dot(send, weights, preferred_element_type=jnp.float32)  13.4 us
  transfers between devices with their start and end apart: 16, of which 13 were waited for; matrix products, arithmetic and copies ran while one was open for 11% of the time, Pallas kernels for 0%

profile of v1, /device:TPU:0, one launch (start us, length us, event | category | flops | bytes accessed | tf_op | source)
XLA Modules:
  0.0 336.2 jit_solution(16218142034892544650)
XLA Ops:
  6.5 0.7 all-gather.2.cloned.1.call-update
  7.3 6.0 %copy.14 = bf16[1024,1792]{0,1:T(8,128)(2,1)} copy(bf16[1024,1792]{1,0:T(8,128)(2,1)} %param.12) | data formatting | bytes 7340032 | tf_op args[2]
  13.3 6.0 %copy.13 = bf16[1024,1792]{0,1:T(8,128)(2,1)} copy(bf16[1024,1792]{1,0:T(8,128)(2,1)} %param.11) | data formatting | bytes 7340032 | tf_op args[1]
  19.3 0.1 iota_compare_fusion.4
  19.4 0.3 fusion.16
  19.7 0.1 iota_compare_fusion.5
  19.8 0.3 fusion.14
  20.1 0.5 broadcast_in_dim.93
  20.7 5.1 %bitcast_select_fusion.1 = bf16[1024,1792]{0,1:T(8,128)(2,1)} fusion(bf16[1024,1792]{0,1:T(8,128)(2,1)} %copy.14, pred[224,8,8,128]{3,2,1,0:T(8,128)(4,1)S(1)} %bitcast.78), kind=kLoop, calls=%fused_computation.5 | loop fusion | flops 1835008 | bytes 9175040 | tf_op jit(solution)/shard_map/jit(_where)/select_n | solution.py:25
  25.8 0.5 broadcast_in_dim.90
  26.4 2.8 bitcast_select_fusion.2
  29.2 34.3 %all-gather.2.cloned.1.call-done = bf16[2048,1024]{1,0:T(8,128)(2,1)} async-done(((bf16[128,1024]{1,0:T(8,128)(2,1)}), bf16[2048,1024]{1,0:T(8,128)(2,1)}) %all-gather.2.cloned.1.call-update) | async-done | bytes 4194320 | tf_op jit(solution)/shard_map/all_gather | solution.py:188
  63.5 13.4 %convolution_convert_fusion = bf16[1024,3584]{1,0:T(8,128)(2,1)} fusion(bf16[1024,1792]{0,1:T(8,128)(2,1)} %bitcast_select_fusion.1, bf16[1024,1792]{0,1:T(8,128)(2,1)} %bitcast_select_fusion.2, bf16[2,1024,1024]{2,1,0:T(8,128)(2,1)} %bitcast.84, s32[]{:T(128)S(6)} %select_n.138), kind=kOutput, calls=%fused_computation.1 | convolution fusion | flops 7534542848 | bytes 16777220 | tf_op jit(solution)/shard_map/dot_general | solution.py:44
  76.9 12.0 %collective-permute-done = bf16[1024,3584]{1,0:T(8,128)(2,1)} collective-permute-done((bf16[1024,3584]{1,0:T(8,128)(2,1)}, bf16[1024,3584]{1,0:T(8,128)(2,1)}, u32[]{:S(2)}, u32[]{:S(2)}) %collective-permute-start) | collective-permute-done | bytes 7340064 | tf_op jit(solution)/shard_map/ppermute | solution.py:46
  88.9 14.5 %add_convert_fusion = bf16[1024,3584]{1,0:T(8,128)(2,1)} fusion(bf16[1024,3584]{1,0:T(8,128)(2,1)} %collective-permute-done, bf16[1024,1792]{0,1:T(8,128)(2,1)} %bitcast_select_fusion.1, bf16[1024,1792]{0,1:T(8,128)(2,1)} %bitcast_select_fusion.2, bf16[2,1024,1024]{2,1,0:T(8,128)(2,1)} %bitcast.85, s32[]{:T(128)S(6)} %select_n.135), kind=kOutput, calls=%fused_computation | convolution fusion | flops 7549222912 | bytes 24117252 | tf_op jit(solution)/shard_map/dot_general | solution.py:47
  103.4 5.4 %fusion.22 = (bf16[4,256,1792]{2,1,0:T(8,128)(2,1)S(1)}, bf16[4,256,1792]{2,1,0:T(8,128)(2,1)}) fusion(bf16[4,256,3584]{2,1,0:T(8,128)(2,1)} %bitcast.76), kind=kLoop, calls=%fused_computation.59 | loop fusion | bytes 14680064 | tf_op jit(solution)/shard_map/slice | solution.py:55
  108.8 1.8 copy-done
  110.7 0.1 dynamic-slice_bitcast_fusion.1
  110.7 1.6 collective-permute-start.1
  112.3 2.2 dynamic-slice_bitcast_fusion
  114.5 1.8 collective-permute-start.4
  116.2 18.1 %collective-permute-done.1 = bf16[256,1792]{1,0:T(8,128)(2,1)S(1)} collective-permute-done((bf16[256,1792]{1,0:T(8,128)(2,1)S(1)}, bf16[256,1792]{1,0:T(8,128)(2,1)S(1)}, u32[]{:S(2)}, u32[]{:S(2)}) %collective-permute-start.1) | collective-permute-done | bytes 917536 | tf_op jit(solution)/shard_map/ppermute | solution.py:59
  134.4 1.4 fusion.9
  135.8 0.3 collective-permute-start.2
  136.1 0.7 collective-permute-done.4
  136.8 2.4 fusion.7
  139.2 3.0 collective-permute-start.5
  142.2 16.4 %collective-permute-done.2 = bf16[256,1792]{1,0:T(8,128)(2,1)S(1)} collective-permute-done((bf16[256,1792]{1,0:T(8,128)(2,1)S(1)}, bf16[256,1792]{1,0:T(8,128)(2,1)S(1)}, u32[]{:S(2)}, u32[]{:S(2)}) %collective-permute-start.2) | collective-permute-done | bytes 917536 | tf_op jit(solution)/shard_map/ppermute | solution.py:59
  158.6 1.4 fusion.8
  160.0 0.1 collective-permute-start.3
  160.1 1.2 collective-permute-done.5
  161.3 2.7 fusion.6
  163.9 3.7 %collective-permute-start.6 = (bf16[256,1792]{1,0:T(8,128)(2,1)}, bf16[256,1792]{1,0:T(8,128)(2,1)S(1)}, u32[]{:S(2)}, u32[]{:S(2)}) collective-permute-start(bf16[256,1792]{1,0:T(8,128)(2,1)} %fusion.6), channel_id=1, source_target_pairs={{0,96},{16,112},{32,0},{48,16},{64,32},{80,48},{96,64},{112,80},{1... | collective-permute-start | bytes 2752520 | tf_op jit(solution)/shard_map/ppermute | solution.py:59
  167.6 14.3 %collective-permute-done.3 = bf16[256,1792]{1,0:T(8,128)(2,1)S(1)} collective-permute-done((bf16[256,1792]{1,0:T(8,128)(2,1)S(1)}, bf16[256,1792]{1,0:T(8,128)(2,1)S(1)}, u32[]{:S(2)}, u32[]{:S(2)}) %collective-permute-start.3) | collective-permute-done | bytes 917536 | tf_op jit(solution)/shard_map/ppermute | solution.py:59
  181.9 3.9 %collective-permute-done.6 = bf16[256,1792]{1,0:T(8,128)(2,1)S(1)} collective-permute-done((bf16[256,1792]{1,0:T(8,128)(2,1)}, bf16[256,1792]{1,0:T(8,128)(2,1)S(1)}, u32[]{:S(2)}, u32[]{:S(2)}) %collective-permute-start.6) | collective-permute-done | bytes 917536 | tf_op jit(solution)/shard_map/ppermute | solution.py:59
  185.9 2.2 fusion.5
  188.1 0.1 fusion.24
  188.1 0.1 collective-permute-start.7
  188.2 3.7 %collective-permute-start.10 = (bf16[256,896]{1,0:T(8,128)(2,1)S(1)}, bf16[256,896]{1,0:T(8,128)(2,1)S(1)}, u32[]{:S(2)}, u32[]{:S(2)}) collective-permute-start(bf16[256,896]{1,0:T(8,128)(2,1)S(1)} %get-tuple-element.10), channel_id=1, source_target_pairs={{0,96},{16,112},{32,0},{48,16},{64,32},{80,48},{96,64},{112,80},{1... | collective-permute-start | bytes 1376264 | tf_op jit(solution)/shard_map/ppermute | solution.py:78
  191.9 0.1 broadcast.73.clone.1
  192.0 0.1 bitcast_dynamic-update-slice_fusion.9
  192.1 0.1 broadcast.73.clone
  192.2 0.1 bitcast_dynamic-update-slice_fusion.5
  192.3 7.5 %collective-permute-done.7 = bf16[256,896]{1,0:T(8,128)(2,1)S(1)} collective-permute-done((bf16[256,896]{1,0:T(8,128)(2,1)S(1)}, bf16[256,896]{1,0:T(8,128)(2,1)S(1)}, u32[]{:S(2)}, u32[]{:S(2)}) %collective-permute-start.7) | collective-permute-done | bytes 458784 | tf_op jit(solution)/shard_map/ppermute | solution.py:78
  199.8 3.2 collective-permute-start.11
  203.1 7.3 %collective-permute-done.8 = bf16[256,896]{1,0:T(8,128)(2,1)S(1)} collective-permute-done((bf16[256,896]{1,0:T(8,128)(2,1)S(1)}, bf16[256,896]{1,0:T(8,128)(2,1)S(1)}, u32[]{:S(2)}, u32[]{:S(2)}) %collective-permute-start.8) | collective-permute-done | bytes 458784 | tf_op jit(solution)/shard_map/ppermute | solution.py:78
  210.5 3.2 collective-permute-start.12
  213.8 0.1 bitcast_dynamic-update-slice_fusion.3
  213.8 6.3 %collective-permute-done.9 = bf16[256,896]{1,0:T(8,128)(2,1)S(1)} collective-permute-done((bf16[256,896]{1,0:T(8,128)(2,1)S(1)}, bf16[256,896]{1,0:T(8,128)(2,1)S(1)}, u32[]{:S(2)}, u32[]{:S(2)}) %collective-permute-start.9) | collective-permute-done | bytes 458784 | tf_op jit(solution)/shard_map/ppermute | solution.py:78
  220.2 0.1 bitcast_dynamic-update-slice_fusion.2
  220.3 2.0 pad_maximum_fusion.3
  222.4 0.1 iota_compare_fusion.3
  222.4 0.3 fusion.12
  222.8 0.5 broadcast_in_dim.89
  223.2 2.5 bitcast_dynamic-update-slice_fusion.1
  225.7 3.4 %collective-permute-done.13 = bf16[1024,1792]{1,0:T(8,128)(2,1)} collective-permute-done((bf16[1024,1792]{1,0:T(8,128)(2,1)}, bf16[1024,1792]{1,0:T(8,128)(2,1)}, u32[]{:S(2)}, u32[]{:S(2)}) %collective-permute-start.13) | collective-permute-done | bytes 3670048 | tf_op jit(solution)/shard_map/ppermute | solution.py:83
  229.1 2.5 bitcast_dynamic-update-slice_fusion
  231.6 0.5 broadcast_in_dim.105
  232.1 8.2 %convolution_convert_fusion.2 = bf16[2048,1024]{1,0:T(8,128)(2,1)S(1)} fusion(bf16[2048,1792]{1,0:T(8,128)(2,1)S(1)} %bitcast.77, bf16[1792,1024]{1,0:T(8,128)(2,1)S(1)} %copy-done.8, pred[224,8,8,128]{3,2,1,0:T(8,128)(4,1)S(1)} %bitcast.80), kind=kOutput, calls=%fused_computation.7 | convolution fusion | flops 7520124928 | bytes 17039360 | tf_op jit(solution)/shard_map/dot_general | solution.py:197
  240.4 2.3 fusion.23
  242.7 37.1 %all_to_all.5 = bf16[16,128,512]{2,1,0:T(8,128)(2,1)S(1)} all-to-all(bf16[16,128,512]{2,1,0:T(8,128)(2,1)} %bitcast.75), channel_id=1, replica_groups=mesh['row'=8,'col'=16] {'col'}, dimensions={0} | all-to-all | bytes 4194304 | tf_op jit(solution)/shard_map/all_to_all | solution.py:207
  279.8 0.3 reduce_sum.12
  280.1 47.7 %reduce-scatter.2.cloned.1.call-done = bf16[128,512]{1,0:T(8,128)(2,1)} async-done(((bf16[2048,512]{1,0:T(8,128)(2,1)}), bf16[128,512]{1,0:T(8,128)(2,1)}) %reduce-scatter.2.cloned.1.call-update) | async-done | bytes 131088 | tf_op jit(solution)/shard_map/reduce_scatter | solution.py:205
  327.7 1.6 pad_maximum_fusion.4
  (33 shorter events, 0.3 us)
Async XLA Ops:
  6.5 57.0 %all-gather.2.cloned.1.call-start = ((), (), s32[]{:S(2)}) async-start(), calls=%async_computation.2 | async-start | bytes 4456448 | tf_op jit(solution)/shard_map/all_gather | solution.py:188
  7.3 320.5 %reduce-scatter.2.cloned.1.call-start = ((), (), s32[]{:S(2)}) async-start(), calls=%async_computation.3 | async-start | bytes 2228224 | tf_op jit(solution)/shard_map/reduce_scatter | solution.py:205
  13.3 6.0 %copy-start.5 = (s32[14]{0:T(128)S(1)}, s32[14]{0:T(128)}, u32[]{:S(2)}) copy-start(s32[14]{0:T(128)} %param.17) | copy-start | bytes 172
  13.3 6.1 %copy-start.3 = (s32[14,48]{1,0:T(8,128)S(1)}, s32[14,48]{1,0:T(8,128)}, u32[]{:S(2)}) copy-start(s32[14,48]{1,0:T(8,128)} %param.16) | copy-start | bytes 8068
  13.3 6.1 %copy-start.4 = (s32[14,48]{1,0:T(8,128)S(1)}, s32[14,48]{1,0:T(8,128)}, u32[]{:S(2)}) copy-start(s32[14,48]{1,0:T(8,128)} %param.14) | copy-start | bytes 8068
  13.3 6.4 %copy-start.6 = (s32[14]{0:T(128)S(1)}, s32[14]{0:T(128)}, u32[]{:S(2)}) copy-start(s32[14]{0:T(128)} %param.15) | copy-start | bytes 172
  20.7 5.7 %copy-start.1 = (bf16[1024,1792]{0,1:T(8,128)(2,1)S(1)}, bf16[1024,1792]{0,1:T(8,128)(2,1)}, u32[]{:S(2)}) copy-start(bf16[1024,1792]{0,1:T(8,128)(2,1)} %copy.13) | copy-start | bytes 11010052
  76.9 12.0 %collective-permute-start = (bf16[1024,3584]{1,0:T(8,128)(2,1)}, bf16[1024,3584]{1,0:T(8,128)(2,1)}, u32[]{:S(2)}, u32[]{:S(2)}) collective-permute-start(bf16[1024,3584]{1,0:T(8,128)(2,1)} %convolution_convert_fusion), channel_id=1, source_target_pairs={{0,16},{16,0},{32,48},{48,32},{64,80},{80,64},{96,112},{112,96},{1... | collective-permute-start | bytes 22020104 | tf_op jit(solution)/shard_map/ppermute | solution.py:46
  108.8 1.8 copy-start
  110.7 23.7 %collective-permute-start.1 = (bf16[256,1792]{1,0:T(8,128)(2,1)S(1)}, bf16[256,1792]{1,0:T(8,128)(2,1)S(1)}, u32[]{:S(2)}, u32[]{:S(2)}) collective-permute-start(bf16[256,1792]{1,0:T(8,128)(2,1)S(1)} %dynamic-slice_bitcast_fusion.1), channel_id=1, source_target_pairs={{0,32},{16,48},{32,64},{48,80},{64,96},{80,112},{96,0},{112,16},{1... | collective-permute-start | bytes 2752520 | tf_op jit(solution)/shard_map/ppermute | solution.py:59
  114.5 22.3 %collective-permute-start.4 = (bf16[256,1792]{1,0:T(8,128)(2,1)}, bf16[256,1792]{1,0:T(8,128)(2,1)S(1)}, u32[]{:S(2)}, u32[]{:S(2)}) collective-permute-start(bf16[256,1792]{1,0:T(8,128)(2,1)} %dynamic-slice_bitcast_fusion), channel_id=1, source_target_pairs={{0,96},{16,112},{32,0},{48,16},{64,32},{80,48},{96,64},{112,80},{1... | collective-permute-start | bytes 2752520 | tf_op jit(solution)/shard_map/ppermute | solution.py:59
  135.8 22.8 %collective-permute-start.2 = (bf16[256,1792]{1,0:T(8,128)(2,1)S(1)}, bf16[256,1792]{1,0:T(8,128)(2,1)S(1)}, u32[]{:S(2)}, u32[]{:S(2)}) collective-permute-start(bf16[256,1792]{1,0:T(8,128)(2,1)S(1)} %fusion.9), channel_id=1, source_target_pairs={{0,32},{16,48},{32,64},{48,80},{64,96},{80,112},{96,0},{112,16},{1... | collective-permute-start | bytes 2752520 | tf_op jit(solution)/shard_map/ppermute | solution.py:59
  139.2 22.0 %collective-permute-start.5 = (bf16[256,1792]{1,0:T(8,128)(2,1)}, bf16[256,1792]{1,0:T(8,128)(2,1)}, u32[]{:S(2)}, u32[]{:S(2)}) collective-permute-start(bf16[256,1792]{1,0:T(8,128)(2,1)} %fusion.7), channel_id=1, source_target_pairs={{0,96},{16,112},{32,0},{48,16},{64,32},{80,48},{96,64},{112,80},{1... | collective-permute-start | bytes 2752520 | tf_op jit(solution)/shard_map/ppermute | solution.py:59
  160.0 22.0 %collective-permute-start.3 = (bf16[256,1792]{1,0:T(8,128)(2,1)S(1)}, bf16[256,1792]{1,0:T(8,128)(2,1)S(1)}, u32[]{:S(2)}, u32[]{:S(2)}) collective-permute-start(bf16[256,1792]{1,0:T(8,128)(2,1)S(1)} %fusion.8), channel_id=1, source_target_pairs={{0,32},{16,48},{32,64},{48,80},{64,96},{80,112},{96,0},{112,16},{1... | collective-permute-start | bytes 2752520 | tf_op jit(solution)/shard_map/ppermute | solution.py:59
  163.9 21.9 %collective-permute-start.6 = (bf16[256,1792]{1,0:T(8,128)(2,1)}, bf16[256,1792]{1,0:T(8,128)(2,1)S(1)}, u32[]{:S(2)}, u32[]{:S(2)}) collective-permute-start(bf16[256,1792]{1,0:T(8,128)(2,1)} %fusion.6), channel_id=1, source_target_pairs={{0,96},{16,112},{32,0},{48,16},{64,32},{80,48},{96,64},{112,80},{1... | collective-permute-start | bytes 2752520 | tf_op jit(solution)/shard_map/ppermute | solution.py:59
  188.1 11.6 %collective-permute-start.7 = (bf16[256,896]{1,0:T(8,128)(2,1)S(1)}, bf16[256,896]{1,0:T(8,128)(2,1)S(1)}, u32[]{:S(2)}, u32[]{:S(2)}) collective-permute-start(bf16[256,896]{1,0:T(8,128)(2,1)S(1)} %get-tuple-element.9), channel_id=1, source_target_pairs={{0,32},{16,48},{32,64},{48,80},{64,96},{80,112},{96,0},{112,16},{1... | collective-permute-start | bytes 1376264 | tf_op jit(solution)/shard_map/ppermute | solution.py:78
  188.2 11.5 %collective-permute-start.10 = (bf16[256,896]{1,0:T(8,128)(2,1)S(1)}, bf16[256,896]{1,0:T(8,128)(2,1)S(1)}, u32[]{:S(2)}, u32[]{:S(2)}) collective-permute-start(bf16[256,896]{1,0:T(8,128)(2,1)S(1)} %get-tuple-element.10), channel_id=1, source_target_pairs={{0,96},{16,112},{32,0},{48,16},{64,32},{80,48},{96,64},{112,80},{1... | collective-permute-start | bytes 1376264 | tf_op jit(solution)/shard_map/ppermute | solution.py:78
  199.8 10.7 %collective-permute-start.8 = (bf16[256,896]{1,0:T(8,128)(2,1)S(1)}, bf16[256,896]{1,0:T(8,128)(2,1)S(1)}, u32[]{:S(2)}, u32[]{:S(2)}) collective-permute-start(bf16[256,896]{1,0:T(8,128)(2,1)S(1)} %collective-permute-done.7), channel_id=1, source_target_pairs={{0,32},{16,48},{32,64},{48,80},{64,96},{80,112},{96,0},{112,16},{1... | collective-permute-start | bytes 1376264 | tf_op jit(solution)/shard_map/ppermute | solution.py:78
  199.8 10.7 %collective-permute-start.11 = (bf16[256,896]{1,0:T(8,128)(2,1)S(1)}, bf16[256,896]{1,0:T(8,128)(2,1)S(1)}, u32[]{:S(2)}, u32[]{:S(2)}) collective-permute-start(bf16[256,896]{1,0:T(8,128)(2,1)S(1)} %collective-permute-done.10), channel_id=1, source_target_pairs={{0,96},{16,112},{32,0},{48,16},{64,32},{80,48},{96,64},{112,80},{1... | collective-permute-start | bytes 1376264 | tf_op jit(solution)/shard_map/ppermute | solution.py:78
  210.5 9.7 %collective-permute-start.9 = (bf16[256,896]{1,0:T(8,128)(2,1)S(1)}, bf16[256,896]{1,0:T(8,128)(2,1)S(1)}, u32[]{:S(2)}, u32[]{:S(2)}) collective-permute-start(bf16[256,896]{1,0:T(8,128)(2,1)S(1)} %collective-permute-done.8), channel_id=1, source_target_pairs={{0,32},{16,48},{32,64},{48,80},{64,96},{80,112},{96,0},{112,16},{1... | collective-permute-start | bytes 1376264 | tf_op jit(solution)/shard_map/ppermute | solution.py:78
  210.5 9.7 %collective-permute-start.12 = (bf16[256,896]{1,0:T(8,128)(2,1)S(1)}, bf16[256,896]{1,0:T(8,128)(2,1)S(1)}, u32[]{:S(2)}, u32[]{:S(2)}) collective-permute-start(bf16[256,896]{1,0:T(8,128)(2,1)S(1)} %collective-permute-done.11), channel_id=1, source_target_pairs={{0,96},{16,112},{32,0},{48,16},{64,32},{80,48},{96,64},{112,80},{1... | collective-permute-start | bytes 1376264 | tf_op jit(solution)/shard_map/ppermute | solution.py:78
  220.3 2.1 copy-start.7
  220.3 2.1 copy-start.2
  222.3 6.8 %collective-permute-start.13 = (bf16[1024,1792]{1,0:T(8,128)(2,1)}, bf16[1024,1792]{1,0:T(8,128)(2,1)}, u32[]{:S(2)}, u32[]{:S(2)}) collective-permute-start(bf16[1024,1792]{1,0:T(8,128)(2,1)} %bitcast.23), channel_id=1, source_target_pairs={{0,16},{16,0},{32,48},{48,32},{64,80},{80,64},{96,112},{112,96},{1... | collective-permute-start | bytes 11010056 | tf_op jit(solution)/shard_map/ppermute | solution.py:83
  225.7 6.4 %copy-start.8 = (bf16[1792,1024]{1,0:T(8,128)(2,1)S(1)}, bf16[1792,1024]{1,0:T(8,128)(2,1)}, u32[]{:S(2)}) copy-start(bf16[1792,1024]{1,0:T(8,128)(2,1)} %param.13) | copy-start | bytes 11010052
Sparse Core Ops, SparseCore 0:
  9.5 54.0 all-gather.1
  242.8 84.8 reduce-scatter.1

commit v2 on v0

--- a/solution.py
+++ b/solution.py
@@ -45,6 +45,7 @@
     swap = [(i, i ^ 1) for i in range(n_row)]
     got = lax.ppermute(send, "row", swap)
     keep = jnp.dot(keep, weights, preferred_element_type=jnp.float32).astype(jnp.bfloat16)
+    keep = lax.optimization_barrier(keep)
     pair = (keep.astype(jnp.float32) + got.astype(jnp.float32)).astype(jnp.bfloat16)
     if after is not None:
         pair, after = lax.optimization_barrier((pair, after))
@@ -63,7 +64,7 @@
     return results
 
 
-def row_all_gather(value, n_row):
+def row_all_gather(value, n_row, down):
     n_y = n_row // 2
     r = lax.axis_index("row")
     y = r // 2
@@ -81,10 +82,12 @@
     half = jnp.concatenate(parts, axis=2).reshape(n_y * chunk, width)
     swap = [(i, i ^ 1) for i in range(n_row)]
     other = lax.ppermute(half, "row", swap)
-    both = jnp.zeros((2, n_y * chunk, width), value.dtype)
-    both = lax.dynamic_update_index_in_dim(both, half, core, 0)
-    both = lax.dynamic_update_index_in_dim(both, other, 1 - core, 0)
-    return both.reshape(2 * n_y * chunk, width)
+    mine = jnp.dot(half, down, preferred_element_type=jnp.float32).astype(jnp.bfloat16)
+    theirs = jnp.dot(other, down, preferred_element_type=jnp.float32).astype(jnp.bfloat16)
+    both = jnp.zeros((2, n_y * chunk, down.shape[1]), jnp.bfloat16)
+    both = lax.dynamic_update_index_in_dim(both, mine, core, 0)
+    both = lax.dynamic_update_index_in_dim(both, theirs, 1 - core, 0)
+    return both.reshape(2 * n_y * chunk, down.shape[1])
 
 
 def ring_reduce_scatter(own, pos, n, perm_of):
@@ -193,10 +196,7 @@
         chunk = gathered[:, k].reshape(n_col * rows, gathered.shape[3])
         gate_sums, up_sums = row_reduce_scatter(chunk, both_weights, n_row, previous)
         hidden = (jax.nn.silu(gate_sums) * up_sums).astype(jnp.bfloat16)
-        hidden = row_all_gather(hidden, n_row)
-        terms = jnp.dot(hidden, down_pruned, preferred_element_type=jnp.float32).astype(
-            jnp.bfloat16
-        )
+        terms = row_all_gather(hidden, n_row, down_pruned)
         previous = terms
         if COL_RING:
             outs.append(col_reduce_scatter(terms, n_col))

time: 308 us -> 304 us (0.987)
  waiting for transfers between devices: 126 us -> 113 us
  other arithmetic: 25.1 us -> 35.1 us
  local copies, waits for them, and re-layouts: 29.3 us -> 25 us
  matrix products: 36.1 us -> 39.6 us
    ppermute x1, waiting for transfers between devices: 12 us -> 0.01 us  [row_reduce_scatter(): got = lax.ppermute(send, 'row', swap)]
    convert_element_type x0 -> x1, other arithmetic: none -> 10 us  [row_reduce_scatter(): (keep.astype(jnp.float32) + got.astype(jnp.float32)).astype(jnp.bfloat16)]
    dynamic_update_slice x2 -> x0, local copies, waits for them, and re-layouts: 4.94 us -> none  [the longest x1 2.47 us: row_all_gather(): both = lax.dynamic_update_index_in_dim(both, half, core, 0)]
    dot_general x1 -> x2, matrix products: 8.24 us -> 12.9 us  [the longest x1 6.46 us: row_all_gather(): jnp.dot(other, down, preferred_element_type=jnp.float32)]
    ppermute x1, waiting for transfers between devices: 3.36 us -> 0.01 us  [row_all_gather(): other = lax.ppermute(half, 'row', swap)]
  transfers between devices with their start and end apart: 15 -> 15, of which waited for: 12 -> 10; matrix products, arithmetic and copies ran while one was open for 12% -> 18% of each run, Pallas kernels for 0% -> 0%
where the time goes in v2:
time: 304 us; the launch traced here: 303 us
  waiting for transfers between devices  113 us (37%)
  blocking collectives  56.6 us (19%)
  matrix products  39.6 us (13%)
  other arithmetic  35.1 us (12%)
  local copies, waits for them, and re-layouts  25 us (8%)
  starting transfers between devices  20.6 us (7%)
  between operations  13.6 us (4%)
    all_to_all x1, blocking collectives, on_device(): terms = lax.all_to_all(terms, 'col', 0, 0, tiled=False)  56.6 us
    ppermute x6, waiting for transfers between devices, row_reduce_scatter(): lax.ppermute(acc.astype(jnp.bfloat16), 'row', row_perm(n_row, direction))  55.8 us
    all_gather x1, waiting for transfers between devices, on_device(): gathered = lax.all_gather(tokens, 'col', axis=0, tiled=True)  34.5 us
    ppermute x6, waiting for transfers between devices, row_all_gather(): held = lax.ppermute(held, 'row', row_perm(n_row, direction))  21.7 us
    unnamed x20, local copies, waits for them, and re-layouts  14.4 us
    dot_general x1, matrix products, row_reduce_scatter(): jnp.dot(send, weights, preferred_element_type=jnp.float32)  13.4 us
    dot_general x1, matrix products, row_reduce_scatter(): jnp.dot(keep, weights, preferred_element_type=jnp.float32)  13.3 us
    ppermute x6, starting transfers between devices, row_reduce_scatter(): lax.ppermute(acc.astype(jnp.bfloat16), 'row', row_perm(n_row, direction))  10.4 us
  transfers between devices with their start and end apart: 15, of which 10 were waited for; matrix products, arithmetic and copies ran while one was open for 18% of the time, Pallas kernels for 0%

profile of v2, /device:TPU:0, one launch (start us, length us, event | category | flops | bytes accessed | tf_op | source)
XLA Modules:
  0.0 303.2 jit_solution(8895791569120512801)
XLA Ops:
  6.5 0.7 all-gather.2.cloned.1.call-update
  7.3 6.0 %copy.14 = bf16[1024,1792]{0,1:T(8,128)(2,1)} copy(bf16[1024,1792]{1,0:T(8,128)(2,1)} %param.12) | data formatting | bytes 7340032 | tf_op args[2]
  13.3 6.0 %copy.13 = bf16[1024,1792]{0,1:T(8,128)(2,1)} copy(bf16[1024,1792]{1,0:T(8,128)(2,1)} %param.11) | data formatting | bytes 7340032 | tf_op args[1]
  19.3 0.1 iota_compare_fusion.4
  19.4 0.3 fusion.17
  19.7 0.1 iota_compare_fusion.5
  19.8 0.3 fusion.15
  20.1 0.5 broadcast_in_dim.93
  20.6 5.1 %bitcast_select_fusion.1 = bf16[1024,1792]{0,1:T(8,128)(2,1)} fusion(bf16[1024,1792]{0,1:T(8,128)(2,1)} %copy.14, pred[224,8,8,128]{3,2,1,0:T(8,128)(4,1)S(1)} %bitcast.77), kind=kLoop, calls=%fused_computation.5 | loop fusion | flops 1835008 | bytes 9175040 | tf_op jit(solution)/shard_map/jit(_where)/select_n | solution.py:25
  25.7 0.5 broadcast_in_dim.90
  26.3 2.8 bitcast_select_fusion.2
  29.1 34.5 %all-gather.2.cloned.1.call-done = bf16[2048,1024]{1,0:T(8,128)(2,1)} async-done(((bf16[128,1024]{1,0:T(8,128)(2,1)}), bf16[2048,1024]{1,0:T(8,128)(2,1)}) %all-gather.2.cloned.1.call-update) | async-done | bytes 4194320 | tf_op jit(solution)/shard_map/all_gather | solution.py:191
  63.6 13.4 %convolution_convert_fusion = bf16[1024,3584]{1,0:T(8,128)(2,1)} fusion(bf16[1024,1792]{0,1:T(8,128)(2,1)} %bitcast_select_fusion.1, bf16[1024,1792]{0,1:T(8,128)(2,1)} %bitcast_select_fusion.2, bf16[2,1024,1024]{2,1,0:T(8,128)(2,1)} %bitcast.84, s32[]{:T(128)S(6)} %select_n.138), kind=kOutput, calls=%fused_computation.1 | convolution fusion | flops 7534542848 | bytes 16777220 | tf_op jit(solution)/shard_map/dot_general | solution.py:44
  77.0 0.0 collective-permute-start
  77.0 13.3 %convolution_convert_fusion.1 = bf16[1024,3584]{1,0:T(8,128)(2,1)} fusion(bf16[1024,1792]{0,1:T(8,128)(2,1)} %bitcast_select_fusion.1, bf16[1024,1792]{0,1:T(8,128)(2,1)} %bitcast_select_fusion.2, bf16[2,1024,1024]{2,1,0:T(8,128)(2,1)} %bitcast.85, s32[]{:T(128)S(6)} %select_n.135), kind=kOutput, calls=%fused_computation.2 | convolution fusion | flops 7534542848 | bytes 16777220 | tf_op jit(solution)/shard_map/dot_general | solution.py:47
  90.3 10.0 %add_convert_fusion = bf16[1024,3584]{1,0:T(8,128)(2,1)} fusion(bf16[1024,3584]{1,0:T(8,128)(2,1)} %collective-permute-done, bf16[1024,3584]{1,0:T(8,128)(2,1)} %convolution_convert_fusion.1), kind=kLoop, calls=%fused_computation | loop fusion | flops 14680064 | bytes 22020096 | tf_op jit(solution)/shard_map/convert_element_type | solution.py:49
  100.4 5.4 %fusion.24 = (bf16[4,256,1792]{2,1,0:T(8,128)(2,1)S(1)}, bf16[4,256,1792]{2,1,0:T(8,128)(2,1)}) fusion(bf16[4,256,3584]{2,1,0:T(8,128)(2,1)} %bitcast.75), kind=kLoop, calls=%fused_computation.59 | loop fusion | bytes 14680064 | tf_op jit(solution)/shard_map/slice | solution.py:56
  105.8 1.9 copy-done
  107.6 0.1 dynamic-slice_bitcast_fusion.1
  107.7 1.6 collective-permute-start.1
  109.2 2.2 dynamic-slice_bitcast_fusion
  111.5 1.8 collective-permute-start.4
  113.2 18.5 %collective-permute-done.1 = bf16[256,1792]{1,0:T(8,128)(2,1)S(1)} collective-permute-done((bf16[256,1792]{1,0:T(8,128)(2,1)S(1)}, bf16[256,1792]{1,0:T(8,128)(2,1)S(1)}, u32[]{:S(2)}, u32[]{:S(2)}) %collective-permute-start.1) | collective-permute-done | bytes 917536 | tf_op jit(solution)/shard_map/ppermute | solution.py:60
  131.7 1.4 fusion.9
  133.1 0.3 collective-permute-start.2
  133.5 0.7 collective-permute-done.4
  134.1 2.4 fusion.7
  136.5 3.0 collective-permute-start.5
  139.5 16.8 %collective-permute-done.2 = bf16[256,1792]{1,0:T(8,128)(2,1)S(1)} collective-permute-done((bf16[256,1792]{1,0:T(8,128)(2,1)S(1)}, bf16[256,1792]{1,0:T(8,128)(2,1)S(1)}, u32[]{:S(2)}, u32[]{:S(2)}) %collective-permute-start.2) | collective-permute-done | bytes 917536 | tf_op jit(solution)/shard_map/ppermute | solution.py:60
  156.3 1.4 fusion.8
  157.7 0.1 collective-permute-start.3
  157.8 1.2 collective-permute-done.5
  158.9 2.7 fusion.6
  161.6 3.7 %collective-permute-start.6 = (bf16[256,1792]{1,0:T(8,128)(2,1)}, bf16[256,1792]{1,0:T(8,128)(2,1)S(1)}, u32[]{:S(2)}, u32[]{:S(2)}) collective-permute-start(bf16[256,1792]{1,0:T(8,128)(2,1)} %fusion.6), channel_id=1, source_target_pairs={{0,96},{16,112},{32,0},{48,16},{64,32},{80,48},{96,64},{112,80},{1... | collective-permute-start | bytes 2752520 | tf_op jit(solution)/shard_map/ppermute | solution.py:60
  165.3 14.7 %collective-permute-done.3 = bf16[256,1792]{1,0:T(8,128)(2,1)S(1)} collective-permute-done((bf16[256,1792]{1,0:T(8,128)(2,1)S(1)}, bf16[256,1792]{1,0:T(8,128)(2,1)S(1)}, u32[]{:S(2)}, u32[]{:S(2)}) %collective-permute-start.3) | collective-permute-done | bytes 917536 | tf_op jit(solution)/shard_map/ppermute | solution.py:60
  180.0 3.9 %collective-permute-done.6 = bf16[256,1792]{1,0:T(8,128)(2,1)S(1)} collective-permute-done((bf16[256,1792]{1,0:T(8,128)(2,1)}, bf16[256,1792]{1,0:T(8,128)(2,1)S(1)}, u32[]{:S(2)}, u32[]{:S(2)}) %collective-permute-start.6) | collective-permute-done | bytes 917536 | tf_op jit(solution)/shard_map/ppermute | solution.py:60
  183.9 2.2 fusion.5
  186.1 0.1 fusion.25
  186.2 0.1 collective-permute-start.7
  186.3 3.7 %collective-permute-start.10 = (bf16[256,896]{1,0:T(8,128)(2,1)S(1)}, bf16[256,896]{1,0:T(8,128)(2,1)S(1)}, u32[]{:S(2)}, u32[]{:S(2)}) collective-permute-start(bf16[256,896]{1,0:T(8,128)(2,1)S(1)} %get-tuple-element.8), channel_id=1, source_target_pairs={{0,96},{16,112},{32,0},{48,16},{64,32},{80,48},{96,64},{112,80},{1... | collective-permute-start | bytes 1376264 | tf_op jit(solution)/shard_map/ppermute | solution.py:79
  189.9 0.1 broadcast.73.clone.1
  190.1 0.1 bitcast_dynamic-update-slice_fusion.9
  190.1 0.1 broadcast.73.clone
  190.3 0.1 bitcast_dynamic-update-slice_fusion.5
  190.3 7.8 %collective-permute-done.7 = bf16[256,896]{1,0:T(8,128)(2,1)S(1)} collective-permute-done((bf16[256,896]{1,0:T(8,128)(2,1)S(1)}, bf16[256,896]{1,0:T(8,128)(2,1)S(1)}, u32[]{:S(2)}, u32[]{:S(2)}) %collective-permute-start.7) | collective-permute-done | bytes 458784 | tf_op jit(solution)/shard_map/ppermute | solution.py:79
  198.2 3.2 %collective-permute-start.11 = (bf16[256,896]{1,0:T(8,128)(2,1)S(1)}, bf16[256,896]{1,0:T(8,128)(2,1)S(1)}, u32[]{:S(2)}, u32[]{:S(2)}) collective-permute-start(bf16[256,896]{1,0:T(8,128)(2,1)S(1)} %collective-permute-done.10), channel_id=1, source_target_pairs={{0,96},{16,112},{32,0},{48,16},{64,32},{80,48},{96,64},{112,80},{1... | collective-permute-start | bytes 1376264 | tf_op jit(solution)/shard_map/ppermute | solution.py:79
  201.4 0.1 bitcast_dynamic-update-slice_fusion.4
  201.5 7.3 %collective-permute-done.8 = bf16[256,896]{1,0:T(8,128)(2,1)S(1)} collective-permute-done((bf16[256,896]{1,0:T(8,128)(2,1)S(1)}, bf16[256,896]{1,0:T(8,128)(2,1)S(1)}, u32[]{:S(2)}, u32[]{:S(2)}) %collective-permute-start.8) | collective-permute-done | bytes 458784 | tf_op jit(solution)/shard_map/ppermute | solution.py:79
  208.9 3.2 %collective-permute-start.12 = (bf16[256,896]{1,0:T(8,128)(2,1)S(1)}, bf16[256,896]{1,0:T(8,128)(2,1)S(1)}, u32[]{:S(2)}, u32[]{:S(2)}) collective-permute-start(bf16[256,896]{1,0:T(8,128)(2,1)S(1)} %collective-permute-done.11), channel_id=1, source_target_pairs={{0,96},{16,112},{32,0},{48,16},{64,32},{80,48},{96,64},{112,80},{1... | collective-permute-start | bytes 1376264 | tf_op jit(solution)/shard_map/ppermute | solution.py:79
  212.2 0.1 bitcast_dynamic-update-slice_fusion.3
  212.2 6.5 %collective-permute-done.9 = bf16[256,896]{1,0:T(8,128)(2,1)S(1)} collective-permute-done((bf16[256,896]{1,0:T(8,128)(2,1)S(1)}, bf16[256,896]{1,0:T(8,128)(2,1)S(1)}, u32[]{:S(2)}, u32[]{:S(2)}) %collective-permute-start.9) | collective-permute-done | bytes 458784 | tf_op jit(solution)/shard_map/ppermute | solution.py:79
  218.8 0.1 bitcast_dynamic-update-slice_fusion.2
  218.8 0.0 copy-start.7
  218.8 0.0 copy-start.2
  218.9 2.1 pad_maximum_fusion.3
  220.9 0.1 iota_compare_fusion.3
  221.0 0.3 fusion.13
  221.3 0.5 broadcast_in_dim.103
  221.9 0.5 broadcast_in_dim.89
  222.4 0.5 copy-done.8
  223.0 6.4 %bitcast_dynamic-update-slice_fusion.1 = bf16[2,1024,1024]{2,1,0:T(8,128)(2,1)S(1)} fusion(bf16[2,1024,1024]{2,1,0:T(8,128)(2,1)S(1)} %broadcast_in_dim.89, s32[]{:T(128)S(6)} %select_n.135, bf16[1024,1792]{1,0:T(8,128)(2,1)} %bitcast.22, bf16[1792,1024]{1,0:T(8,128)(2,1)S(1)} %copy-done.8, pred[224,8,8,128]{3,2,1,0:T(8,128)(4,1)S(1)} %bitcast.79), kind=kOutput, calls=%fused_computation.9 | convolution fusion | flops 3760979968 | bytes 11272196 | tf_op jit(solution)/shard_map/dot_general | solution.py:85
  229.4 6.5 %bitcast_dynamic-update-slice_fusion = bf16[2,1024,1024]{2,1,0:T(8,128)(2,1)S(1)} fusion(bf16[2,1024,1024]{2,1,0:T(8,128)(2,1)S(1)} %bitcast_dynamic-update-slice_fusion.1, s32[]{:T(128)S(6)} %select_n.138, bf16[1024,1792]{1,0:T(8,128)(2,1)} %collective-permute-done.13, bf16[1792,1024]{1,0:T(8,128)(2,1)S(1)} %copy-done.8, ...), kind=kOutput, calls=%fused_computation.8 | convolution fusion | flops 3760979968 | bytes 11272196 | tf_op jit(solution)/shard_map/dot_general | solution.py:86
  235.9 56.6 %all_to_all.5 = bf16[16,128,1024]{2,1,0:T(8,128)(2,1)} all-to-all(bf16[16,128,1024]{2,1,0:T(8,128)(2,1)S(1)} %bitcast.76), channel_id=1, replica_groups=mesh['row'=8,'col'=16] {'col'}, dimensions={0} | all-to-all | bytes 8388608 | tf_op jit(solution)/shard_map/all_to_all | solution.py:205
  292.5 3.9 %reduce_sum.12 = bf16[128,1024]{1,0:T(8,128)(2,1)} reduce(bf16[16,128,1024]{2,1,0:T(8,128)(2,1)} %all_to_all.5, bf16[]{:T(256)} %constant.162.clone.1), dimensions={0}, to_apply=%region_3.4 | reduce | flops 1966080 | bytes 4456450 | tf_op jit(solution)/shard_map/reduce_sum | solution.py:206
  (28 shorter events, 0.2 us)
Async XLA Ops:
  6.5 57.0 %all-gather.2.cloned.1.call-start = ((), (), s32[]{:S(2)}) async-start(), calls=%async_computation.1 | async-start | bytes 4456448 | tf_op jit(solution)/shard_map/all_gather | solution.py:191
  13.2 6.0 %copy-start.5 = (s32[14]{0:T(128)S(1)}, s32[14]{0:T(128)}, u32[]{:S(2)}) copy-start(s32[14]{0:T(128)} %param.17) | copy-start | bytes 172
  13.2 6.1 %copy-start.3 = (s32[14,48]{1,0:T(8,128)S(1)}, s32[14,48]{1,0:T(8,128)}, u32[]{:S(2)}) copy-start(s32[14,48]{1,0:T(8,128)} %param.16) | copy-start | bytes 8068
  13.3 6.1 %copy-start.4 = (s32[14,48]{1,0:T(8,128)S(1)}, s32[14,48]{1,0:T(8,128)}, u32[]{:S(2)}) copy-start(s32[14,48]{1,0:T(8,128)} %param.14) | copy-start | bytes 8068
  13.3 6.4 %copy-start.6 = (s32[14]{0:T(128)S(1)}, s32[14]{0:T(128)}, u32[]{:S(2)}) copy-start(s32[14]{0:T(128)} %param.15) | copy-start | bytes 172
  20.6 5.6 %copy-start.1 = (bf16[1024,1792]{0,1:T(8,128)(2,1)S(1)}, bf16[1024,1792]{0,1:T(8,128)(2,1)}, u32[]{:S(2)}) copy-start(bf16[1024,1792]{0,1:T(8,128)(2,1)} %copy.13) | copy-start | bytes 11010052
  77.0 13.3 %collective-permute-start = (bf16[1024,3584]{1,0:T(8,128)(2,1)}, bf16[1024,3584]{1,0:T(8,128)(2,1)}, u32[]{:S(2)}, u32[]{:S(2)}) collective-permute-start(bf16[1024,3584]{1,0:T(8,128)(2,1)} %convolution_convert_fusion), channel_id=1, source_target_pairs={{0,16},{16,0},{32,48},{48,32},{64,80},{80,64},{96,112},{112,96},{1... | collective-permute-start | bytes 22020104 | tf_op jit(solution)/shard_map/ppermute | solution.py:46
  105.8 1.9 copy-start
  107.7 24.0 %collective-permute-start.1 = (bf16[256,1792]{1,0:T(8,128)(2,1)S(1)}, bf16[256,1792]{1,0:T(8,128)(2,1)S(1)}, u32[]{:S(2)}, u32[]{:S(2)}) collective-permute-start(bf16[256,1792]{1,0:T(8,128)(2,1)S(1)} %dynamic-slice_bitcast_fusion.1), channel_id=1, source_target_pairs={{0,32},{16,48},{32,64},{48,80},{64,96},{80,112},{96,0},{112,16},{1... | collective-permute-start | bytes 2752520 | tf_op jit(solution)/shard_map/ppermute | solution.py:60
  111.5 22.7 %collective-permute-start.4 = (bf16[256,1792]{1,0:T(8,128)(2,1)}, bf16[256,1792]{1,0:T(8,128)(2,1)S(1)}, u32[]{:S(2)}, u32[]{:S(2)}) collective-permute-start(bf16[256,1792]{1,0:T(8,128)(2,1)} %dynamic-slice_bitcast_fusion), channel_id=1, source_target_pairs={{0,96},{16,112},{32,0},{48,16},{64,32},{80,48},{96,64},{112,80},{1... | collective-permute-start | bytes 2752520 | tf_op jit(solution)/shard_map/ppermute | solution.py:60
  133.1 23.2 %collective-permute-start.2 = (bf16[256,1792]{1,0:T(8,128)(2,1)S(1)}, bf16[256,1792]{1,0:T(8,128)(2,1)S(1)}, u32[]{:S(2)}, u32[]{:S(2)}) collective-permute-start(bf16[256,1792]{1,0:T(8,128)(2,1)S(1)} %fusion.9), channel_id=1, source_target_pairs={{0,32},{16,48},{32,64},{48,80},{64,96},{80,112},{96,0},{112,16},{1... | collective-permute-start | bytes 2752520 | tf_op jit(solution)/shard_map/ppermute | solution.py:60
  136.5 22.4 %collective-permute-start.5 = (bf16[256,1792]{1,0:T(8,128)(2,1)}, bf16[256,1792]{1,0:T(8,128)(2,1)}, u32[]{:S(2)}, u32[]{:S(2)}) collective-permute-start(bf16[256,1792]{1,0:T(8,128)(2,1)} %fusion.7), channel_id=1, source_target_pairs={{0,96},{16,112},{32,0},{48,16},{64,32},{80,48},{96,64},{112,80},{1... | collective-permute-start | bytes 2752520 | tf_op jit(solution)/shard_map/ppermute | solution.py:60
  157.7 22.3 %collective-permute-start.3 = (bf16[256,1792]{1,0:T(8,128)(2,1)S(1)}, bf16[256,1792]{1,0:T(8,128)(2,1)S(1)}, u32[]{:S(2)}, u32[]{:S(2)}) collective-permute-start(bf16[256,1792]{1,0:T(8,128)(2,1)S(1)} %fusion.8), channel_id=1, source_target_pairs={{0,32},{16,48},{32,64},{48,80},{64,96},{80,112},{96,0},{112,16},{1... | collective-permute-start | bytes 2752520 | tf_op jit(solution)/shard_map/ppermute | solution.py:60
  161.6 22.3 %collective-permute-start.6 = (bf16[256,1792]{1,0:T(8,128)(2,1)}, bf16[256,1792]{1,0:T(8,128)(2,1)S(1)}, u32[]{:S(2)}, u32[]{:S(2)}) collective-permute-start(bf16[256,1792]{1,0:T(8,128)(2,1)} %fusion.6), channel_id=1, source_target_pairs={{0,96},{16,112},{32,0},{48,16},{64,32},{80,48},{96,64},{112,80},{1... | collective-permute-start | bytes 2752520 | tf_op jit(solution)/shard_map/ppermute | solution.py:60
  186.2 12.0 %collective-permute-start.7 = (bf16[256,896]{1,0:T(8,128)(2,1)S(1)}, bf16[256,896]{1,0:T(8,128)(2,1)S(1)}, u32[]{:S(2)}, u32[]{:S(2)}) collective-permute-start(bf16[256,896]{1,0:T(8,128)(2,1)S(1)} %get-tuple-element.7), channel_id=1, source_target_pairs={{0,32},{16,48},{32,64},{48,80},{64,96},{80,112},{96,0},{112,16},{1... | collective-permute-start | bytes 1376264 | tf_op jit(solution)/shard_map/ppermute | solution.py:79
  186.3 11.9 %collective-permute-start.10 = (bf16[256,896]{1,0:T(8,128)(2,1)S(1)}, bf16[256,896]{1,0:T(8,128)(2,1)S(1)}, u32[]{:S(2)}, u32[]{:S(2)}) collective-permute-start(bf16[256,896]{1,0:T(8,128)(2,1)S(1)} %get-tuple-element.8), channel_id=1, source_target_pairs={{0,96},{16,112},{32,0},{48,16},{64,32},{80,48},{96,64},{112,80},{1... | collective-permute-start | bytes 1376264 | tf_op jit(solution)/shard_map/ppermute | solution.py:79
  198.2 10.7 %collective-permute-start.8 = (bf16[256,896]{1,0:T(8,128)(2,1)S(1)}, bf16[256,896]{1,0:T(8,128)(2,1)S(1)}, u32[]{:S(2)}, u32[]{:S(2)}) collective-permute-start(bf16[256,896]{1,0:T(8,128)(2,1)S(1)} %collective-permute-done.7), channel_id=1, source_target_pairs={{0,32},{16,48},{32,64},{48,80},{64,96},{80,112},{96,0},{112,16},{1... | collective-permute-start | bytes 1376264 | tf_op jit(solution)/shard_map/ppermute | solution.py:79
  198.2 10.7 %collective-permute-start.11 = (bf16[256,896]{1,0:T(8,128)(2,1)S(1)}, bf16[256,896]{1,0:T(8,128)(2,1)S(1)}, u32[]{:S(2)}, u32[]{:S(2)}) collective-permute-start(bf16[256,896]{1,0:T(8,128)(2,1)S(1)} %collective-permute-done.10), channel_id=1, source_target_pairs={{0,96},{16,112},{32,0},{48,16},{64,32},{80,48},{96,64},{112,80},{1... | collective-permute-start | bytes 1376264 | tf_op jit(solution)/shard_map/ppermute | solution.py:79
  208.9 9.8 %collective-permute-start.9 = (bf16[256,896]{1,0:T(8,128)(2,1)S(1)}, bf16[256,896]{1,0:T(8,128)(2,1)S(1)}, u32[]{:S(2)}, u32[]{:S(2)}) collective-permute-start(bf16[256,896]{1,0:T(8,128)(2,1)S(1)} %collective-permute-done.8), channel_id=1, source_target_pairs={{0,32},{16,48},{32,64},{48,80},{64,96},{80,112},{96,0},{112,16},{1... | collective-permute-start | bytes 1376264 | tf_op jit(solution)/shard_map/ppermute | solution.py:79
  208.9 9.9 %collective-permute-start.12 = (bf16[256,896]{1,0:T(8,128)(2,1)S(1)}, bf16[256,896]{1,0:T(8,128)(2,1)S(1)}, u32[]{:S(2)}, u32[]{:S(2)}) collective-permute-start(bf16[256,896]{1,0:T(8,128)(2,1)S(1)} %collective-permute-done.11), channel_id=1, source_target_pairs={{0,96},{16,112},{32,0},{48,16},{64,32},{80,48},{96,64},{112,80},{1... | collective-permute-start | bytes 1376264 | tf_op jit(solution)/shard_map/ppermute | solution.py:79
  218.8 2.1 copy-start.7
  218.8 2.1 copy-start.2
  220.9 8.5 %collective-permute-start.13 = (bf16[1024,1792]{1,0:T(8,128)(2,1)}, bf16[1024,1792]{1,0:T(8,128)(2,1)}, u32[]{:S(2)}, u32[]{:S(2)}) collective-permute-start(bf16[1024,1792]{1,0:T(8,128)(2,1)} %bitcast.22), channel_id=1, source_target_pairs={{0,16},{16,0},{32,48},{48,32},{64,80},{80,64},{96,112},{112,96},{1... | collective-permute-start | bytes 11010056 | tf_op jit(solution)/shard_map/ppermute | solution.py:84
  220.9 2.0 copy-start.8
Sparse Core Ops, SparseCore 0:
  9.5 54.0 all-gather.1

commit v3 on v2

--- a/solution.py
+++ b/solution.py
@@ -46,20 +46,25 @@
     got = lax.ppermute(send, "row", swap)
     keep = jnp.dot(keep, weights, preferred_element_type=jnp.float32).astype(jnp.bfloat16)
     keep = lax.optimization_barrier(keep)
-    pair = (keep.astype(jnp.float32) + got.astype(jnp.float32)).astype(jnp.bfloat16)
     if after is not None:
-        pair, after = lax.optimization_barrier((pair, after))
+        keep, got, after = lax.optimization_barrier((keep, got, after))
     chunk = rows // 2 // n_y
-    pair = pair.reshape(n_y, chunk, width)
+    keep = keep.reshape(n_y, chunk, width)
+    got = got.reshape(n_y, chunk, width)
     results = []
     for direction, cols in ((1, slice(0, width // 2)), (-1, slice(width // 2, width))):
-        own = pair[:, :, cols]
+
+        def own(index, cols=cols):
+            mine = lax.dynamic_index_in_dim(keep, index, 0, keepdims=False)[:, cols]
+            theirs = lax.dynamic_index_in_dim(got, index, 0, keepdims=False)[:, cols]
+            return mine.astype(jnp.float32) + theirs.astype(jnp.float32)
+
         index = (y - direction) % n_y
-        acc = lax.dynamic_index_in_dim(own, index, 0, keepdims=False)
+        acc = own(index)
         for step in range(n_y - 1):
-            got = lax.ppermute(acc.astype(jnp.bfloat16), "row", row_perm(n_row, direction))
+            received = lax.ppermute(acc.astype(jnp.bfloat16), "row", row_perm(n_row, direction))
             index = (index - direction) % n_y
-            acc = got.astype(jnp.float32) + lax.dynamic_index_in_dim(own, index, 0, keepdims=False)
+            acc = received.astype(jnp.float32) + own(index)
         results.append(acc)
     return results
 

time: 304 us -> 294 us (0.967)
  other arithmetic: 35.1 us -> 23.1 us
    convert_element_type x1 -> x0, other arithmetic: 10 us -> none  [row_reduce_scatter(): (keep.astype(jnp.float32) + got.astype(jnp.float32)).astype(jnp.bfloat16)]
    squeeze x2, local copies, waits for them, and re-layouts: 2.27 us -> 10.7 us  [the longest x1 7.87 us: own(): theirs = lax.dynamic_index_in_dim(got, index, 0, keepdims=False)[:, cols]]
    slice x1 -> x0, local copies, waits for them, and re-layouts: 5.42 us -> none  [row_reduce_scatter(): own = pair[:, :, cols]]
    convert_element_type x4 -> x6, other arithmetic: 7.83 us -> 4.99 us  [row_reduce_scatter(): acc.astype(jnp.bfloat16)]
    unnamed x20 -> x22, local copies, waits for them, and re-layouts: 14.4 us -> 13.5 us
  transfers between devices with their start and end apart: 15 -> 15, of which waited for: 10 -> 8; matrix products, arithmetic and copies ran while one was open for 18% -> 16% of each run, Pallas kernels for 0% -> 0%
where the time goes in v3:
time: 294 us
  waiting for transfers between devices  115 us (39%)
  blocking collectives  56.7 us (19%)
  matrix products  37.8 us (13%)
  local copies, waits for them, and re-layouts  27.1 us (9%)
  other arithmetic  23.1 us (8%)
  starting transfers between devices  20.3 us (7%)
  between operations  13.7 us (5%)
    ppermute x6, waiting for transfers between devices, row_reduce_scatter(): lax.ppermute(acc.astype(jnp.bfloat16), 'row', row_perm(n_row, direction))  58.5 us
    all_to_all x1, blocking collectives, on_device(): terms = lax.all_to_all(terms, 'col', 0, 0, tiled=False)  56.7 us
    all_gather x1, waiting for transfers between devices, on_device(): gathered = lax.all_gather(tokens, 'col', axis=0, tiled=True)  34.4 us
    ppermute x6, waiting for transfers between devices, row_all_gather(): held = lax.ppermute(held, 'row', row_perm(n_row, direction))  21.7 us
    unnamed x22, local copies, waits for them, and re-layouts  13.5 us
    dot_general x1, matrix products, row_reduce_scatter(): jnp.dot(send, weights, preferred_element_type=jnp.float32)  13.4 us
    dot_general x1, matrix products, row_reduce_scatter(): jnp.dot(keep, weights, preferred_element_type=jnp.float32)  11.5 us
    ppermute x6, starting transfers between devices, row_all_gather(): held = lax.ppermute(held, 'row', row_perm(n_row, direction))  10.3 us
  transfers between devices with their start and end apart: 15, of which 8 were waited for; matrix products, arithmetic and copies ran while one was open for 16% of the time, Pallas kernels for 0%

profile of v3, /device:TPU:0, one launch (start us, length us, event | category | flops | bytes accessed | tf_op | source)
XLA Modules:
  0.0 293.9 jit_solution(18239976783153450082)
XLA Ops:
  6.5 0.7 all-gather.2.cloned.1.call-update
  7.3 6.0 %copy.14 = bf16[1024,1792]{0,1:T(8,128)(2,1)} copy(bf16[1024,1792]{1,0:T(8,128)(2,1)} %param.12) | data formatting | bytes 7340032 | tf_op args[2]
  13.3 6.0 %copy.13 = bf16[1024,1792]{0,1:T(8,128)(2,1)} copy(bf16[1024,1792]{1,0:T(8,128)(2,1)} %param.11) | data formatting | bytes 7340032 | tf_op args[1]
  19.2 0.1 iota_compare_fusion.4
  19.3 0.3 fusion.11
  19.7 0.1 iota_compare_fusion.5
  19.7 0.3 fusion.9
  20.1 0.5 broadcast_in_dim.93
  20.6 5.2 %bitcast_select_fusion.1 = bf16[1024,1792]{0,1:T(8,128)(2,1)} fusion(bf16[1024,1792]{0,1:T(8,128)(2,1)} %copy.14, pred[224,8,8,128]{3,2,1,0:T(8,128)(4,1)S(1)} %bitcast.88), kind=kLoop, calls=%fused_computation.4 | loop fusion | flops 1835008 | bytes 9175040 | tf_op jit(solution)/shard_map/jit(_where)/select_n | solution.py:25
  25.8 0.5 broadcast_in_dim.90
  26.3 2.8 bitcast_select_fusion.2
  29.2 34.4 %all-gather.2.cloned.1.call-done = bf16[2048,1024]{1,0:T(8,128)(2,1)} async-done(((bf16[128,1024]{1,0:T(8,128)(2,1)}), bf16[2048,1024]{1,0:T(8,128)(2,1)}) %all-gather.2.cloned.1.call-update) | async-done | bytes 4194320 | tf_op jit(solution)/shard_map/all_gather | solution.py:196
  63.6 13.4 %convolution_convert_fusion = bf16[1024,3584]{1,0:T(8,128)(2,1)} fusion(bf16[1024,1792]{0,1:T(8,128)(2,1)} %bitcast_select_fusion.1, bf16[1024,1792]{0,1:T(8,128)(2,1)} %bitcast_select_fusion.2, bf16[2,1024,1024]{2,1,0:T(8,128)(2,1)} %bitcast.95, s32[]{:T(128)S(6)} %select_n.149), kind=kOutput, calls=%fused_computation | convolution fusion | flops 7534542848 | bytes 16777220 | tf_op jit(solution)/shard_map/dot_general | solution.py:44
  77.0 0.0 collective-permute-start
  77.0 11.5 %convolution_convert_fusion.1 = bf16[1024,3584]{1,0:T(8,128)(2,1)S(1)} fusion(bf16[1024,1792]{0,1:T(8,128)(2,1)} %bitcast_select_fusion.1, bf16[1024,1792]{0,1:T(8,128)(2,1)} %bitcast_select_fusion.2, bf16[2,1024,1024]{2,1,0:T(8,128)(2,1)} %bitcast.96, s32[]{:T(128)S(6)} %select_n.143), kind=kOutput, calls=%fused_computation.1 | convolution fusion | flops 7534542848 | bytes 16777220 | tf_op jit(solution)/shard_map/dot_general | solution.py:47
  88.5 2.8 dynamic-slice_bitcast_fusion.9
  91.4 7.9 %dynamic-slice_bitcast_fusion.8 = (bf16[256,3584]{1,0:T(8,128)(2,1)}, bf16[256,3584]{1,0:T(8,128)(2,1)}, bf16[256,3584]{1,0:T(8,128)(2,1)S(1)}, bf16[256,3584]{1...) fusion(bf16[4,256,3584]{2,1,0:T(8,128)(2,1)} %bitcast.7, ...), kind=kLoop, calls=%fused_computation.27 | loop fusion | bytes 29360160 | tf_op jit(solution)/shard_map/jit(dynamic_index_in_dim)/squeeze | solution.py:59
  99.2 1.5 add_convert_fusion.5
  100.8 1.6 collective-permute-start.1
  102.3 0.2 add_convert_fusion.2
  102.5 1.8 collective-permute-start.4
  104.4 20.4 %collective-permute-done.1 = bf16[256,1792]{1,0:T(8,128)(2,1)S(1)} collective-permute-done((bf16[256,1792]{1,0:T(8,128)(2,1)S(1)}, bf16[256,1792]{1,0:T(8,128)(2,1)S(1)}, u32[]{:S(2)}, u32[]{:S(2)}) %collective-permute-start.1) | collective-permute-done | bytes 917536 | tf_op jit(solution)/shard_map/ppermute | solution.py:65
  124.8 0.3 add_convert_fusion.4
  125.1 0.3 collective-permute-start.2
  125.5 0.0 collective-permute-done.4
  125.5 0.3 add_convert_fusion.1
  125.8 3.0 %collective-permute-start.5 = (bf16[256,1792]{1,0:T(8,128)(2,1)S(1)}, bf16[256,1792]{1,0:T(8,128)(2,1)S(1)}, u32[]{:S(2)}, u32[]{:S(2)}) collective-permute-start(bf16[256,1792]{1,0:T(8,128)(2,1)S(1)} %add_convert_fusion.1), channel_id=1, source_target_pairs={{0,96},{16,112},{32,0},{48,16},{64,32},{80,48},{96,64},{112,80},{1... | collective-permute-start | bytes 2752520 | tf_op jit(solution)/shard_map/ppermute | solution.py:65
  128.8 19.5 %collective-permute-done.2 = bf16[256,1792]{1,0:T(8,128)(2,1)S(1)} collective-permute-done((bf16[256,1792]{1,0:T(8,128)(2,1)S(1)}, bf16[256,1792]{1,0:T(8,128)(2,1)S(1)}, u32[]{:S(2)}, u32[]{:S(2)}) %collective-permute-start.2) | collective-permute-done | bytes 917536 | tf_op jit(solution)/shard_map/ppermute | solution.py:65
  148.3 1.3 add_convert_fusion.3
  149.6 0.0 collective-permute-done.5
  149.6 1.3 add_convert_fusion
  150.9 3.2 %collective-permute-start.6 = (bf16[256,1792]{1,0:T(8,128)(2,1)}, bf16[256,1792]{1,0:T(8,128)(2,1)}, u32[]{:S(2)}, u32[]{:S(2)}) collective-permute-start(bf16[256,1792]{1,0:T(8,128)(2,1)} %add_convert_fusion), channel_id=1, source_target_pairs={{0,96},{16,112},{32,0},{48,16},{64,32},{80,48},{96,64},{112,80},{1... | collective-permute-start | bytes 2752520 | tf_op jit(solution)/shard_map/ppermute | solution.py:65
  154.1 17.9 %collective-permute-done.3 = bf16[256,1792]{1,0:T(8,128)(2,1)S(1)} collective-permute-done((bf16[256,1792]{1,0:T(8,128)(2,1)}, bf16[256,1792]{1,0:T(8,128)(2,1)S(1)}, u32[]{:S(2)}, u32[]{:S(2)}) %collective-permute-start.3) | collective-permute-done | bytes 917536 | tf_op jit(solution)/shard_map/ppermute | solution.py:65
  172.0 0.7 collective-permute-done.6
  172.7 3.0 %multiply_convert_fusion = bf16[256,1792]{1,0:T(8,128)(2,1)S(1)} fusion(bf16[256,1792]{1,0:T(8,128)(2,1)} %collective-permute-done.6, bf16[256,1792]{1,0:T(8,128)(2,1)S(1)} %collective-permute-done.3, bf16[256,3584]{1,0:T(8,128)(2,1)} %get-tuple-element.14, bf16[256,3584]{1,0:T(8,128)(2,1)} %get-tuple-element.6, bf16[256,3584]{1,0:T(8,128)(2,1)} %get-tuple-element.13, ...), kind=kLoop, calls=%fused_computation.15 | loop fusion | flops 7340032 | bytes 6422528 | tf_op jit(solution)/shard_map/convert_element_type | solution.py:203
  175.7 0.1 fusion.18
  175.8 0.1 collective-permute-start.7
  175.9 3.8 %collective-permute-start.10 = (bf16[256,896]{1,0:T(8,128)(2,1)S(1)}, bf16[256,896]{1,0:T(8,128)(2,1)S(1)}, u32[]{:S(2)}, u32[]{:S(2)}) collective-permute-start(bf16[256,896]{1,0:T(8,128)(2,1)S(1)} %get-tuple-element.22), channel_id=1, source_target_pairs={{0,96},{16,112},{32,0},{48,16},{64,32},{80,48},{96,64},{112,80},{1... | collective-permute-start | bytes 1376264 | tf_op jit(solution)/shard_map/ppermute | solution.py:84
  179.6 0.1 broadcast.73.clone.1
  179.8 0.1 bitcast_dynamic-update-slice_fusion.9
  179.8 0.1 broadcast.73.clone
  180.0 0.1 bitcast_dynamic-update-slice_fusion.5
  180.1 7.8 %collective-permute-done.7 = bf16[256,896]{1,0:T(8,128)(2,1)S(1)} collective-permute-done((bf16[256,896]{1,0:T(8,128)(2,1)S(1)}, bf16[256,896]{1,0:T(8,128)(2,1)S(1)}, u32[]{:S(2)}, u32[]{:S(2)}) %collective-permute-start.7) | collective-permute-done | bytes 458784 | tf_op jit(solution)/shard_map/ppermute | solution.py:84
  187.9 0.0 collective-permute-start.8
  187.9 3.2 %collective-permute-start.11 = (bf16[256,896]{1,0:T(8,128)(2,1)S(1)}, bf16[256,896]{1,0:T(8,128)(2,1)S(1)}, u32[]{:S(2)}, u32[]{:S(2)}) collective-permute-start(bf16[256,896]{1,0:T(8,128)(2,1)S(1)} %collective-permute-done.10), channel_id=1, source_target_pairs={{0,96},{16,112},{32,0},{48,16},{64,32},{80,48},{96,64},{112,80},{1... | collective-permute-start | bytes 1376264 | tf_op jit(solution)/shard_map/ppermute | solution.py:84
  191.2 0.1 bitcast_dynamic-update-slice_fusion.4
  191.2 7.3 %collective-permute-done.8 = bf16[256,896]{1,0:T(8,128)(2,1)S(1)} collective-permute-done((bf16[256,896]{1,0:T(8,128)(2,1)S(1)}, bf16[256,896]{1,0:T(8,128)(2,1)S(1)}, u32[]{:S(2)}, u32[]{:S(2)}) %collective-permute-start.8) | collective-permute-done | bytes 458784 | tf_op jit(solution)/shard_map/ppermute | solution.py:84
  198.6 3.2 %collective-permute-start.12 = (bf16[256,896]{1,0:T(8,128)(2,1)S(1)}, bf16[256,896]{1,0:T(8,128)(2,1)S(1)}, u32[]{:S(2)}, u32[]{:S(2)}) collective-permute-start(bf16[256,896]{1,0:T(8,128)(2,1)S(1)} %collective-permute-done.11), channel_id=1, source_target_pairs={{0,96},{16,112},{32,0},{48,16},{64,32},{80,48},{96,64},{112,80},{1... | collective-permute-start | bytes 1376264 | tf_op jit(solution)/shard_map/ppermute | solution.py:84
  201.9 0.1 bitcast_dynamic-update-slice_fusion.3
  201.9 6.5 %collective-permute-done.9 = bf16[256,896]{1,0:T(8,128)(2,1)S(1)} collective-permute-done((bf16[256,896]{1,0:T(8,128)(2,1)S(1)}, bf16[256,896]{1,0:T(8,128)(2,1)S(1)}, u32[]{:S(2)}, u32[]{:S(2)}) %collective-permute-start.9) | collective-permute-done | bytes 458784 | tf_op jit(solution)/shard_map/ppermute | solution.py:84
  208.5 0.1 bitcast_dynamic-update-slice_fusion.2
  208.6 0.0 copy-start.8
  208.6 0.0 copy-start.3
  208.6 2.0 pad_maximum_fusion.3
  210.6 0.1 iota_compare_fusion.3
  210.7 0.3 fusion.7
  211.0 0.5 broadcast_in_dim.103
  211.6 0.0 copy-start.9
  211.6 0.5 broadcast_in_dim.89
  212.1 1.5 copy-done.9
  213.6 6.4 %bitcast_dynamic-update-slice_fusion.1 = bf16[2,1024,1024]{2,1,0:T(8,128)(2,1)S(1)} fusion(bf16[2,1024,1024]{2,1,0:T(8,128)(2,1)S(1)} %broadcast_in_dim.89, s32[]{:T(128)S(6)} %select_n.143, bf16[1024,1792]{1,0:T(8,128)(2,1)} %bitcast.31, bf16[1792,1024]{1,0:T(8,128)(2,1)S(1)} %copy-done.9, pred[224,8,8,128]{3,2,1,0:T(8,128)(4,1)S(1)} %bitcast.90), kind=kOutput, calls=%fused_computation.8 | convolution fusion | flops 3760979968 | bytes 11272196 | tf_op jit(solution)/shard_map/dot_general | solution.py:90
  220.1 6.5 %bitcast_dynamic-update-slice_fusion = bf16[2,1024,1024]{2,1,0:T(8,128)(2,1)S(1)} fusion(bf16[2,1024,1024]{2,1,0:T(8,128)(2,1)S(1)} %bitcast_dynamic-update-slice_fusion.1, s32[]{:T(128)S(6)} %select_n.149, bf16[1024,1792]{1,0:T(8,128)(2,1)} %collective-permute-done.13, bf16[1792,1024]{1,0:T(8,128)(2,1)S(1)} %copy-done.9, ...), kind=kOutput, calls=%fused_computation.7 | convolution fusion | flops 3760979968 | bytes 11272196 | tf_op jit(solution)/shard_map/dot_general | solution.py:91
  226.6 56.7 %all_to_all.5 = bf16[16,128,1024]{2,1,0:T(8,128)(2,1)} all-to-all(bf16[16,128,1024]{2,1,0:T(8,128)(2,1)S(1)} %bitcast.87), channel_id=1, replica_groups=mesh['row'=8,'col'=16] {'col'}, dimensions={0} | all-to-all | bytes 8388608 | tf_op jit(solution)/shard_map/all_to_all | solution.py:210
  283.2 3.9 %reduce_sum.12 = bf16[128,1024]{1,0:T(8,128)(2,1)} reduce(bf16[16,128,1024]{2,1,0:T(8,128)(2,1)} %all_to_all.5, bf16[]{:T(256)} %constant.178.clone.1), dimensions={0}, to_apply=%region_3.4 | reduce | flops 1966080 | bytes 4456450 | tf_op jit(solution)/shard_map/reduce_sum | solution.py:211
  (30 shorter events, 0.2 us)
Async XLA Ops:
  6.5 57.0 %all-gather.2.cloned.1.call-start = ((), (), s32[]{:S(2)}) async-start(), calls=%async_computation.1 | async-start | bytes 4456448 | tf_op jit(solution)/shard_map/all_gather | solution.py:196
  13.2 6.0 %copy-start.6 = (s32[14]{0:T(128)S(1)}, s32[14]{0:T(128)}, u32[]{:S(2)}) copy-start(s32[14]{0:T(128)} %param.17) | copy-start | bytes 172
  13.2 6.1 %copy-start.4 = (s32[14,48]{1,0:T(8,128)S(1)}, s32[14,48]{1,0:T(8,128)}, u32[]{:S(2)}) copy-start(s32[14,48]{1,0:T(8,128)} %param.16) | copy-start | bytes 8068
  13.2 6.1 %copy-start.5 = (s32[14,48]{1,0:T(8,128)S(1)}, s32[14,48]{1,0:T(8,128)}, u32[]{:S(2)}) copy-start(s32[14,48]{1,0:T(8,128)} %param.14) | copy-start | bytes 8068
  13.2 6.4 %copy-start.7 = (s32[14]{0:T(128)S(1)}, s32[14]{0:T(128)}, u32[]{:S(2)}) copy-start(s32[14]{0:T(128)} %param.15) | copy-start | bytes 172
  20.6 5.7 %copy-start = (bf16[1024,1792]{0,1:T(8,128)(2,1)S(1)}, bf16[1024,1792]{0,1:T(8,128)(2,1)}, u32[]{:S(2)}) copy-start(bf16[1024,1792]{0,1:T(8,128)(2,1)} %copy.13) | copy-start | bytes 11010052
  77.0 14.4 %collective-permute-start = (bf16[1024,3584]{1,0:T(8,128)(2,1)}, bf16[1024,3584]{1,0:T(8,128)(2,1)}, u32[]{:S(2)}, u32[]{:S(2)}) collective-permute-start(bf16[1024,3584]{1,0:T(8,128)(2,1)} %convolution_convert_fusion), channel_id=1, source_target_pairs={{0,16},{16,0},{32,48},{48,32},{64,80},{80,64},{96,112},{112,96},{1... | collective-permute-start | bytes 22020104 | tf_op jit(solution)/shard_map/ppermute | solution.py:46
  91.4 7.9 %copy-start.2 = (bf16[256,3584]{1,0:T(8,128)(2,1)S(1)}, bf16[256,3584]{1,0:T(8,128)(2,1)}, u32[]{:S(2)}) copy-start(bf16[256,3584]{1,0:T(8,128)(2,1)} %get-tuple-element.12) | copy-start | bytes 5505028
  99.2 3.1 %copy-start.1 = (bf16[256,3584]{1,0:T(8,128)(2,1)S(1)}, bf16[256,3584]{1,0:T(8,128)(2,1)}, u32[]{:S(2)}) copy-start(bf16[256,3584]{1,0:T(8,128)(2,1)} %get-tuple-element.9) | copy-start | bytes 5505028
  100.8 24.0 %collective-permute-start.1 = (bf16[256,1792]{1,0:T(8,128)(2,1)S(1)}, bf16[256,1792]{1,0:T(8,128)(2,1)S(1)}, u32[]{:S(2)}, u32[]{:S(2)}) collective-permute-start(bf16[256,1792]{1,0:T(8,128)(2,1)S(1)} %add_convert_fusion.5), channel_id=1, source_target_pairs={{0,32},{16,48},{32,64},{48,80},{64,96},{80,112},{96,0},{112,16},{1... | collective-permute-start | bytes 2752520 | tf_op jit(solution)/shard_map/ppermute | solution.py:65
  102.5 22.9 %collective-permute-start.4 = (bf16[256,1792]{1,0:T(8,128)(2,1)S(1)}, bf16[256,1792]{1,0:T(8,128)(2,1)S(1)}, u32[]{:S(2)}, u32[]{:S(2)}) collective-permute-start(bf16[256,1792]{1,0:T(8,128)(2,1)S(1)} %add_convert_fusion.2), channel_id=1, source_target_pairs={{0,96},{16,112},{32,0},{48,16},{64,32},{80,48},{96,64},{112,80},{1... | collective-permute-start | bytes 2752520 | tf_op jit(solution)/shard_map/ppermute | solution.py:65
  125.1 23.2 %collective-permute-start.2 = (bf16[256,1792]{1,0:T(8,128)(2,1)S(1)}, bf16[256,1792]{1,0:T(8,128)(2,1)S(1)}, u32[]{:S(2)}, u32[]{:S(2)}) collective-permute-start(bf16[256,1792]{1,0:T(8,128)(2,1)S(1)} %add_convert_fusion.4), channel_id=1, source_target_pairs={{0,32},{16,48},{32,64},{48,80},{64,96},{80,112},{96,0},{112,16},{1... | collective-permute-start | bytes 2752520 | tf_op jit(solution)/shard_map/ppermute | solution.py:65
  125.8 23.8 %collective-permute-start.5 = (bf16[256,1792]{1,0:T(8,128)(2,1)S(1)}, bf16[256,1792]{1,0:T(8,128)(2,1)S(1)}, u32[]{:S(2)}, u32[]{:S(2)}) collective-permute-start(bf16[256,1792]{1,0:T(8,128)(2,1)S(1)} %add_convert_fusion.1), channel_id=1, source_target_pairs={{0,96},{16,112},{32,0},{48,16},{64,32},{80,48},{96,64},{112,80},{1... | collective-permute-start | bytes 2752520 | tf_op jit(solution)/shard_map/ppermute | solution.py:65
  149.6 22.5 %collective-permute-start.3 = (bf16[256,1792]{1,0:T(8,128)(2,1)}, bf16[256,1792]{1,0:T(8,128)(2,1)S(1)}, u32[]{:S(2)}, u32[]{:S(2)}) collective-permute-start(bf16[256,1792]{1,0:T(8,128)(2,1)} %add_convert_fusion.3), channel_id=1, source_target_pairs={{0,32},{16,48},{32,64},{48,80},{64,96},{80,112},{96,0},{112,16},{1... | collective-permute-start | bytes 2752520 | tf_op jit(solution)/shard_map/ppermute | solution.py:65
  150.9 21.8 %collective-permute-start.6 = (bf16[256,1792]{1,0:T(8,128)(2,1)}, bf16[256,1792]{1,0:T(8,128)(2,1)}, u32[]{:S(2)}, u32[]{:S(2)}) collective-permute-start(bf16[256,1792]{1,0:T(8,128)(2,1)} %add_convert_fusion), channel_id=1, source_target_pairs={{0,96},{16,112},{32,0},{48,16},{64,32},{80,48},{96,64},{112,80},{1... | collective-permute-start | bytes 2752520 | tf_op jit(solution)/shard_map/ppermute | solution.py:65
  175.8 12.1 %collective-permute-start.7 = (bf16[256,896]{1,0:T(8,128)(2,1)S(1)}, bf16[256,896]{1,0:T(8,128)(2,1)S(1)}, u32[]{:S(2)}, u32[]{:S(2)}) collective-permute-start(bf16[256,896]{1,0:T(8,128)(2,1)S(1)} %get-tuple-element.21), channel_id=1, source_target_pairs={{0,32},{16,48},{32,64},{48,80},{64,96},{80,112},{96,0},{112,16},{1... | collective-permute-start | bytes 1376264 | tf_op jit(solution)/shard_map/ppermute | solution.py:84
  175.9 12.0 %collective-permute-start.10 = (bf16[256,896]{1,0:T(8,128)(2,1)S(1)}, bf16[256,896]{1,0:T(8,128)(2,1)S(1)}, u32[]{:S(2)}, u32[]{:S(2)}) collective-permute-start(bf16[256,896]{1,0:T(8,128)(2,1)S(1)} %get-tuple-element.22), channel_id=1, source_target_pairs={{0,96},{16,112},{32,0},{48,16},{64,32},{80,48},{96,64},{112,80},{1... | collective-permute-start | bytes 1376264 | tf_op jit(solution)/shard_map/ppermute | solution.py:84
  187.9 10.7 %collective-permute-start.8 = (bf16[256,896]{1,0:T(8,128)(2,1)S(1)}, bf16[256,896]{1,0:T(8,128)(2,1)S(1)}, u32[]{:S(2)}, u32[]{:S(2)}) collective-permute-start(bf16[256,896]{1,0:T(8,128)(2,1)S(1)} %collective-permute-done.7), channel_id=1, source_target_pairs={{0,32},{16,48},{32,64},{48,80},{64,96},{80,112},{96,0},{112,16},{1... | collective-permute-start | bytes 1376264 | tf_op jit(solution)/shard_map/ppermute | solution.py:84
  187.9 10.7 %collective-permute-start.11 = (bf16[256,896]{1,0:T(8,128)(2,1)S(1)}, bf16[256,896]{1,0:T(8,128)(2,1)S(1)}, u32[]{:S(2)}, u32[]{:S(2)}) collective-permute-start(bf16[256,896]{1,0:T(8,128)(2,1)S(1)} %collective-permute-done.10), channel_id=1, source_target_pairs={{0,96},{16,112},{32,0},{48,16},{64,32},{80,48},{96,64},{112,80},{1... | collective-permute-start | bytes 1376264 | tf_op jit(solution)/shard_map/ppermute | solution.py:84
  198.6 9.8 %collective-permute-start.9 = (bf16[256,896]{1,0:T(8,128)(2,1)S(1)}, bf16[256,896]{1,0:T(8,128)(2,1)S(1)}, u32[]{:S(2)}, u32[]{:S(2)}) collective-permute-start(bf16[256,896]{1,0:T(8,128)(2,1)S(1)} %collective-permute-done.8), channel_id=1, source_target_pairs={{0,32},{16,48},{32,64},{48,80},{64,96},{80,112},{96,0},{112,16},{1... | collective-permute-start | bytes 1376264 | tf_op jit(solution)/shard_map/ppermute | solution.py:84
  198.6 9.9 %collective-permute-start.12 = (bf16[256,896]{1,0:T(8,128)(2,1)S(1)}, bf16[256,896]{1,0:T(8,128)(2,1)S(1)}, u32[]{:S(2)}, u32[]{:S(2)}) collective-permute-start(bf16[256,896]{1,0:T(8,128)(2,1)S(1)} %collective-permute-done.11), channel_id=1, source_target_pairs={{0,96},{16,112},{32,0},{48,16},{64,32},{80,48},{96,64},{112,80},{1... | collective-permute-start | bytes 1376264 | tf_op jit(solution)/shard_map/ppermute | solution.py:84
  208.6 2.1 copy-start.8
  208.6 2.1 copy-start.3
  210.6 9.5 %collective-permute-start.13 = (bf16[1024,1792]{1,0:T(8,128)(2,1)}, bf16[1024,1792]{1,0:T(8,128)(2,1)}, u32[]{:S(2)}, u32[]{:S(2)}) collective-permute-start(bf16[1024,1792]{1,0:T(8,128)(2,1)} %bitcast.31), channel_id=1, source_target_pairs={{0,16},{16,0},{32,48},{48,32},{64,80},{80,64},{96,112},{112,96},{1... | collective-permute-start | bytes 11010056 | tf_op jit(solution)/shard_map/ppermute | solution.py:89
  211.6 2.0 copy-start.9
Sparse Core Ops, SparseCore 0:
  9.5 54.0 all-gather.1

commit v4 on v3

--- a/solution.py
+++ b/solution.py
@@ -37,27 +37,26 @@
     y = r // 2
     core = r % 2
     rows = tokens.shape[0]
-    width = weights.shape[1]
     halves = tokens.reshape(2, rows // 2, tokens.shape[1])
     send = lax.dynamic_index_in_dim(halves, 1 - core, 0, keepdims=False)
     keep = lax.dynamic_index_in_dim(halves, core, 0, keepdims=False)
-    send = jnp.dot(send, weights, preferred_element_type=jnp.float32).astype(jnp.bfloat16)
     swap = [(i, i ^ 1) for i in range(n_row)]
-    got = lax.ppermute(send, "row", swap)
-    keep = jnp.dot(keep, weights, preferred_element_type=jnp.float32).astype(jnp.bfloat16)
-    keep = lax.optimization_barrier(keep)
-    if after is not None:
-        keep, got, after = lax.optimization_barrier((keep, got, after))
     chunk = rows // 2 // n_y
-    keep = keep.reshape(n_y, chunk, width)
-    got = got.reshape(n_y, chunk, width)
+    sent = []
+    for w in weights:
+        part = jnp.dot(send, w, preferred_element_type=jnp.float32).astype(jnp.bfloat16)
+        sent.append(lax.ppermute(part, "row", swap))
     results = []
-    for direction, cols in ((1, slice(0, width // 2)), (-1, slice(width // 2, width))):
-
-        def own(index, cols=cols):
-            mine = lax.dynamic_index_in_dim(keep, index, 0, keepdims=False)[:, cols]
-            theirs = lax.dynamic_index_in_dim(got, index, 0, keepdims=False)[:, cols]
-            return mine.astype(jnp.float32) + theirs.astype(jnp.float32)
+    for direction, w, got in ((1, weights[0], sent[0]), (-1, weights[1], sent[1])):
+        mine = jnp.dot(keep, w, preferred_element_type=jnp.float32).astype(jnp.bfloat16)
+        mine = lax.optimization_barrier(mine).reshape(n_y, chunk, w.shape[1])
+        got = got.reshape(n_y, chunk, w.shape[1])
+
+        def own(index, mine=mine, got=got):
+            return (
+                lax.dynamic_index_in_dim(mine, index, 0, keepdims=False).astype(jnp.float32)
+                + lax.dynamic_index_in_dim(got, index, 0, keepdims=False).astype(jnp.float32)
+            )
 
         index = (y - direction) % n_y
         acc = own(index)
@@ -191,7 +190,6 @@
     down_pruned = apply_mask(
         down_weight, local_mask(down_keep, down_count, col_offset, hidden_blocks).T, BLOCK
     )
-    both_weights = jnp.concatenate([gate_pruned, up_pruned], axis=1)
     rows = tokens.shape[0] // CHUNKS
     gathered = lax.all_gather(tokens, "col", axis=0, tiled=True)
     gathered = gathered.reshape(n_col, CHUNKS, rows, gathered.shape[1])
@@ -199,7 +197,7 @@
     previous = None
     for k in range(CHUNKS):
         chunk = gathered[:, k].reshape(n_col * rows, gathered.shape[3])
-        gate_sums, up_sums = row_reduce_scatter(chunk, both_weights, n_row, previous)
+        gate_sums, up_sums = row_reduce_scatter(chunk, (gate_pruned, up_pruned), n_row, previous)
         hidden = (jax.nn.silu(gate_sums) * up_sums).astype(jnp.bfloat16)
         terms = row_all_gather(hidden, n_row, down_pruned)
         previous = terms

time: 294 us -> 291 us (0.990)
  local copies, waits for them, and re-layouts: 27.1 us -> 18.2 us
  waiting for transfers between devices: 115 us -> 118 us
    squeeze x2 -> x0, local copies, waits for them, and re-layouts: 10.7 us -> none  [the longest x1 7.87 us: own(): theirs = lax.dynamic_index_in_dim(got, index, 0, keepdims=False)[:, cols]]
    all_gather x1, waiting for transfers between devices: 34.4 us -> 43.8 us  [on_device(): gathered = lax.all_gather(tokens, 'col', axis=0, tiled=True)]
    select_n x2 -> x0, other arithmetic: 7.98 us -> none  [apply_mask(): jnp.where(block_mask[:, None, :, None], shaped, jnp.zeros((), weight.dtype))]
    convert_element_type x6, other arithmetic: 4.99 us -> 12.7 us  [row_reduce_scatter(): acc.astype(jnp.bfloat16)]
    ppermute x6, waiting for transfers between devices: 58.5 us -> 52.6 us  [row_reduce_scatter(): lax.ppermute(acc.astype(jnp.bfloat16), 'row', row_perm(n_row, direction))]
    dot_general x2 -> x4, matrix products: 24.9 us -> 26.8 us  [the longest x2 15 us: row_reduce_scatter(): jnp.dot(send, w, preferred_element_type=jnp.float32).astype(jnp.bfloat16)]
    unnamed x22 -> x30, local copies, waits for them, and re-layouts: 13.5 us -> 15.3 us
  transfers between devices with their start and end apart: 15 -> 16, of which waited for: 8 -> 10; matrix products, arithmetic and copies ran while one was open for 16% -> 18% of each run, Pallas kernels for 0% -> 0%
where the time goes in v4:
time: 291 us
  waiting for transfers between devices  118 us (41%)
  blocking collectives  56.6 us (19%)
  matrix products  39.7 us (14%)
  other arithmetic  22.9 us (8%)
  starting transfers between devices  21.6 us (7%)
  local copies, waits for them, and re-layouts  18.2 us (6%)
  between operations  13.7 us (5%)
    all_to_all x1, blocking collectives, on_device(): terms = lax.all_to_all(terms, 'col', 0, 0, tiled=False)  56.6 us
    ppermute x6, waiting for transfers between devices, row_reduce_scatter(): lax.ppermute(acc.astype(jnp.bfloat16), 'row', row_perm(n_row, direction))  52.6 us
    all_gather x1, waiting for transfers between devices, on_device(): gathered = lax.all_gather(tokens, 'col', axis=0, tiled=True)  43.8 us
    ppermute x6, waiting for transfers between devices, row_all_gather(): held = lax.ppermute(held, 'row', row_perm(n_row, direction))  20.8 us
    unnamed x30, local copies, waits for them, and re-layouts  15.3 us
    dot_general x2, matrix products, row_reduce_scatter(): jnp.dot(send, w, preferred_element_type=jnp.float32).astype(jnp.bfloat16)  15 us
    convert_element_type x6, other arithmetic, row_reduce_scatter(): acc.astype(jnp.bfloat16)  12.7 us
    dot_general x2, matrix products, row_reduce_scatter(): jnp.dot(keep, w, preferred_element_type=jnp.float32).astype(jnp.bfloat16)  11.8 us
  transfers between devices with their start and end apart: 16, of which 10 were waited for; matrix products, arithmetic and copies ran while one was open for 18% of the time, Pallas kernels for 0%

profile of v4, /device:TPU:0, one launch (start us, length us, event | category | flops | bytes accessed | tf_op | source)
XLA Modules:
  0.0 290.6 jit_solution(3159127821454913794)
XLA Ops:
  6.5 0.7 all-gather.2.cloned.1.call-update
  7.3 5.9 %copy.13 = bf16[1024,1792]{0,1:T(8,128)(2,1)} copy(bf16[1024,1792]{1,0:T(8,128)(2,1)} %param.11) | data formatting | bytes 7340032 | tf_op args[1]
  13.2 6.0 %copy.14 = bf16[1024,1792]{0,1:T(8,128)(2,1)} copy(bf16[1024,1792]{1,0:T(8,128)(2,1)} %param.12) | data formatting | bytes 7340032 | tf_op args[2]
  19.2 0.1 iota_compare_fusion.5
  19.3 0.3 fusion.25
  19.6 43.8 %all-gather.2.cloned.1.call-done = bf16[2048,1024]{1,0:T(8,128)(2,1)} async-done(((bf16[128,1024]{1,0:T(8,128)(2,1)}), bf16[2048,1024]{1,0:T(8,128)(2,1)}) %all-gather.2.cloned.1.call-update) | async-done | bytes 4194320 | tf_op jit(solution)/shard_map/all_gather | solution.py:194
  63.5 0.5 broadcast_in_dim.90
  64.0 0.0 copy-start.9
  64.1 9.3 %convolution_convert_fusion.2 = bf16[1024,1792]{1,0:T(8,128)(2,1)} fusion(bf16[1024,1792]{0,1:T(8,128)(2,1)} %copy.13, pred[224,8,8,128]{3,2,1,0:T(8,128)(4,1)S(1)} %bitcast.105, bf16[2,1024,1024]{2,1,0:T(8,128)(2,1)} %bitcast.112, s32[]{:T(128)S(6)} %select_n.148), kind=kOutput, calls=%fused_computation.5 | convolution fusion | flops 3761766400 | bytes 11272196 | tf_op jit(solution)/shard_map/dot_general | solution.py:47
  73.4 0.1 iota_compare_fusion.4
  73.4 0.3 fusion.27
  73.8 0.6 broadcast_in_dim.93
  74.3 5.7 %convolution_convert_fusion = bf16[1024,1792]{1,0:T(8,128)(2,1)} fusion(bf16[1024,1792]{0,1:T(8,128)(2,1)S(1)} %copy-done, pred[224,8,8,128]{3,2,1,0:T(8,128)(4,1)S(1)} %bitcast.103, bf16[2,1024,1024]{2,1,0:T(8,128)(2,1)S(1)} %bitcast.114, s32[]{:T(128)S(6)} %select_n.148), kind=kOutput, calls=%fused_computation.3 | convolution fusion | flops 3761766400 | bytes 11272196 | tf_op jit(solution)/shard_map/dot_general | solution.py:47
  80.1 0.5 collective-permute-start.4
  80.6 7.4 %convolution_convert_fusion.3 = bf16[1024,1792]{1,0:T(8,128)(2,1)S(1)} fusion(bf16[1024,1792]{0,1:T(8,128)(2,1)} %copy.13, pred[224,8,8,128]{3,2,1,0:T(8,128)(4,1)} %bitcast.106, bf16[2,1024,1024]{2,1,0:T(8,128)(2,1)} %bitcast.113, s32[]{:T(128)S(6)} %select_n.143), kind=kOutput, calls=%fused_computation.6 | convolution fusion | flops 3761766400 | bytes 11272196 | tf_op jit(solution)/shard_map/dot_general | solution.py:51
  88.0 2.1 fusion.20
  90.1 1.6 collective-permute-start.1
  91.7 4.4 %convolution_convert_fusion.1 = bf16[1024,1792]{1,0:T(8,128)(2,1)S(1)} fusion(bf16[1024,1792]{0,1:T(8,128)(2,1)S(1)} %copy-done.1, pred[224,8,8,128]{3,2,1,0:T(8,128)(4,1)S(1)} %bitcast.104, bf16[2,1024,1024]{2,1,0:T(8,128)(2,1)S(1)} %bitcast.115, s32[]{:T(128)S(6)} %select_n.143), kind=kOutput, calls=%fused_computation.4 | convolution fusion | flops 3761766400 | bytes 11272196 | tf_op jit(solution)/shard_map/dot_general | solution.py:51
  96.1 1.8 copy-done.3
  97.9 1.4 fusion.21
  99.3 1.8 collective-permute-start.5
  101.1 12.6 %collective-permute-done.1 = bf16[256,1792]{1,0:T(8,128)(2,1)} collective-permute-done((bf16[256,1792]{1,0:T(8,128)(2,1)S(1)}, bf16[256,1792]{1,0:T(8,128)(2,1)}, u32[]{:S(2)}, u32[]{:S(2)}) %collective-permute-start.1) | collective-permute-done | bytes 917536 | tf_op jit(solution)/shard_map/ppermute | solution.py:64
  113.8 2.1 fusion.13
  115.8 0.3 collective-permute-start.2
  116.2 5.3 %collective-permute-done.5 = bf16[256,1792]{1,0:T(8,128)(2,1)} collective-permute-done((bf16[256,1792]{1,0:T(8,128)(2,1)S(1)}, bf16[256,1792]{1,0:T(8,128)(2,1)}, u32[]{:S(2)}, u32[]{:S(2)}) %collective-permute-start.5) | collective-permute-done | bytes 917536 | tf_op jit(solution)/shard_map/ppermute | solution.py:64
  121.5 2.1 fusion.11
  123.5 3.0 %collective-permute-start.6 = (bf16[256,1792]{1,0:T(8,128)(2,1)S(1)}, bf16[256,1792]{1,0:T(8,128)(2,1)}, u32[]{:S(2)}, u32[]{:S(2)}) collective-permute-start(bf16[256,1792]{1,0:T(8,128)(2,1)S(1)} %fusion.11), channel_id=1, source_target_pairs={{0,96},{16,112},{32,0},{48,16},{64,32},{80,48},{96,64},{112,80},{1... | collective-permute-start | bytes 2752520 | tf_op jit(solution)/shard_map/ppermute | solution.py:64
  126.6 12.1 %collective-permute-done.2 = bf16[256,1792]{1,0:T(8,128)(2,1)} collective-permute-done((bf16[256,1792]{1,0:T(8,128)(2,1)S(1)}, bf16[256,1792]{1,0:T(8,128)(2,1)}, u32[]{:S(2)}, u32[]{:S(2)}) %collective-permute-start.2) | collective-permute-done | bytes 917536 | tf_op jit(solution)/shard_map/ppermute | solution.py:64
  138.6 2.1 fusion.12
  140.7 0.1 collective-permute-start.3
  140.8 4.4 %collective-permute-done.6 = bf16[256,1792]{1,0:T(8,128)(2,1)} collective-permute-done((bf16[256,1792]{1,0:T(8,128)(2,1)S(1)}, bf16[256,1792]{1,0:T(8,128)(2,1)}, u32[]{:S(2)}, u32[]{:S(2)}) %collective-permute-start.6) | collective-permute-done | bytes 917536 | tf_op jit(solution)/shard_map/ppermute | solution.py:64
  145.2 3.0 %fusion.10 = bf16[256,1792]{1,0:T(8,128)(2,1)} fusion(bf16[256,1792]{1,0:T(8,128)(2,1)} %collective-permute-done.6, bf16[4,256,1792]{2,1,0:T(8,128)(2,1)} %bitcast.12, s32[]{:T(128)S(6)} %select_n.161, bf16[4,256,1792]{2,1,0:T(8,128)(2,1)} %bitcast.101), kind=kLoop, calls=%fused_computation.22 | loop fusion | flops 2752512 | bytes 3670020 | tf_op jit(solution)/shard_map/convert_element_type | solution.py:64
  148.2 3.8 %collective-permute-start.7 = (bf16[256,1792]{1,0:T(8,128)(2,1)}, bf16[256,1792]{1,0:T(8,128)(2,1)S(1)}, u32[]{:S(2)}, u32[]{:S(2)}) collective-permute-start(bf16[256,1792]{1,0:T(8,128)(2,1)} %fusion.10), channel_id=1, source_target_pairs={{0,96},{16,112},{32,0},{48,16},{64,32},{80,48},{96,64},{112,80},{1... | collective-permute-start | bytes 2752520 | tf_op jit(solution)/shard_map/ppermute | solution.py:64
  152.0 10.5 %collective-permute-done.3 = bf16[256,1792]{1,0:T(8,128)(2,1)S(1)} collective-permute-done((bf16[256,1792]{1,0:T(8,128)(2,1)S(1)}, bf16[256,1792]{1,0:T(8,128)(2,1)S(1)}, u32[]{:S(2)}, u32[]{:S(2)}) %collective-permute-start.3) | collective-permute-done | bytes 917536 | tf_op jit(solution)/shard_map/ppermute | solution.py:64
  162.5 7.6 %collective-permute-done.7 = bf16[256,1792]{1,0:T(8,128)(2,1)S(1)} collective-permute-done((bf16[256,1792]{1,0:T(8,128)(2,1)}, bf16[256,1792]{1,0:T(8,128)(2,1)S(1)}, u32[]{:S(2)}, u32[]{:S(2)}) %collective-permute-start.7) | collective-permute-done | bytes 917536 | tf_op jit(solution)/shard_map/ppermute | solution.py:64
  170.1 3.0 %fusion.9 = bf16[256,1792]{1,0:T(8,128)(2,1)S(1)} fusion(bf16[256,1792]{1,0:T(8,128)(2,1)S(1)} %collective-permute-done.7, bf16[256,1792]{1,0:T(8,128)(2,1)S(1)} %collective-permute-done.3, bf16[4,256,1792]{2,1,0:T(8,128)(2,1)} %bitcast.12, s32[]{:T(128)S(6)} %select_n.163, bf16[4,256,1792]{2,1,0:T(8,128)(2,1)} %bitcast.102, ...), kind=kLoop, calls=%fused_computation.20 | loop fusion | flops 7340032 | bytes 6422536 | tf_op jit(solution)/shard_map/convert_element_type | solution.py:201
  173.1 0.1 fusion.38
  173.2 0.1 collective-permute-start.8
  173.3 3.9 %collective-permute-start.11 = (bf16[256,896]{1,0:T(8,128)(2,1)S(1)}, bf16[256,896]{1,0:T(8,128)(2,1)S(1)}, u32[]{:S(2)}, u32[]{:S(2)}) collective-permute-start(bf16[256,896]{1,0:T(8,128)(2,1)S(1)} %get-tuple-element.6), channel_id=1, source_target_pairs={{0,96},{16,112},{32,0},{48,16},{64,32},{80,48},{96,64},{112,80},{1... | collective-permute-start | bytes 1376264 | tf_op jit(solution)/shard_map/ppermute | solution.py:83
  177.2 0.1 broadcast.73.clone.1
  177.3 0.1 bitcast_dynamic-update-slice_fusion.9
  177.4 0.1 broadcast.73.clone
  177.5 0.1 bitcast_dynamic-update-slice_fusion.5
  177.6 7.1 %collective-permute-done.8 = bf16[256,896]{1,0:T(8,128)(2,1)S(1)} collective-permute-done((bf16[256,896]{1,0:T(8,128)(2,1)S(1)}, bf16[256,896]{1,0:T(8,128)(2,1)S(1)}, u32[]{:S(2)}, u32[]{:S(2)}) %collective-permute-start.8) | collective-permute-done | bytes 458784 | tf_op jit(solution)/shard_map/ppermute | solution.py:83
  184.7 3.2 %collective-permute-start.12 = (bf16[256,896]{1,0:T(8,128)(2,1)S(1)}, bf16[256,896]{1,0:T(8,128)(2,1)S(1)}, u32[]{:S(2)}, u32[]{:S(2)}) collective-permute-start(bf16[256,896]{1,0:T(8,128)(2,1)S(1)} %collective-permute-done.11), channel_id=1, source_target_pairs={{0,96},{16,112},{32,0},{48,16},{64,32},{80,48},{96,64},{112,80},{1... | collective-permute-start | bytes 1376264 | tf_op jit(solution)/shard_map/ppermute | solution.py:83
  188.0 0.1 bitcast_dynamic-update-slice_fusion.4
  188.1 7.3 %collective-permute-done.9 = bf16[256,896]{1,0:T(8,128)(2,1)S(1)} collective-permute-done((bf16[256,896]{1,0:T(8,128)(2,1)S(1)}, bf16[256,896]{1,0:T(8,128)(2,1)S(1)}, u32[]{:S(2)}, u32[]{:S(2)}) %collective-permute-start.9) | collective-permute-done | bytes 458784 | tf_op jit(solution)/shard_map/ppermute | solution.py:83
  195.4 3.2 %collective-permute-start.13 = (bf16[256,896]{1,0:T(8,128)(2,1)S(1)}, bf16[256,896]{1,0:T(8,128)(2,1)S(1)}, u32[]{:S(2)}, u32[]{:S(2)}) collective-permute-start(bf16[256,896]{1,0:T(8,128)(2,1)S(1)} %collective-permute-done.12), channel_id=1, source_target_pairs={{0,96},{16,112},{32,0},{48,16},{64,32},{80,48},{96,64},{112,80},{1... | collective-permute-start | bytes 1376264 | tf_op jit(solution)/shard_map/ppermute | solution.py:83
  198.7 0.1 bitcast_dynamic-update-slice_fusion.3
  198.7 6.3 %collective-permute-done.10 = bf16[256,896]{1,0:T(8,128)(2,1)S(1)} collective-permute-done((bf16[256,896]{1,0:T(8,128)(2,1)S(1)}, bf16[256,896]{1,0:T(8,128)(2,1)S(1)}, u32[]{:S(2)}, u32[]{:S(2)}) %collective-permute-start.10) | collective-permute-done | bytes 458784 | tf_op jit(solution)/shard_map/ppermute | solution.py:83
  205.1 0.1 bitcast_dynamic-update-slice_fusion.2
  205.2 0.0 copy-start.10
  205.2 0.0 copy-start.5
  205.2 2.1 pad_maximum_fusion
  207.3 0.1 iota_compare_fusion.3
  207.4 0.3 fusion.23
  207.7 0.5 broadcast_in_dim.103
  208.3 0.0 copy-start.13
  208.3 0.5 broadcast_in_dim.89
  208.8 1.5 copy-done.13
  210.3 6.4 %bitcast_dynamic-update-slice_fusion.1 = bf16[2,1024,1024]{2,1,0:T(8,128)(2,1)S(1)} fusion(bf16[2,1024,1024]{2,1,0:T(8,128)(2,1)S(1)} %broadcast_in_dim.89, s32[]{:T(128)S(6)} %select_n.143, bf16[1024,1792]{1,0:T(8,128)(2,1)} %bitcast.25, bf16[1792,1024]{1,0:T(8,128)(2,1)S(1)} %copy-done.13, pred[224,8,8,128]{3,2,1,0:T(8,128)(4,1)S(1)} %bitcast.107), kind=kOutput, calls=%fused_computation.9 | convolution fusion | flops 3760979968 | bytes 11272196 | tf_op jit(solution)/shard_map/dot_general | solution.py:89
  216.7 6.5 %bitcast_dynamic-update-slice_fusion = bf16[2,1024,1024]{2,1,0:T(8,128)(2,1)S(1)} fusion(bf16[2,1024,1024]{2,1,0:T(8,128)(2,1)S(1)} %bitcast_dynamic-update-slice_fusion.1, s32[]{:T(128)S(6)} %select_n.148, bf16[1024,1792]{1,0:T(8,128)(2,1)} %collective-permute-done.14, bf16[1792,1024]{1,0:T(8,128)(2,1)S(1)} %copy-done.13, ...), kind=kOutput, calls=%fused_computation.8 | convolution fusion | flops 3760979968 | bytes 11272196 | tf_op jit(solution)/shard_map/dot_general | solution.py:90
  223.2 56.6 %all_to_all.5 = bf16[16,128,1024]{2,1,0:T(8,128)(2,1)} all-to-all(bf16[16,128,1024]{2,1,0:T(8,128)(2,1)S(1)} %bitcast.94), channel_id=1, replica_groups=mesh['row'=8,'col'=16] {'col'}, dimensions={0} | all-to-all | bytes 8388608 | tf_op jit(solution)/shard_map/all_to_all | solution.py:208
  279.9 3.9 %reduce_sum.12 = bf16[128,1024]{1,0:T(8,128)(2,1)} reduce(bf16[16,128,1024]{2,1,0:T(8,128)(2,1)} %all_to_all.5, bf16[]{:T(256)} %constant.178.clone.1), dimensions={0}, to_apply=%region_3.4 | reduce | flops 1966080 | bytes 4456450 | tf_op jit(solution)/shard_map/reduce_sum | solution.py:209
  (38 shorter events, 0.2 us)
Async XLA Ops:
  6.5 56.9 %all-gather.2.cloned.1.call-start = ((), (), s32[]{:S(2)}) async-start(), calls=%async_computation.1 | async-start | bytes 4456448 | tf_op jit(solution)/shard_map/all_gather | solution.py:194
  13.2 6.0 %copy-start.8 = (s32[14]{0:T(128)S(1)}, s32[14]{0:T(128)}, u32[]{:S(2)}) copy-start(s32[14]{0:T(128)} %param.15) | copy-start | bytes 172
  13.2 6.1 %copy-start.6 = (s32[14,48]{1,0:T(8,128)S(1)}, s32[14,48]{1,0:T(8,128)}, u32[]{:S(2)}) copy-start(s32[14,48]{1,0:T(8,128)} %param.16) | copy-start | bytes 8068
  13.2 6.1 %copy-start.7 = (s32[14,48]{1,0:T(8,128)S(1)}, s32[14,48]{1,0:T(8,128)}, u32[]{:S(2)}) copy-start(s32[14,48]{1,0:T(8,128)} %param.14) | copy-start | bytes 8068
  64.0 9.3 %copy-start.4 = (pred[8,128,14,128]{1,0,3,2:T(8,128)(4,1)}, pred[8,128,14,128]{1,0,3,2:T(8,128)(4,1)S(1)}, u32[]{:S(2)}) copy-start(pred[8,128,14,128]{1,0,3,2:T(8,128)(4,1)S(1)} %broadcast_in_dim.90) | copy-start | bytes 5505028
  64.0 9.3 %copy-start.9 = (s32[14]{0:T(128)S(1)}, s32[14]{0:T(128)}, u32[]{:S(2)}) copy-start(s32[14]{0:T(128)} %param.17) | copy-start | bytes 172
  64.1 10.3 %copy-start = (bf16[1024,1792]{0,1:T(8,128)(2,1)S(1)}, bf16[1024,1792]{0,1:T(8,128)(2,1)}, u32[]{:S(2)}) copy-start(bf16[1024,1792]{0,1:T(8,128)(2,1)} %copy.14) | copy-start | bytes 11010052
  64.1 10.3 %copy-start.11 = (bf16[2048,1024]{1,0:T(8,128)(2,1)S(1)}, bf16[2048,1024]{1,0:T(8,128)(2,1)}, u32[]{:S(2)}) copy-start(bf16[2048,1024]{1,0:T(8,128)(2,1)} %all-gather.2.cloned.1.call-done) | copy-start | bytes 12582916
  73.4 14.6 %collective-permute-start = (bf16[1024,1792]{1,0:T(8,128)(2,1)}, bf16[1024,1792]{1,0:T(8,128)(2,1)}, u32[]{:S(2)}, u32[]{:S(2)}) collective-permute-start(bf16[1024,1792]{1,0:T(8,128)(2,1)} %convolution_convert_fusion.2), channel_id=1, source_target_pairs={{0,16},{16,0},{32,48},{48,32},{64,80},{80,64},{96,112},{112,96},{1... | collective-permute-start | bytes 11010056 | tf_op jit(solution)/shard_map/ppermute | solution.py:48
  80.1 16.0 %collective-permute-start.4 = (bf16[1024,1792]{1,0:T(8,128)(2,1)}, bf16[1024,1792]{1,0:T(8,128)(2,1)}, u32[]{:S(2)}, u32[]{:S(2)}) collective-permute-start(bf16[1024,1792]{1,0:T(8,128)(2,1)} %convolution_convert_fusion), channel_id=1, source_target_pairs={{0,16},{16,0},{32,48},{48,32},{64,80},{80,64},{96,112},{112,96},{1... | collective-permute-start | bytes 11010056 | tf_op jit(solution)/shard_map/ppermute | solution.py:48
  80.6 11.1 %copy-start.1 = (bf16[1024,1792]{0,1:T(8,128)(2,1)S(1)}, bf16[1024,1792]{0,1:T(8,128)(2,1)}, u32[]{:S(2)}) copy-start(bf16[1024,1792]{0,1:T(8,128)(2,1)} %copy.14) | copy-start | bytes 11010052
  80.6 11.1 %copy-start.12 = (bf16[2048,1024]{1,0:T(8,128)(2,1)S(1)}, bf16[2048,1024]{1,0:T(8,128)(2,1)}, u32[]{:S(2)}) copy-start(bf16[2048,1024]{1,0:T(8,128)(2,1)} %all-gather.2.cloned.1.call-done) | copy-start | bytes 12582916
  88.0 8.1 %copy-start.2 = (bf16[1024,1792]{1,0:T(8,128)(2,1)}, bf16[1024,1792]{1,0:T(8,128)(2,1)S(1)}, u32[]{:S(2)}) copy-start(bf16[1024,1792]{1,0:T(8,128)(2,1)S(1)} %convolution_convert_fusion.3) | copy-start | bytes 11010052
  90.1 23.7 %collective-permute-start.1 = (bf16[256,1792]{1,0:T(8,128)(2,1)S(1)}, bf16[256,1792]{1,0:T(8,128)(2,1)}, u32[]{:S(2)}, u32[]{:S(2)}) collective-permute-start(bf16[256,1792]{1,0:T(8,128)(2,1)S(1)} %fusion.20), channel_id=1, source_target_pairs={{0,32},{16,48},{32,64},{48,80},{64,96},{80,112},{96,0},{112,16},{1... | collective-permute-start | bytes 2752520 | tf_op jit(solution)/shard_map/ppermute | solution.py:64
  96.1 1.8 copy-start.3
  99.3 22.2 %collective-permute-start.5 = (bf16[256,1792]{1,0:T(8,128)(2,1)S(1)}, bf16[256,1792]{1,0:T(8,128)(2,1)}, u32[]{:S(2)}, u32[]{:S(2)}) collective-permute-start(bf16[256,1792]{1,0:T(8,128)(2,1)S(1)} %fusion.21), channel_id=1, source_target_pairs={{0,96},{16,112},{32,0},{48,16},{64,32},{80,48},{96,64},{112,80},{1... | collective-permute-start | bytes 2752520 | tf_op jit(solution)/shard_map/ppermute | solution.py:64
  115.8 22.8 %collective-permute-start.2 = (bf16[256,1792]{1,0:T(8,128)(2,1)S(1)}, bf16[256,1792]{1,0:T(8,128)(2,1)}, u32[]{:S(2)}, u32[]{:S(2)}) collective-permute-start(bf16[256,1792]{1,0:T(8,128)(2,1)S(1)} %fusion.13), channel_id=1, source_target_pairs={{0,32},{16,48},{32,64},{48,80},{64,96},{80,112},{96,0},{112,16},{1... | collective-permute-start | bytes 2752520 | tf_op jit(solution)/shard_map/ppermute | solution.py:64
  123.5 21.7 %collective-permute-start.6 = (bf16[256,1792]{1,0:T(8,128)(2,1)S(1)}, bf16[256,1792]{1,0:T(8,128)(2,1)}, u32[]{:S(2)}, u32[]{:S(2)}) collective-permute-start(bf16[256,1792]{1,0:T(8,128)(2,1)S(1)} %fusion.11), channel_id=1, source_target_pairs={{0,96},{16,112},{32,0},{48,16},{64,32},{80,48},{96,64},{112,80},{1... | collective-permute-start | bytes 2752520 | tf_op jit(solution)/shard_map/ppermute | solution.py:64
  140.7 21.8 %collective-permute-start.3 = (bf16[256,1792]{1,0:T(8,128)(2,1)S(1)}, bf16[256,1792]{1,0:T(8,128)(2,1)S(1)}, u32[]{:S(2)}, u32[]{:S(2)}) collective-permute-start(bf16[256,1792]{1,0:T(8,128)(2,1)S(1)} %fusion.12), channel_id=1, source_target_pairs={{0,32},{16,48},{32,64},{48,80},{64,96},{80,112},{96,0},{112,16},{1... | collective-permute-start | bytes 2752520 | tf_op jit(solution)/shard_map/ppermute | solution.py:64
  148.2 21.9 %collective-permute-start.7 = (bf16[256,1792]{1,0:T(8,128)(2,1)}, bf16[256,1792]{1,0:T(8,128)(2,1)S(1)}, u32[]{:S(2)}, u32[]{:S(2)}) collective-permute-start(bf16[256,1792]{1,0:T(8,128)(2,1)} %fusion.10), channel_id=1, source_target_pairs={{0,96},{16,112},{32,0},{48,16},{64,32},{80,48},{96,64},{112,80},{1... | collective-permute-start | bytes 2752520 | tf_op jit(solution)/shard_map/ppermute | solution.py:64
  173.2 11.5 %collective-permute-start.8 = (bf16[256,896]{1,0:T(8,128)(2,1)S(1)}, bf16[256,896]{1,0:T(8,128)(2,1)S(1)}, u32[]{:S(2)}, u32[]{:S(2)}) collective-permute-start(bf16[256,896]{1,0:T(8,128)(2,1)S(1)} %get-tuple-element.5), channel_id=1, source_target_pairs={{0,32},{16,48},{32,64},{48,80},{64,96},{80,112},{96,0},{112,16},{1... | collective-permute-start | bytes 1376264 | tf_op jit(solution)/shard_map/ppermute | solution.py:83
  173.3 11.4 %collective-permute-start.11 = (bf16[256,896]{1,0:T(8,128)(2,1)S(1)}, bf16[256,896]{1,0:T(8,128)(2,1)S(1)}, u32[]{:S(2)}, u32[]{:S(2)}) collective-permute-start(bf16[256,896]{1,0:T(8,128)(2,1)S(1)} %get-tuple-element.6), channel_id=1, source_target_pairs={{0,96},{16,112},{32,0},{48,16},{64,32},{80,48},{96,64},{112,80},{1... | collective-permute-start | bytes 1376264 | tf_op jit(solution)/shard_map/ppermute | solution.py:83
  184.7 10.7 %collective-permute-start.9 = (bf16[256,896]{1,0:T(8,128)(2,1)S(1)}, bf16[256,896]{1,0:T(8,128)(2,1)S(1)}, u32[]{:S(2)}, u32[]{:S(2)}) collective-permute-start(bf16[256,896]{1,0:T(8,128)(2,1)S(1)} %collective-permute-done.8), channel_id=1, source_target_pairs={{0,32},{16,48},{32,64},{48,80},{64,96},{80,112},{96,0},{112,16},{1... | collective-permute-start | bytes 1376264 | tf_op jit(solution)/shard_map/ppermute | solution.py:83
  184.7 10.7 %collective-permute-start.12 = (bf16[256,896]{1,0:T(8,128)(2,1)S(1)}, bf16[256,896]{1,0:T(8,128)(2,1)S(1)}, u32[]{:S(2)}, u32[]{:S(2)}) collective-permute-start(bf16[256,896]{1,0:T(8,128)(2,1)S(1)} %collective-permute-done.11), channel_id=1, source_target_pairs={{0,96},{16,112},{32,0},{48,16},{64,32},{80,48},{96,64},{112,80},{1... | collective-permute-start | bytes 1376264 | tf_op jit(solution)/shard_map/ppermute | solution.py:83
  195.4 9.7 %collective-permute-start.10 = (bf16[256,896]{1,0:T(8,128)(2,1)S(1)}, bf16[256,896]{1,0:T(8,128)(2,1)S(1)}, u32[]{:S(2)}, u32[]{:S(2)}) collective-permute-start(bf16[256,896]{1,0:T(8,128)(2,1)S(1)} %collective-permute-done.9), channel_id=1, source_target_pairs={{0,32},{16,48},{32,64},{48,80},{64,96},{80,112},{96,0},{112,16},{1... | collective-permute-start | bytes 1376264 | tf_op jit(solution)/shard_map/ppermute | solution.py:83
  195.4 9.7 %collective-permute-start.13 = (bf16[256,896]{1,0:T(8,128)(2,1)S(1)}, bf16[256,896]{1,0:T(8,128)(2,1)S(1)}, u32[]{:S(2)}, u32[]{:S(2)}) collective-permute-start(bf16[256,896]{1,0:T(8,128)(2,1)S(1)} %collective-permute-done.12), channel_id=1, source_target_pairs={{0,96},{16,112},{32,0},{48,16},{64,32},{80,48},{96,64},{112,80},{1... | collective-permute-start | bytes 1376264 | tf_op jit(solution)/shard_map/ppermute | solution.py:83
  205.2 2.1 copy-start.10
  205.2 2.2 copy-start.5
  207.3 9.5 %collective-permute-start.14 = (bf16[1024,1792]{1,0:T(8,128)(2,1)}, bf16[1024,1792]{1,0:T(8,128)(2,1)}, u32[]{:S(2)}, u32[]{:S(2)}) collective-permute-start(bf16[1024,1792]{1,0:T(8,128)(2,1)} %bitcast.25), channel_id=1, source_target_pairs={{0,16},{16,0},{32,48},{48,32},{64,80},{80,64},{96,112},{112,96},{1... | collective-permute-start | bytes 11010056 | tf_op jit(solution)/shard_map/ppermute | solution.py:88
  208.3 2.0 copy-start.13
Sparse Core Ops, SparseCore 0:
  9.5 53.9 all-gather.1

commit v5 on v4

--- a/solution.py
+++ b/solution.py
@@ -7,6 +7,7 @@
 CHUNKS = 1
 COL_A2A = True
 COL_RING = False
+SUB_RINGS = 2
 
 
 def local_mask(keep_list, keep_count, offset, blocks):
@@ -58,13 +59,23 @@
                 + lax.dynamic_index_in_dim(got, index, 0, keepdims=False).astype(jnp.float32)
             )
 
-        index = (y - direction) % n_y
-        acc = own(index)
-        for step in range(n_y - 1):
-            received = lax.ppermute(acc.astype(jnp.bfloat16), "row", row_perm(n_row, direction))
-            index = (index - direction) % n_y
-            acc = received.astype(jnp.float32) + own(index)
-        results.append(acc)
+        pieces = []
+        for sub in range(SUB_RINGS):
+            rows_of = slice(sub * chunk // SUB_RINGS, (sub + 1) * chunk // SUB_RINGS)
+            index = (y - direction) % n_y
+            acc = own(index)[rows_of]
+            if sub > 0:
+                acc, lead = lax.optimization_barrier((acc, lead))
+            for step in range(n_y - 1):
+                received = lax.ppermute(
+                    acc.astype(jnp.bfloat16), "row", row_perm(n_row, direction)
+                )
+                if step == 0:
+                    lead = received
+                index = (index - direction) % n_y
+                acc = received.astype(jnp.float32) + own(index)[rows_of]
+            pieces.append(acc)
+        results.append(jnp.concatenate(pieces, axis=0))
     return results
 
 

time: 291 us -> 285 us (0.979)
  other arithmetic: 22.9 us -> 16.3 us
  starting transfers between devices: 21.6 us -> 26.5 us
    convert_element_type x6 -> x4, other arithmetic: 12.7 us -> 0.73 us  [row_reduce_scatter(): acc.astype(jnp.bfloat16)]
    add x0 -> x6, other arithmetic: none -> 7.9 us  [the longest x4 7.49 us: own(): lax.dynamic_index_in_dim(mine, index, 0, keepdims=False).astype(jnp.float32)]
    ppermute x6 -> x12, starting transfers between devices: 10.6 us -> 15.3 us  [row_reduce_scatter(): lax.ppermute(acc.astype(jnp.bfloat16), 'row', row_perm(n_row, direction))]
    ppermute x6 -> x12, waiting for transfers between devices: 52.6 us -> 50.7 us  [row_reduce_scatter(): lax.ppermute(acc.astype(jnp.bfloat16), 'row', row_perm(n_row, direction))]
    unnamed x30 -> x28, local copies, waits for them, and re-layouts: 15.3 us -> 13.5 us
  transfers between devices with their start and end apart: 16 -> 22, of which waited for: 10 -> 13; matrix products, arithmetic and copies ran while one was open for 18% -> 17% of each run, Pallas kernels for 0% -> 0%
where the time goes in v5:
time: 285 us; the launch traced here: 284 us
  waiting for transfers between devices  116 us (41%)
  blocking collectives  56.6 us (20%)
  matrix products  38.5 us (14%)
  starting transfers between devices  26.5 us (9%)
  local copies, waits for them, and re-layouts  16.5 us (6%)
  other arithmetic  16.3 us (6%)
  between operations  13.8 us (5%)
    all_to_all x1, blocking collectives, on_device(): terms = lax.all_to_all(terms, 'col', 0, 0, tiled=False)  56.6 us
    ppermute x12, waiting for transfers between devices, row_reduce_scatter(): lax.ppermute(acc.astype(jnp.bfloat16), 'row', row_perm(n_row, direction))  50.7 us
    all_gather x1, waiting for transfers between devices, on_device(): gathered = lax.all_gather(tokens, 'col', axis=0, tiled=True)  43.5 us
    ppermute x6, waiting for transfers between devices, row_all_gather(): held = lax.ppermute(held, 'row', row_perm(n_row, direction))  21.2 us
    ppermute x12, starting transfers between devices, row_reduce_scatter(): lax.ppermute(acc.astype(jnp.bfloat16), 'row', row_perm(n_row, direction))  15.3 us
    dot_general x2, matrix products, row_reduce_scatter(): jnp.dot(send, w, preferred_element_type=jnp.float32).astype(jnp.bfloat16)  14.3 us
    unnamed x28, local copies, waits for them, and re-layouts  13.5 us
    dot_general x2, matrix products, row_reduce_scatter(): jnp.dot(keep, w, preferred_element_type=jnp.float32).astype(jnp.bfloat16)  11.3 us
  transfers between devices with their start and end apart: 22, of which 13 were waited for; matrix products, arithmetic and copies ran while one was open for 17% of the time, Pallas kernels for 0%

profile of v5, /device:TPU:0, one launch (start us, length us, event | category | flops | bytes accessed | tf_op | source)
XLA Modules:
  0.0 284.3 jit_solution(7789716334389243071)
XLA Ops:
  6.5 0.7 all-gather.2.cloned.1.call-update
  7.3 5.9 %copy.13 = bf16[1024,1792]{0,1:T(8,128)(2,1)} copy(bf16[1024,1792]{1,0:T(8,128)(2,1)} %param.11) | data formatting | bytes 7340032 | tf_op args[1]
  13.2 6.0 %copy.14 = bf16[1024,1792]{0,1:T(8,128)(2,1)} copy(bf16[1024,1792]{1,0:T(8,128)(2,1)} %param.12) | data formatting | bytes 7340032 | tf_op args[2]
  19.3 0.3 fusion.40
  19.7 0.3 fusion.42
  20.0 43.5 %all-gather.2.cloned.1.call-done = bf16[2048,1024]{1,0:T(8,128)(2,1)} async-done(((bf16[128,1024]{1,0:T(8,128)(2,1)}), bf16[2048,1024]{1,0:T(8,128)(2,1)}) %all-gather.2.cloned.1.call-update) | async-done | bytes 4194320 | tf_op jit(solution)/shard_map/all_gather | solution.py:205
  63.5 0.5 broadcast_in_dim.90
  64.1 8.7 %convolution_convert_fusion.2 = bf16[1024,1792]{1,0:T(8,128)(2,1)} fusion(bf16[1024,1792]{0,1:T(8,128)(2,1)} %copy.13, pred[224,8,8,128]{3,2,1,0:T(8,128)(4,1)S(1)} %bitcast.141, bf16[2,1024,1024]{2,1,0:T(8,128)(2,1)} %bitcast.150, s32[]{:T(128)S(6)} %select_n.180), kind=kOutput, calls=%fused_computation.5 | convolution fusion | flops 3761766400 | bytes 11272196 | tf_op jit(solution)/shard_map/dot_general | solution.py:48
  72.8 0.5 broadcast_in_dim.93
  73.4 5.6 %convolution_convert_fusion = bf16[1024,1792]{1,0:T(8,128)(2,1)} fusion(bf16[1024,1792]{0,1:T(8,128)(2,1)S(1)} %copy-done, pred[224,8,8,128]{3,2,1,0:T(8,128)(4,1)S(1)} %bitcast.143, bf16[2,1024,1024]{2,1,0:T(8,128)(2,1)S(1)} %bitcast.152, s32[]{:T(128)S(6)} %select_n.180), kind=kOutput, calls=%fused_computation.3 | convolution fusion | flops 3761766400 | bytes 11272196 | tf_op jit(solution)/shard_map/dot_general | solution.py:48
  79.0 0.5 collective-permute-start.7
  79.5 6.8 %convolution_convert_fusion.3 = bf16[1024,1792]{1,0:T(8,128)(2,1)S(1)} fusion(bf16[1024,1792]{0,1:T(8,128)(2,1)} %copy.13, pred[224,8,8,128]{3,2,1,0:T(8,128)(4,1)S(1)} %bitcast.142, bf16[2,1024,1024]{2,1,0:T(8,128)(2,1)} %bitcast.151, s32[]{:T(128)S(6)} %select_n.175), kind=kOutput, calls=%fused_computation.6 | convolution fusion | flops 3761766400 | bytes 11272196 | tf_op jit(solution)/shard_map/dot_general | solution.py:52
  86.4 4.5 %convolution_convert_fusion.1 = bf16[1024,1792]{1,0:T(8,128)(2,1)S(1)} fusion(bf16[1024,1792]{0,1:T(8,128)(2,1)S(1)} %copy-done.1, pred[224,8,8,128]{3,2,1,0:T(8,128)(4,1)S(1)} %bitcast.144, bf16[2,1024,1024]{2,1,0:T(8,128)(2,1)S(1)} %bitcast.153, s32[]{:T(128)S(6)} %select_n.175), kind=kOutput, calls=%fused_computation.4 | convolution fusion | flops 3761766400 | bytes 11272196 | tf_op jit(solution)/shard_map/dot_general | solution.py:52
  90.9 1.4 convert_add_fusion.7
  92.3 1.6 collective-permute-start.1
  93.9 1.4 convert_add_fusion.3
  95.4 1.8 collective-permute-start.8
  97.2 8.9 %collective-permute-done.1 = bf16[128,1792]{1,0:T(8,128)(2,1)S(1)} collective-permute-done((bf16[128,1792]{1,0:T(8,128)(2,1)S(1)}, bf16[128,1792]{1,0:T(8,128)(2,1)S(1)}, u32[]{:S(2)}, u32[]{:S(2)}) %collective-permute-start.1) | collective-permute-done | bytes 458784 | tf_op jit(solution)/shard_map/ppermute | solution.py:70
  106.1 0.3 collective-permute-start.4
  106.3 2.3 convert_add_fusion.6
  108.7 2.3 convert_add_fusion.2
  111.1 3.0 %collective-permute-start.11 = (bf16[128,1792]{1,0:T(8,128)(2,1)S(1)}, bf16[128,1792]{1,0:T(8,128)(2,1)S(1)}, u32[]{:S(2)}, u32[]{:S(2)}) collective-permute-start(bf16[128,1792]{1,0:T(8,128)(2,1)S(1)} %get-tuple-element.8), channel_id=1, source_target_pairs={{0,96},{16,112},{32,0},{48,16},{64,32},{80,48},{96,64},{112,80},{1... | collective-permute-start | bytes 1376264 | tf_op jit(solution)/shard_map/ppermute | solution.py:70
  114.1 4.8 %collective-permute-done.4 = bf16[128,1792]{1,0:T(8,128)(2,1)S(1)} collective-permute-done((bf16[128,1792]{1,0:T(8,128)(2,1)S(1)}, bf16[128,1792]{1,0:T(8,128)(2,1)S(1)}, u32[]{:S(2)}, u32[]{:S(2)}) %collective-permute-start.4) | collective-permute-done | bytes 458784 | tf_op jit(solution)/shard_map/ppermute | solution.py:70
  118.9 0.2 fusion.34
  119.0 0.1 collective-permute-start.2
  119.1 0.5 collective-permute-start.5
  119.7 3.2 %collective-permute-done.11 = bf16[128,1792]{1,0:T(8,128)(2,1)S(1)} collective-permute-done((bf16[128,1792]{1,0:T(8,128)(2,1)S(1)}, bf16[128,1792]{1,0:T(8,128)(2,1)S(1)}, u32[]{:S(2)}, u32[]{:S(2)}) %collective-permute-start.11) | collective-permute-done | bytes 458784 | tf_op jit(solution)/shard_map/ppermute | solution.py:70
  122.9 0.2 fusion.24
  123.1 3.8 %collective-permute-start.12 = (bf16[128,1792]{1,0:T(8,128)(2,1)S(1)}, bf16[128,1792]{1,0:T(8,128)(2,1)S(1)}, u32[]{:S(2)}, u32[]{:S(2)}) collective-permute-start(bf16[128,1792]{1,0:T(8,128)(2,1)S(1)} %get-tuple-element.26), channel_id=1, source_target_pairs={{0,96},{16,112},{32,0},{48,16},{64,32},{80,48},{96,64},{112,80},{1... | collective-permute-start | bytes 1376264 | tf_op jit(solution)/shard_map/ppermute | solution.py:70
  126.8 0.1 collective-permute-start.9
  126.9 6.8 %collective-permute-done.2 = bf16[128,1792]{1,0:T(8,128)(2,1)S(1)} collective-permute-done((bf16[128,1792]{1,0:T(8,128)(2,1)S(1)}, bf16[128,1792]{1,0:T(8,128)(2,1)S(1)}, u32[]{:S(2)}, u32[]{:S(2)}) %collective-permute-start.2) | collective-permute-done | bytes 458784 | tf_op jit(solution)/shard_map/ppermute | solution.py:70
  133.7 7.2 %collective-permute-done.5 = bf16[128,1792]{1,0:T(8,128)(2,1)S(1)} collective-permute-done((bf16[128,1792]{1,0:T(8,128)(2,1)S(1)}, bf16[128,1792]{1,0:T(8,128)(2,1)S(1)}, u32[]{:S(2)}, u32[]{:S(2)}) %collective-permute-start.5) | collective-permute-done | bytes 458784 | tf_op jit(solution)/shard_map/ppermute | solution.py:70
  140.9 0.2 fusion.32
  141.1 0.1 collective-permute-start.3
  141.2 0.3 collective-permute-start.6
  141.5 3.2 %collective-permute-done.9 = bf16[128,1792]{1,0:T(8,128)(2,1)S(1)} collective-permute-done((bf16[128,1792]{1,0:T(8,128)(2,1)S(1)}, bf16[128,1792]{1,0:T(8,128)(2,1)S(1)}, u32[]{:S(2)}, u32[]{:S(2)}) %collective-permute-start.9) | collective-permute-done | bytes 458784 | tf_op jit(solution)/shard_map/ppermute | solution.py:70
  144.7 0.2 fusion.22
  144.9 3.8 %collective-permute-start.10 = (bf16[128,1792]{1,0:T(8,128)(2,1)S(1)}, bf16[128,1792]{1,0:T(8,128)(2,1)S(1)}, u32[]{:S(2)}, u32[]{:S(2)}) collective-permute-start(bf16[128,1792]{1,0:T(8,128)(2,1)S(1)} %get-tuple-element.23), channel_id=1, source_target_pairs={{0,96},{16,112},{32,0},{48,16},{64,32},{80,48},{96,64},{112,80},{1... | collective-permute-start | bytes 1376264 | tf_op jit(solution)/shard_map/ppermute | solution.py:70
  148.6 0.1 collective-permute-start.13
  148.7 7.1 %collective-permute-done.3 = bf16[128,1792]{1,0:T(8,128)(2,1)S(1)} collective-permute-done((bf16[128,1792]{1,0:T(8,128)(2,1)S(1)}, bf16[128,1792]{1,0:T(8,128)(2,1)S(1)}, u32[]{:S(2)}, u32[]{:S(2)}) %collective-permute-start.3) | collective-permute-done | bytes 458784 | tf_op jit(solution)/shard_map/ppermute | solution.py:70
  155.8 6.3 %collective-permute-done.6 = bf16[128,1792]{1,0:T(8,128)(2,1)S(1)} collective-permute-done((bf16[128,1792]{1,0:T(8,128)(2,1)S(1)}, bf16[128,1792]{1,0:T(8,128)(2,1)S(1)}, u32[]{:S(2)}, u32[]{:S(2)}) %collective-permute-start.6) | collective-permute-done | bytes 458784 | tf_op jit(solution)/shard_map/ppermute | solution.py:70
  162.1 0.2 fusion.30
  162.3 3.3 %collective-permute-done.13 = bf16[128,1792]{1,0:T(8,128)(2,1)S(1)} collective-permute-done((bf16[128,1792]{1,0:T(8,128)(2,1)S(1)}, bf16[128,1792]{1,0:T(8,128)(2,1)S(1)}, u32[]{:S(2)}, u32[]{:S(2)}) %collective-permute-start.13) | collective-permute-done | bytes 458784 | tf_op jit(solution)/shard_map/ppermute | solution.py:70
  165.6 0.2 fusion.20
  165.8 0.5 fusion.8
  166.3 0.1 fusion.53
  166.4 0.1 collective-permute-start.14
  166.4 3.8 %collective-permute-start.17 = (bf16[256,896]{1,0:T(8,128)(2,1)S(1)}, bf16[256,896]{1,0:T(8,128)(2,1)S(1)}, u32[]{:S(2)}, u32[]{:S(2)}) collective-permute-start(bf16[256,896]{1,0:T(8,128)(2,1)S(1)} %get-tuple-element.28), channel_id=1, source_target_pairs={{0,96},{16,112},{32,0},{48,16},{64,32},{80,48},{96,64},{112,80},{1... | collective-permute-start | bytes 1376264 | tf_op jit(solution)/shard_map/ppermute | solution.py:94
  170.2 0.1 broadcast.73.clone.1
  170.4 0.1 broadcast.73.clone
  170.6 7.0 %collective-permute-done.14 = bf16[256,896]{1,0:T(8,128)(2,1)S(1)} collective-permute-done((bf16[256,896]{1,0:T(8,128)(2,1)S(1)}, bf16[256,896]{1,0:T(8,128)(2,1)S(1)}, u32[]{:S(2)}, u32[]{:S(2)}) %collective-permute-start.14) | collective-permute-done | bytes 458784 | tf_op jit(solution)/shard_map/ppermute | solution.py:94
  177.6 3.2 %collective-permute-start.18 = (bf16[256,896]{1,0:T(8,128)(2,1)S(1)}, bf16[256,896]{1,0:T(8,128)(2,1)S(1)}, u32[]{:S(2)}, u32[]{:S(2)}) collective-permute-start(bf16[256,896]{1,0:T(8,128)(2,1)S(1)} %collective-permute-done.17), channel_id=1, source_target_pairs={{0,96},{16,112},{32,0},{48,16},{64,32},{80,48},{96,64},{112,80},{1... | collective-permute-start | bytes 1376264 | tf_op jit(solution)/shard_map/ppermute | solution.py:94
  180.9 7.9 %collective-permute-done.15 = bf16[256,896]{1,0:T(8,128)(2,1)S(1)} collective-permute-done((bf16[256,896]{1,0:T(8,128)(2,1)S(1)}, bf16[256,896]{1,0:T(8,128)(2,1)S(1)}, u32[]{:S(2)}, u32[]{:S(2)}) %collective-permute-start.15) | collective-permute-done | bytes 458784 | tf_op jit(solution)/shard_map/ppermute | solution.py:94
  188.9 3.5 %collective-permute-start.19 = (bf16[256,896]{1,0:T(8,128)(2,1)S(1)}, bf16[256,896]{1,0:T(8,128)(2,1)S(1)}, u32[]{:S(2)}, u32[]{:S(2)}) collective-permute-start(bf16[256,896]{1,0:T(8,128)(2,1)S(1)} %collective-permute-done.18), channel_id=1, source_target_pairs={{0,96},{16,112},{32,0},{48,16},{64,32},{80,48},{96,64},{112,80},{1... | collective-permute-start | bytes 1376264 | tf_op jit(solution)/shard_map/ppermute | solution.py:94
  192.5 6.3 %collective-permute-done.16 = bf16[256,896]{1,0:T(8,128)(2,1)S(1)} collective-permute-done((bf16[256,896]{1,0:T(8,128)(2,1)S(1)}, bf16[256,896]{1,0:T(8,128)(2,1)S(1)}, u32[]{:S(2)}, u32[]{:S(2)}) %collective-permute-start.16) | collective-permute-done | bytes 458784 | tf_op jit(solution)/shard_map/ppermute | solution.py:94
  199.0 2.0 pad_maximum_fusion
  201.1 0.3 fusion.38
  201.4 0.5 broadcast_in_dim.103
  202.0 0.5 broadcast_in_dim.89
  202.5 1.5 copy-done.12
  204.0 6.4 %bitcast_dynamic-update-slice_fusion.1 = bf16[2,1024,1024]{2,1,0:T(8,128)(2,1)S(1)} fusion(bf16[2,1024,1024]{2,1,0:T(8,128)(2,1)S(1)} %broadcast_in_dim.89, s32[]{:T(128)S(6)} %select_n.175, bf16[1024,1792]{1,0:T(8,128)(2,1)} %bitcast.33, bf16[1792,1024]{1,0:T(8,128)(2,1)S(1)} %copy-done.12, pred[224,8,8,128]{3,2,1,0:T(8,128)(4,1)S(1)} %bitcast.145), kind=kOutput, calls=%fused_computation.9 | convolution fusion | flops 3760979968 | bytes 11272196 | tf_op jit(solution)/shard_map/dot_general | solution.py:100
  210.5 6.5 %bitcast_dynamic-update-slice_fusion = bf16[2,1024,1024]{2,1,0:T(8,128)(2,1)S(1)} fusion(bf16[2,1024,1024]{2,1,0:T(8,128)(2,1)S(1)} %bitcast_dynamic-update-slice_fusion.1, s32[]{:T(128)S(6)} %select_n.180, bf16[1024,1792]{1,0:T(8,128)(2,1)} %collective-permute-done.20, bf16[1792,1024]{1,0:T(8,128)(2,1)S(1)} %copy-done.12, ...), kind=kOutput, calls=%fused_computation.8 | convolution fusion | flops 3760979968 | bytes 11272196 | tf_op jit(solution)/shard_map/dot_general | solution.py:101
  216.9 56.6 %all_to_all.5 = bf16[16,128,1024]{2,1,0:T(8,128)(2,1)} all-to-all(bf16[16,128,1024]{2,1,0:T(8,128)(2,1)S(1)} %bitcast.136), channel_id=1, replica_groups=mesh['row'=8,'col'=16] {'col'}, dimensions={0} | all-to-all | bytes 8388608 | tf_op jit(solution)/shard_map/all_to_all | solution.py:219
  273.6 3.9 %reduce_sum.12 = bf16[128,1024]{1,0:T(8,128)(2,1)} reduce(bf16[16,128,1024]{2,1,0:T(8,128)(2,1)} %all_to_all.5, bf16[]{:T(256)} %constant.226.clone.1), dimensions={0}, to_apply=%region_3.4 | reduce | flops 1966080 | bytes 4456450 | tf_op jit(solution)/shard_map/reduce_sum | solution.py:220
  (54 shorter events, 0.9 us)
Async XLA Ops:
  6.5 57.0 %all-gather.2.cloned.1.call-start = ((), (), s32[]{:S(2)}) async-start(), calls=%async_computation.1 | async-start | bytes 4456448 | tf_op jit(solution)/shard_map/all_gather | solution.py:205
  13.2 6.0 %copy-start.7 = (s32[14]{0:T(128)S(1)}, s32[14]{0:T(128)}, u32[]{:S(2)}) copy-start(s32[14]{0:T(128)} %param.15) | copy-start | bytes 172
  13.2 6.1 %copy-start.5 = (s32[14,48]{1,0:T(8,128)S(1)}, s32[14,48]{1,0:T(8,128)}, u32[]{:S(2)}) copy-start(s32[14,48]{1,0:T(8,128)} %param.16) | copy-start | bytes 8068
  13.2 6.1 %copy-start.6 = (s32[14,48]{1,0:T(8,128)S(1)}, s32[14,48]{1,0:T(8,128)}, u32[]{:S(2)}) copy-start(s32[14,48]{1,0:T(8,128)} %param.14) | copy-start | bytes 8068
  13.2 6.4 %copy-start.8 = (s32[14]{0:T(128)S(1)}, s32[14]{0:T(128)}, u32[]{:S(2)}) copy-start(s32[14]{0:T(128)} %param.17) | copy-start | bytes 172
  64.1 9.3 %copy-start = (bf16[1024,1792]{0,1:T(8,128)(2,1)S(1)}, bf16[1024,1792]{0,1:T(8,128)(2,1)}, u32[]{:S(2)}) copy-start(bf16[1024,1792]{0,1:T(8,128)(2,1)} %copy.14) | copy-start | bytes 11010052
  64.1 9.3 %copy-start.10 = (bf16[2048,1024]{1,0:T(8,128)(2,1)S(1)}, bf16[2048,1024]{1,0:T(8,128)(2,1)}, u32[]{:S(2)}) copy-start(bf16[2048,1024]{1,0:T(8,128)(2,1)} %all-gather.2.cloned.1.call-done) | copy-start | bytes 12582916
  72.8 18.1 %collective-permute-start = (bf16[1024,1792]{1,0:T(8,128)(2,1)}, bf16[1024,1792]{1,0:T(8,128)(2,1)}, u32[]{:S(2)}, u32[]{:S(2)}) collective-permute-start(bf16[1024,1792]{1,0:T(8,128)(2,1)} %convolution_convert_fusion.2), channel_id=1, source_target_pairs={{0,16},{16,0},{32,48},{48,32},{64,80},{80,64},{96,112},{112,96},{1... | collective-permute-start | bytes 11010056 | tf_op jit(solution)/shard_map/ppermute | solution.py:49
  73.3 5.6 %copy-start.2 = (pred[8,128,14,128]{1,0,3,2:T(8,128)(4,1)}, pred[8,128,14,128]{1,0,3,2:T(8,128)(4,1)S(1)}, u32[]{:S(2)}) copy-start(pred[8,128,14,128]{1,0,3,2:T(8,128)(4,1)S(1)} %broadcast_in_dim.93) | copy-start | bytes 5505028
  79.0 14.9 %collective-permute-start.7 = (bf16[1024,1792]{1,0:T(8,128)(2,1)}, bf16[1024,1792]{1,0:T(8,128)(2,1)}, u32[]{:S(2)}, u32[]{:S(2)}) collective-permute-start(bf16[1024,1792]{1,0:T(8,128)(2,1)} %convolution_convert_fusion), channel_id=1, source_target_pairs={{0,16},{16,0},{32,48},{48,32},{64,80},{80,64},{96,112},{112,96},{1... | collective-permute-start | bytes 11010056 | tf_op jit(solution)/shard_map/ppermute | solution.py:49
  79.5 6.8 %copy-start.1 = (bf16[1024,1792]{0,1:T(8,128)(2,1)S(1)}, bf16[1024,1792]{0,1:T(8,128)(2,1)}, u32[]{:S(2)}) copy-start(bf16[1024,1792]{0,1:T(8,128)(2,1)} %copy.14) | copy-start | bytes 11010052
  79.5 6.8 %copy-start.3 = (pred[8,128,14,128]{1,0,3,2:T(8,128)(4,1)S(1)}, pred[8,128,14,128]{1,0,3,2:T(8,128)(4,1)}, u32[]{:S(2)}) copy-start(pred[8,128,14,128]{1,0,3,2:T(8,128)(4,1)} %copy-done.2) | copy-start | bytes 5505028
  79.5 6.9 %copy-start.11 = (bf16[2048,1024]{1,0:T(8,128)(2,1)S(1)}, bf16[2048,1024]{1,0:T(8,128)(2,1)}, u32[]{:S(2)}) copy-start(bf16[2048,1024]{1,0:T(8,128)(2,1)} %all-gather.2.cloned.1.call-done) | copy-start | bytes 12582916
  92.3 13.7 %collective-permute-start.1 = (bf16[128,1792]{1,0:T(8,128)(2,1)S(1)}, bf16[128,1792]{1,0:T(8,128)(2,1)S(1)}, u32[]{:S(2)}, u32[]{:S(2)}) collective-permute-start(bf16[128,1792]{1,0:T(8,128)(2,1)S(1)} %get-tuple-element.29), channel_id=1, source_target_pairs={{0,32},{16,48},{32,64},{48,80},{64,96},{80,112},{96,0},{112,16},{1... | collective-permute-start | bytes 1376264 | tf_op jit(solution)/shard_map/ppermute | solution.py:70
  95.4 15.7 %collective-permute-start.8 = (bf16[128,1792]{1,0:T(8,128)(2,1)S(1)}, bf16[128,1792]{1,0:T(8,128)(2,1)S(1)}, u32[]{:S(2)}, u32[]{:S(2)}) collective-permute-start(bf16[128,1792]{1,0:T(8,128)(2,1)S(1)} %get-tuple-element.31), channel_id=1, source_target_pairs={{0,96},{16,112},{32,0},{48,16},{64,32},{80,48},{96,64},{112,80},{1... | collective-permute-start | bytes 1376264 | tf_op jit(solution)/shard_map/ppermute | solution.py:70
  106.1 12.8 %collective-permute-start.4 = (bf16[128,1792]{1,0:T(8,128)(2,1)S(1)}, bf16[128,1792]{1,0:T(8,128)(2,1)S(1)}, u32[]{:S(2)}, u32[]{:S(2)}) collective-permute-start(bf16[128,1792]{1,0:T(8,128)(2,1)S(1)} %get-tuple-element.7), channel_id=1, source_target_pairs={{0,32},{16,48},{32,64},{48,80},{64,96},{80,112},{96,0},{112,16},{1... | collective-permute-start | bytes 1376264 | tf_op jit(solution)/shard_map/ppermute | solution.py:70
  111.1 11.9 %collective-permute-start.11 = (bf16[128,1792]{1,0:T(8,128)(2,1)S(1)}, bf16[128,1792]{1,0:T(8,128)(2,1)S(1)}, u32[]{:S(2)}, u32[]{:S(2)}) collective-permute-start(bf16[128,1792]{1,0:T(8,128)(2,1)S(1)} %get-tuple-element.8), channel_id=1, source_target_pairs={{0,96},{16,112},{32,0},{48,16},{64,32},{80,48},{96,64},{112,80},{1... | collective-permute-start | bytes 1376264 | tf_op jit(solution)/shard_map/ppermute | solution.py:70
  119.0 14.7 %collective-permute-start.2 = (bf16[128,1792]{1,0:T(8,128)(2,1)S(1)}, bf16[128,1792]{1,0:T(8,128)(2,1)S(1)}, u32[]{:S(2)}, u32[]{:S(2)}) collective-permute-start(bf16[128,1792]{1,0:T(8,128)(2,1)S(1)} %get-tuple-element.19), channel_id=1, source_target_pairs={{0,32},{16,48},{32,64},{48,80},{64,96},{80,112},{96,0},{112,16},{1... | collective-permute-start | bytes 1376264 | tf_op jit(solution)/shard_map/ppermute | solution.py:70
  119.1 21.8 %collective-permute-start.5 = (bf16[128,1792]{1,0:T(8,128)(2,1)S(1)}, bf16[128,1792]{1,0:T(8,128)(2,1)S(1)}, u32[]{:S(2)}, u32[]{:S(2)}) collective-permute-start(bf16[128,1792]{1,0:T(8,128)(2,1)S(1)} %get-tuple-element.20), channel_id=1, source_target_pairs={{0,32},{16,48},{32,64},{48,80},{64,96},{80,112},{96,0},{112,16},{1... | collective-permute-start | bytes 1376264 | tf_op jit(solution)/shard_map/ppermute | solution.py:70
  123.1 18.4 %collective-permute-start.12 = (bf16[128,1792]{1,0:T(8,128)(2,1)S(1)}, bf16[128,1792]{1,0:T(8,128)(2,1)S(1)}, u32[]{:S(2)}, u32[]{:S(2)}) collective-permute-start(bf16[128,1792]{1,0:T(8,128)(2,1)S(1)} %get-tuple-element.26), channel_id=1, source_target_pairs={{0,96},{16,112},{32,0},{48,16},{64,32},{80,48},{96,64},{112,80},{1... | collective-permute-start | bytes 1376264 | tf_op jit(solution)/shard_map/ppermute | solution.py:70
  126.8 17.8 %collective-permute-start.9 = (bf16[128,1792]{1,0:T(8,128)(2,1)S(1)}, bf16[128,1792]{1,0:T(8,128)(2,1)S(1)}, u32[]{:S(2)}, u32[]{:S(2)}) collective-permute-start(bf16[128,1792]{1,0:T(8,128)(2,1)S(1)} %get-tuple-element.25), channel_id=1, source_target_pairs={{0,96},{16,112},{32,0},{48,16},{64,32},{80,48},{96,64},{112,80},{1... | collective-permute-start | bytes 1376264 | tf_op jit(solution)/shard_map/ppermute | solution.py:70
  141.1 14.7 %collective-permute-start.3 = (bf16[128,1792]{1,0:T(8,128)(2,1)S(1)}, bf16[128,1792]{1,0:T(8,128)(2,1)S(1)}, u32[]{:S(2)}, u32[]{:S(2)}) collective-permute-start(bf16[128,1792]{1,0:T(8,128)(2,1)S(1)} %get-tuple-element.17), channel_id=1, source_target_pairs={{0,32},{16,48},{32,64},{48,80},{64,96},{80,112},{96,0},{112,16},{1... | collective-permute-start | bytes 1376264 | tf_op jit(solution)/shard_map/ppermute | solution.py:70
  141.2 20.9 %collective-permute-start.6 = (bf16[128,1792]{1,0:T(8,128)(2,1)S(1)}, bf16[128,1792]{1,0:T(8,128)(2,1)S(1)}, u32[]{:S(2)}, u32[]{:S(2)}) collective-permute-start(bf16[128,1792]{1,0:T(8,128)(2,1)S(1)} %get-tuple-element.18), channel_id=1, source_target_pairs={{0,32},{16,48},{32,64},{48,80},{64,96},{80,112},{96,0},{112,16},{1... | collective-permute-start | bytes 1376264 | tf_op jit(solution)/shard_map/ppermute | solution.py:70
  144.9 17.4 %collective-permute-start.10 = (bf16[128,1792]{1,0:T(8,128)(2,1)S(1)}, bf16[128,1792]{1,0:T(8,128)(2,1)S(1)}, u32[]{:S(2)}, u32[]{:S(2)}) collective-permute-start(bf16[128,1792]{1,0:T(8,128)(2,1)S(1)} %get-tuple-element.23), channel_id=1, source_target_pairs={{0,96},{16,112},{32,0},{48,16},{64,32},{80,48},{96,64},{112,80},{1... | collective-permute-start | bytes 1376264 | tf_op jit(solution)/shard_map/ppermute | solution.py:70
  148.6 17.0 %collective-permute-start.13 = (bf16[128,1792]{1,0:T(8,128)(2,1)S(1)}, bf16[128,1792]{1,0:T(8,128)(2,1)S(1)}, u32[]{:S(2)}, u32[]{:S(2)}) collective-permute-start(bf16[128,1792]{1,0:T(8,128)(2,1)S(1)} %get-tuple-element.24), channel_id=1, source_target_pairs={{0,96},{16,112},{32,0},{48,16},{64,32},{80,48},{96,64},{112,80},{1... | collective-permute-start | bytes 1376264 | tf_op jit(solution)/shard_map/ppermute | solution.py:70
  166.4 11.2 %collective-permute-start.14 = (bf16[256,896]{1,0:T(8,128)(2,1)S(1)}, bf16[256,896]{1,0:T(8,128)(2,1)S(1)}, u32[]{:S(2)}, u32[]{:S(2)}) collective-permute-start(bf16[256,896]{1,0:T(8,128)(2,1)S(1)} %get-tuple-element.27), channel_id=1, source_target_pairs={{0,32},{16,48},{32,64},{48,80},{64,96},{80,112},{96,0},{112,16},{1... | collective-permute-start | bytes 1376264 | tf_op jit(solution)/shard_map/ppermute | solution.py:94
  166.4 11.1 %collective-permute-start.17 = (bf16[256,896]{1,0:T(8,128)(2,1)S(1)}, bf16[256,896]{1,0:T(8,128)(2,1)S(1)}, u32[]{:S(2)}, u32[]{:S(2)}) collective-permute-start(bf16[256,896]{1,0:T(8,128)(2,1)S(1)} %get-tuple-element.28), channel_id=1, source_target_pairs={{0,96},{16,112},{32,0},{48,16},{64,32},{80,48},{96,64},{112,80},{1... | collective-permute-start | bytes 1376264 | tf_op jit(solution)/shard_map/ppermute | solution.py:94
  177.6 11.3 %collective-permute-start.15 = (bf16[256,896]{1,0:T(8,128)(2,1)S(1)}, bf16[256,896]{1,0:T(8,128)(2,1)S(1)}, u32[]{:S(2)}, u32[]{:S(2)}) collective-permute-start(bf16[256,896]{1,0:T(8,128)(2,1)S(1)} %collective-permute-done.14), channel_id=1, source_target_pairs={{0,32},{16,48},{32,64},{48,80},{64,96},{80,112},{96,0},{112,16},{1... | collective-permute-start | bytes 1376264 | tf_op jit(solution)/shard_map/ppermute | solution.py:94
  177.6 11.3 %collective-permute-start.18 = (bf16[256,896]{1,0:T(8,128)(2,1)S(1)}, bf16[256,896]{1,0:T(8,128)(2,1)S(1)}, u32[]{:S(2)}, u32[]{:S(2)}) collective-permute-start(bf16[256,896]{1,0:T(8,128)(2,1)S(1)} %collective-permute-done.17), channel_id=1, source_target_pairs={{0,96},{16,112},{32,0},{48,16},{64,32},{80,48},{96,64},{112,80},{1... | collective-permute-start | bytes 1376264 | tf_op jit(solution)/shard_map/ppermute | solution.py:94
  188.9 10.0 %collective-permute-start.16 = (bf16[256,896]{1,0:T(8,128)(2,1)S(1)}, bf16[256,896]{1,0:T(8,128)(2,1)S(1)}, u32[]{:S(2)}, u32[]{:S(2)}) collective-permute-start(bf16[256,896]{1,0:T(8,128)(2,1)S(1)} %collective-permute-done.15), channel_id=1, source_target_pairs={{0,32},{16,48},{32,64},{48,80},{64,96},{80,112},{96,0},{112,16},{1... | collective-permute-start | bytes 1376264 | tf_op jit(solution)/shard_map/ppermute | solution.py:94
  188.9 10.0 %collective-permute-start.19 = (bf16[256,896]{1,0:T(8,128)(2,1)S(1)}, bf16[256,896]{1,0:T(8,128)(2,1)S(1)}, u32[]{:S(2)}, u32[]{:S(2)}) collective-permute-start(bf16[256,896]{1,0:T(8,128)(2,1)S(1)} %collective-permute-done.18), channel_id=1, source_target_pairs={{0,96},{16,112},{32,0},{48,16},{64,32},{80,48},{96,64},{112,80},{1... | collective-permute-start | bytes 1376264 | tf_op jit(solution)/shard_map/ppermute | solution.py:94
  199.0 2.1 copy-start.9
  199.0 2.1 copy-start.4
  201.0 9.5 %collective-permute-start.20 = (bf16[1024,1792]{1,0:T(8,128)(2,1)}, bf16[1024,1792]{1,0:T(8,128)(2,1)}, u32[]{:S(2)}, u32[]{:S(2)}) collective-permute-start(bf16[1024,1792]{1,0:T(8,128)(2,1)} %bitcast.33), channel_id=1, source_target_pairs={{0,16},{16,0},{32,48},{48,32},{64,80},{80,64},{96,112},{112,96},{1... | collective-permute-start | bytes 11010056 | tf_op jit(solution)/shard_map/ppermute | solution.py:99
  202.0 2.0 copy-start.12
Sparse Core Ops, SparseCore 0:
  9.5 54.0 all-gather.1

commit v6 on v5

--- a/solution.py
+++ b/solution.py
@@ -60,18 +60,19 @@
             )
 
         pieces = []
+        leads = []
         for sub in range(SUB_RINGS):
             rows_of = slice(sub * chunk // SUB_RINGS, (sub + 1) * chunk // SUB_RINGS)
             index = (y - direction) % n_y
             acc = own(index)[rows_of]
-            if sub > 0:
-                acc, lead = lax.optimization_barrier((acc, lead))
             for step in range(n_y - 1):
+                if sub > 0:
+                    acc, _ = lax.optimization_barrier((acc, leads[step]))
                 received = lax.ppermute(
                     acc.astype(jnp.bfloat16), "row", row_perm(n_row, direction)
                 )
-                if step == 0:
-                    lead = received
+                if sub == 0:
+                    leads.append(received)
                 index = (index - direction) % n_y
                 acc = received.astype(jnp.float32) + own(index)[rows_of]
             pieces.append(acc)

time: 285 us -> 281 us (0.986)
  waiting for transfers between devices: 116 us -> 110 us
    ppermute x12, waiting for transfers between devices: 50.7 us -> 44.4 us  [row_reduce_scatter(): lax.ppermute(acc.astype(jnp.bfloat16), 'row', row_perm(n_row, direction))]
  transfers between devices with their start and end apart: 22 -> 22, of which waited for: 13 -> 11; matrix products, arithmetic and copies ran while one was open for 17% -> 17% of each run, Pallas kernels for 0% -> 0%
where the time goes in v6:
time: 281 us; the launch traced here: 280 us
  waiting for transfers between devices  110 us (39%)
  blocking collectives  56.6 us (20%)
  matrix products  38.5 us (14%)
  starting transfers between devices  28.8 us (10%)
  local copies, waits for them, and re-layouts  16.5 us (6%)
  other arithmetic  16.2 us (6%)
  between operations  13.8 us (5%)
    all_to_all x1, blocking collectives, on_device(): terms = lax.all_to_all(terms, 'col', 0, 0, tiled=False)  56.6 us
    ppermute x12, waiting for transfers between devices, row_reduce_scatter(): lax.ppermute(acc.astype(jnp.bfloat16), 'row', row_perm(n_row, direction))  44.4 us
    all_gather x1, waiting for transfers between devices, on_device(): gathered = lax.all_gather(tokens, 'col', axis=0, tiled=True)  43.5 us
    ppermute x6, waiting for transfers between devices, row_all_gather(): held = lax.ppermute(held, 'row', row_perm(n_row, direction))  21.2 us
    ppermute x12, starting transfers between devices, row_reduce_scatter(): lax.ppermute(acc.astype(jnp.bfloat16), 'row', row_perm(n_row, direction))  17.9 us
    dot_general x2, matrix products, row_reduce_scatter(): jnp.dot(send, w, preferred_element_type=jnp.float32).astype(jnp.bfloat16)  14.3 us
    unnamed x28, local copies, waits for them, and re-layouts  13.5 us
    dot_general x2, matrix products, row_reduce_scatter(): jnp.dot(keep, w, preferred_element_type=jnp.float32).astype(jnp.bfloat16)  11.3 us
  transfers between devices with their start and end apart: 22, of which 11 were waited for; matrix products, arithmetic and copies ran while one was open for 17% of the time, Pallas kernels for 0%

profile of v6, /device:TPU:0, one launch (start us, length us, event | category | flops | bytes accessed | tf_op | source)
XLA Modules:
  0.0 280.3 jit_solution(6714322345631379391)
XLA Ops:
  6.5 0.7 all-gather.2.cloned.1.call-update
  7.3 5.9 %copy.13 = bf16[1024,1792]{0,1:T(8,128)(2,1)} copy(bf16[1024,1792]{1,0:T(8,128)(2,1)} %param.11) | data formatting | bytes 7340032 | tf_op args[1]
  13.2 6.0 %copy.14 = bf16[1024,1792]{0,1:T(8,128)(2,1)} copy(bf16[1024,1792]{1,0:T(8,128)(2,1)} %param.12) | data formatting | bytes 7340032 | tf_op args[2]
  19.3 0.3 fusion.36
  19.7 0.3 fusion.38
  20.1 43.5 %all-gather.2.cloned.1.call-done = bf16[2048,1024]{1,0:T(8,128)(2,1)} async-done(((bf16[128,1024]{1,0:T(8,128)(2,1)}), bf16[2048,1024]{1,0:T(8,128)(2,1)}) %all-gather.2.cloned.1.call-update) | async-done | bytes 4194320 | tf_op jit(solution)/shard_map/all_gather | solution.py:206
  63.6 0.5 broadcast_in_dim.90
  64.1 8.7 %convolution_convert_fusion.2 = bf16[1024,1792]{1,0:T(8,128)(2,1)} fusion(bf16[1024,1792]{0,1:T(8,128)(2,1)} %copy.13, pred[224,8,8,128]{3,2,1,0:T(8,128)(4,1)S(1)} %bitcast.133, bf16[2,1024,1024]{2,1,0:T(8,128)(2,1)} %bitcast.142, s32[]{:T(128)S(6)} %select_n.180), kind=kOutput, calls=%fused_computation.5 | convolution fusion | flops 3761766400 | bytes 11272196 | tf_op jit(solution)/shard_map/dot_general | solution.py:48
  72.8 0.5 broadcast_in_dim.93
  73.4 5.6 %convolution_convert_fusion = bf16[1024,1792]{1,0:T(8,128)(2,1)} fusion(bf16[1024,1792]{0,1:T(8,128)(2,1)S(1)} %copy-done, pred[224,8,8,128]{3,2,1,0:T(8,128)(4,1)S(1)} %bitcast.135, bf16[2,1024,1024]{2,1,0:T(8,128)(2,1)S(1)} %bitcast.144, s32[]{:T(128)S(6)} %select_n.180), kind=kOutput, calls=%fused_computation.3 | convolution fusion | flops 3761766400 | bytes 11272196 | tf_op jit(solution)/shard_map/dot_general | solution.py:48
  79.0 0.5 collective-permute-start.7
  79.5 6.8 %convolution_convert_fusion.3 = bf16[1024,1792]{1,0:T(8,128)(2,1)S(1)} fusion(bf16[1024,1792]{0,1:T(8,128)(2,1)} %copy.13, pred[224,8,8,128]{3,2,1,0:T(8,128)(4,1)S(1)} %bitcast.134, bf16[2,1024,1024]{2,1,0:T(8,128)(2,1)} %bitcast.143, s32[]{:T(128)S(6)} %select_n.175), kind=kOutput, calls=%fused_computation.6 | convolution fusion | flops 3761766400 | bytes 11272196 | tf_op jit(solution)/shard_map/dot_general | solution.py:52
  86.4 4.5 %convolution_convert_fusion.1 = bf16[1024,1792]{1,0:T(8,128)(2,1)S(1)} fusion(bf16[1024,1792]{0,1:T(8,128)(2,1)S(1)} %copy-done.1, pred[224,8,8,128]{3,2,1,0:T(8,128)(4,1)S(1)} %bitcast.136, bf16[2,1024,1024]{2,1,0:T(8,128)(2,1)S(1)} %bitcast.145, s32[]{:T(128)S(6)} %select_n.175), kind=kOutput, calls=%fused_computation.4 | convolution fusion | flops 3761766400 | bytes 11272196 | tf_op jit(solution)/shard_map/dot_general | solution.py:52
  90.9 1.4 convert_add_fusion.7
  92.4 1.6 collective-permute-start.1
  93.9 1.4 convert_add_fusion.3
  95.4 1.8 collective-permute-start.8
  97.2 2.3 convert_add_fusion.6
  99.6 2.3 convert_add_fusion.2
  101.9 4.2 %collective-permute-done.1 = bf16[128,1792]{1,0:T(8,128)(2,1)S(1)} collective-permute-done((bf16[128,1792]{1,0:T(8,128)(2,1)S(1)}, bf16[128,1792]{1,0:T(8,128)(2,1)S(1)}, u32[]{:S(2)}, u32[]{:S(2)}) %collective-permute-start.1) | collective-permute-done | bytes 458784 | tf_op jit(solution)/shard_map/ppermute | solution.py:71
  106.1 0.3 collective-permute-start.4
  106.4 0.1 fusion.30
  106.4 1.5 collective-permute-start.2
  108.0 2.6 collective-permute-start.11
  110.6 0.1 fusion.22
  110.7 1.0 collective-permute-start.9
  111.7 9.0 %collective-permute-done.4 = bf16[128,1792]{1,0:T(8,128)(2,1)S(1)} collective-permute-done((bf16[128,1792]{1,0:T(8,128)(2,1)S(1)}, bf16[128,1792]{1,0:T(8,128)(2,1)S(1)}, u32[]{:S(2)}, u32[]{:S(2)}) %collective-permute-start.4) | collective-permute-done | bytes 458784 | tf_op jit(solution)/shard_map/ppermute | solution.py:71
  120.7 0.1 fusion.25
  120.8 7.9 %collective-permute-done.2 = bf16[128,1792]{1,0:T(8,128)(2,1)S(1)} collective-permute-done((bf16[128,1792]{1,0:T(8,128)(2,1)S(1)}, bf16[128,1792]{1,0:T(8,128)(2,1)S(1)}, u32[]{:S(2)}, u32[]{:S(2)}) %collective-permute-start.2) | collective-permute-done | bytes 458784 | tf_op jit(solution)/shard_map/ppermute | solution.py:71
  128.7 0.1 fusion.28
  128.8 0.6 collective-permute-start.3
  129.4 0.1 fusion.17
  129.5 3.4 %collective-permute-start.12 = (bf16[128,1792]{1,0:T(8,128)(2,1)S(1)}, bf16[128,1792]{1,0:T(8,128)(2,1)S(1)}, u32[]{:S(2)}, u32[]{:S(2)}) collective-permute-start(bf16[128,1792]{1,0:T(8,128)(2,1)S(1)} %fusion.17), channel_id=1, source_target_pairs={{0,96},{16,112},{32,0},{48,16},{64,32},{80,48},{96,64},{112,80},{1... | collective-permute-start | bytes 1376264 | tf_op jit(solution)/shard_map/ppermute | solution.py:71
  132.9 0.1 fusion.20
  133.0 1.4 collective-permute-start.10
  134.5 8.8 %collective-permute-done.5 = bf16[128,1792]{1,0:T(8,128)(2,1)S(1)} collective-permute-done((bf16[128,1792]{1,0:T(8,128)(2,1)S(1)}, bf16[128,1792]{1,0:T(8,128)(2,1)S(1)}, u32[]{:S(2)}, u32[]{:S(2)}) %collective-permute-start.5) | collective-permute-done | bytes 458784 | tf_op jit(solution)/shard_map/ppermute | solution.py:71
  143.3 0.1 fusion.24
  143.4 7.1 %collective-permute-done.3 = bf16[128,1792]{1,0:T(8,128)(2,1)S(1)} collective-permute-done((bf16[128,1792]{1,0:T(8,128)(2,1)S(1)}, bf16[128,1792]{1,0:T(8,128)(2,1)S(1)}, u32[]{:S(2)}, u32[]{:S(2)}) %collective-permute-start.3) | collective-permute-done | bytes 458784 | tf_op jit(solution)/shard_map/ppermute | solution.py:71
  150.5 0.1 fusion.16
  150.6 0.1 collective-permute-done.10
  150.8 3.7 %collective-permute-start.13 = (bf16[128,1792]{1,0:T(8,128)(2,1)S(1)}, bf16[128,1792]{1,0:T(8,128)(2,1)S(1)}, u32[]{:S(2)}, u32[]{:S(2)}) collective-permute-start(bf16[128,1792]{1,0:T(8,128)(2,1)S(1)} %fusion.16), channel_id=1, source_target_pairs={{0,96},{16,112},{32,0},{48,16},{64,32},{80,48},{96,64},{112,80},{1... | collective-permute-start | bytes 1376264 | tf_op jit(solution)/shard_map/ppermute | solution.py:71
  154.4 7.1 %collective-permute-done.6 = bf16[128,1792]{1,0:T(8,128)(2,1)S(1)} collective-permute-done((bf16[128,1792]{1,0:T(8,128)(2,1)S(1)}, bf16[128,1792]{1,0:T(8,128)(2,1)S(1)}, u32[]{:S(2)}, u32[]{:S(2)}) %collective-permute-start.6) | collective-permute-done | bytes 458784 | tf_op jit(solution)/shard_map/ppermute | solution.py:71
  161.6 0.2 fusion.26
  161.8 0.2 fusion.18
  162.0 0.5 fusion.8
  162.5 0.1 fusion.49
  162.6 0.1 collective-permute-start.14
  162.7 3.5 %collective-permute-start.17 = (bf16[256,896]{1,0:T(8,128)(2,1)S(1)}, bf16[256,896]{1,0:T(8,128)(2,1)S(1)}, u32[]{:S(2)}, u32[]{:S(2)}) collective-permute-start(bf16[256,896]{1,0:T(8,128)(2,1)S(1)} %get-tuple-element.28), channel_id=1, source_target_pairs={{0,96},{16,112},{32,0},{48,16},{64,32},{80,48},{96,64},{112,80},{1... | collective-permute-start | bytes 1376264 | tf_op jit(solution)/shard_map/ppermute | solution.py:95
  166.2 0.1 broadcast.73.clone.1
  166.4 0.1 broadcast.73.clone
  166.6 7.0 %collective-permute-done.14 = bf16[256,896]{1,0:T(8,128)(2,1)S(1)} collective-permute-done((bf16[256,896]{1,0:T(8,128)(2,1)S(1)}, bf16[256,896]{1,0:T(8,128)(2,1)S(1)}, u32[]{:S(2)}, u32[]{:S(2)}) %collective-permute-start.14) | collective-permute-done | bytes 458784 | tf_op jit(solution)/shard_map/ppermute | solution.py:95
  173.6 3.2 %collective-permute-start.18 = (bf16[256,896]{1,0:T(8,128)(2,1)S(1)}, bf16[256,896]{1,0:T(8,128)(2,1)S(1)}, u32[]{:S(2)}, u32[]{:S(2)}) collective-permute-start(bf16[256,896]{1,0:T(8,128)(2,1)S(1)} %collective-permute-done.17), channel_id=1, source_target_pairs={{0,96},{16,112},{32,0},{48,16},{64,32},{80,48},{96,64},{112,80},{1... | collective-permute-start | bytes 1376264 | tf_op jit(solution)/shard_map/ppermute | solution.py:95
  176.9 7.9 %collective-permute-done.15 = bf16[256,896]{1,0:T(8,128)(2,1)S(1)} collective-permute-done((bf16[256,896]{1,0:T(8,128)(2,1)S(1)}, bf16[256,896]{1,0:T(8,128)(2,1)S(1)}, u32[]{:S(2)}, u32[]{:S(2)}) %collective-permute-start.15) | collective-permute-done | bytes 458784 | tf_op jit(solution)/shard_map/ppermute | solution.py:95
  184.9 3.5 %collective-permute-start.19 = (bf16[256,896]{1,0:T(8,128)(2,1)S(1)}, bf16[256,896]{1,0:T(8,128)(2,1)S(1)}, u32[]{:S(2)}, u32[]{:S(2)}) collective-permute-start(bf16[256,896]{1,0:T(8,128)(2,1)S(1)} %collective-permute-done.18), channel_id=1, source_target_pairs={{0,96},{16,112},{32,0},{48,16},{64,32},{80,48},{96,64},{112,80},{1... | collective-permute-start | bytes 1376264 | tf_op jit(solution)/shard_map/ppermute | solution.py:95
  188.5 6.3 %collective-permute-done.16 = bf16[256,896]{1,0:T(8,128)(2,1)S(1)} collective-permute-done((bf16[256,896]{1,0:T(8,128)(2,1)S(1)}, bf16[256,896]{1,0:T(8,128)(2,1)S(1)}, u32[]{:S(2)}, u32[]{:S(2)}) %collective-permute-start.16) | collective-permute-done | bytes 458784 | tf_op jit(solution)/shard_map/ppermute | solution.py:95
  195.0 2.0 pad_maximum_fusion
  197.1 0.3 fusion.34
  197.4 0.5 broadcast_in_dim.103
  198.0 0.5 broadcast_in_dim.89
  198.5 1.5 copy-done.12
  200.0 6.4 %bitcast_dynamic-update-slice_fusion.1 = bf16[2,1024,1024]{2,1,0:T(8,128)(2,1)S(1)} fusion(bf16[2,1024,1024]{2,1,0:T(8,128)(2,1)S(1)} %broadcast_in_dim.89, s32[]{:T(128)S(6)} %select_n.175, bf16[1024,1792]{1,0:T(8,128)(2,1)} %bitcast.33, bf16[1792,1024]{1,0:T(8,128)(2,1)S(1)} %copy-done.12, pred[224,8,8,128]{3,2,1,0:T(8,128)(4,1)S(1)} %bitcast.137), kind=kOutput, calls=%fused_computation.9 | convolution fusion | flops 3760979968 | bytes 11272196 | tf_op jit(solution)/shard_map/dot_general | solution.py:101
  206.5 6.5 %bitcast_dynamic-update-slice_fusion = bf16[2,1024,1024]{2,1,0:T(8,128)(2,1)S(1)} fusion(bf16[2,1024,1024]{2,1,0:T(8,128)(2,1)S(1)} %bitcast_dynamic-update-slice_fusion.1, s32[]{:T(128)S(6)} %select_n.180, bf16[1024,1792]{1,0:T(8,128)(2,1)} %collective-permute-done.20, bf16[1792,1024]{1,0:T(8,128)(2,1)S(1)} %copy-done.12, ...), kind=kOutput, calls=%fused_computation.8 | convolution fusion | flops 3760979968 | bytes 11272196 | tf_op jit(solution)/shard_map/dot_general | solution.py:102
  213.0 56.6 %all_to_all.5 = bf16[16,128,1024]{2,1,0:T(8,128)(2,1)} all-to-all(bf16[16,128,1024]{2,1,0:T(8,128)(2,1)S(1)} %bitcast.128), channel_id=1, replica_groups=mesh['row'=8,'col'=16] {'col'}, dimensions={0} | all-to-all | bytes 8388608 | tf_op jit(solution)/shard_map/all_to_all | solution.py:220
  269.6 3.9 %reduce_sum.12 = bf16[128,1024]{1,0:T(8,128)(2,1)} reduce(bf16[16,128,1024]{2,1,0:T(8,128)(2,1)} %all_to_all.5, bf16[]{:T(256)} %constant.226.clone.1), dimensions={0}, to_apply=%region_3.4 | reduce | flops 1966080 | bytes 4456450 | tf_op jit(solution)/shard_map/reduce_sum | solution.py:221
  (58 shorter events, 0.9 us)
Async XLA Ops:
  6.5 57.0 %all-gather.2.cloned.1.call-start = ((), (), s32[]{:S(2)}) async-start(), calls=%async_computation.1 | async-start | bytes 4456448 | tf_op jit(solution)/shard_map/all_gather | solution.py:206
  13.2 6.0 %copy-start.7 = (s32[14]{0:T(128)S(1)}, s32[14]{0:T(128)}, u32[]{:S(2)}) copy-start(s32[14]{0:T(128)} %param.15) | copy-start | bytes 172
  13.2 6.1 %copy-start.5 = (s32[14,48]{1,0:T(8,128)S(1)}, s32[14,48]{1,0:T(8,128)}, u32[]{:S(2)}) copy-start(s32[14,48]{1,0:T(8,128)} %param.16) | copy-start | bytes 8068
  13.2 6.1 %copy-start.6 = (s32[14,48]{1,0:T(8,128)S(1)}, s32[14,48]{1,0:T(8,128)}, u32[]{:S(2)}) copy-start(s32[14,48]{1,0:T(8,128)} %param.14) | copy-start | bytes 8068
  13.2 6.4 %copy-start.8 = (s32[14]{0:T(128)S(1)}, s32[14]{0:T(128)}, u32[]{:S(2)}) copy-start(s32[14]{0:T(128)} %param.17) | copy-start | bytes 172
  64.1 9.3 %copy-start = (bf16[1024,1792]{0,1:T(8,128)(2,1)S(1)}, bf16[1024,1792]{0,1:T(8,128)(2,1)}, u32[]{:S(2)}) copy-start(bf16[1024,1792]{0,1:T(8,128)(2,1)} %copy.14) | copy-start | bytes 11010052
  64.1 9.3 %copy-start.10 = (bf16[2048,1024]{1,0:T(8,128)(2,1)S(1)}, bf16[2048,1024]{1,0:T(8,128)(2,1)}, u32[]{:S(2)}) copy-start(bf16[2048,1024]{1,0:T(8,128)(2,1)} %all-gather.2.cloned.1.call-done) | copy-start | bytes 12582916
  72.8 18.1 %collective-permute-start = (bf16[1024,1792]{1,0:T(8,128)(2,1)}, bf16[1024,1792]{1,0:T(8,128)(2,1)}, u32[]{:S(2)}, u32[]{:S(2)}) collective-permute-start(bf16[1024,1792]{1,0:T(8,128)(2,1)} %convolution_convert_fusion.2), channel_id=1, source_target_pairs={{0,16},{16,0},{32,48},{48,32},{64,80},{80,64},{96,112},{112,96},{1... | collective-permute-start | bytes 11010056 | tf_op jit(solution)/shard_map/ppermute | solution.py:49
  73.4 5.6 %copy-start.2 = (pred[8,128,14,128]{1,0,3,2:T(8,128)(4,1)}, pred[8,128,14,128]{1,0,3,2:T(8,128)(4,1)S(1)}, u32[]{:S(2)}) copy-start(pred[8,128,14,128]{1,0,3,2:T(8,128)(4,1)S(1)} %broadcast_in_dim.93) | copy-start | bytes 5505028
  79.0 14.9 %collective-permute-start.7 = (bf16[1024,1792]{1,0:T(8,128)(2,1)}, bf16[1024,1792]{1,0:T(8,128)(2,1)}, u32[]{:S(2)}, u32[]{:S(2)}) collective-permute-start(bf16[1024,1792]{1,0:T(8,128)(2,1)} %convolution_convert_fusion), channel_id=1, source_target_pairs={{0,16},{16,0},{32,48},{48,32},{64,80},{80,64},{96,112},{112,96},{1... | collective-permute-start | bytes 11010056 | tf_op jit(solution)/shard_map/ppermute | solution.py:49
  79.5 6.8 %copy-start.1 = (bf16[1024,1792]{0,1:T(8,128)(2,1)S(1)}, bf16[1024,1792]{0,1:T(8,128)(2,1)}, u32[]{:S(2)}) copy-start(bf16[1024,1792]{0,1:T(8,128)(2,1)} %copy.14) | copy-start | bytes 11010052
  79.5 6.8 %copy-start.3 = (pred[8,128,14,128]{1,0,3,2:T(8,128)(4,1)S(1)}, pred[8,128,14,128]{1,0,3,2:T(8,128)(4,1)}, u32[]{:S(2)}) copy-start(pred[8,128,14,128]{1,0,3,2:T(8,128)(4,1)} %copy-done.2) | copy-start | bytes 5505028
  79.5 6.9 %copy-start.11 = (bf16[2048,1024]{1,0:T(8,128)(2,1)S(1)}, bf16[2048,1024]{1,0:T(8,128)(2,1)}, u32[]{:S(2)}) copy-start(bf16[2048,1024]{1,0:T(8,128)(2,1)} %all-gather.2.cloned.1.call-done) | copy-start | bytes 12582916
  92.4 13.7 %collective-permute-start.1 = (bf16[128,1792]{1,0:T(8,128)(2,1)S(1)}, bf16[128,1792]{1,0:T(8,128)(2,1)S(1)}, u32[]{:S(2)}, u32[]{:S(2)}) collective-permute-start(bf16[128,1792]{1,0:T(8,128)(2,1)S(1)} %get-tuple-element.29), channel_id=1, source_target_pairs={{0,32},{16,48},{32,64},{48,80},{64,96},{80,112},{96,0},{112,16},{1... | collective-permute-start | bytes 1376264 | tf_op jit(solution)/shard_map/ppermute | solution.py:71
  95.4 12.6 %collective-permute-start.8 = (bf16[128,1792]{1,0:T(8,128)(2,1)S(1)}, bf16[128,1792]{1,0:T(8,128)(2,1)S(1)}, u32[]{:S(2)}, u32[]{:S(2)}) collective-permute-start(bf16[128,1792]{1,0:T(8,128)(2,1)S(1)} %get-tuple-element.31), channel_id=1, source_target_pairs={{0,96},{16,112},{32,0},{48,16},{64,32},{80,48},{96,64},{112,80},{1... | collective-permute-start | bytes 1376264 | tf_op jit(solution)/shard_map/ppermute | solution.py:71
  106.1 14.6 %collective-permute-start.4 = (bf16[128,1792]{1,0:T(8,128)(2,1)S(1)}, bf16[128,1792]{1,0:T(8,128)(2,1)S(1)}, u32[]{:S(2)}, u32[]{:S(2)}) collective-permute-start(bf16[128,1792]{1,0:T(8,128)(2,1)S(1)} %get-tuple-element.11), channel_id=1, source_target_pairs={{0,32},{16,48},{32,64},{48,80},{64,96},{80,112},{96,0},{112,16},{1... | collective-permute-start | bytes 1376264 | tf_op jit(solution)/shard_map/ppermute | solution.py:71
  106.4 22.3 %collective-permute-start.2 = (bf16[128,1792]{1,0:T(8,128)(2,1)S(1)}, bf16[128,1792]{1,0:T(8,128)(2,1)S(1)}, u32[]{:S(2)}, u32[]{:S(2)}) collective-permute-start(bf16[128,1792]{1,0:T(8,128)(2,1)S(1)} %fusion.30), channel_id=1, source_target_pairs={{0,32},{16,48},{32,64},{48,80},{64,96},{80,112},{96,0},{112,16},{1... | collective-permute-start | bytes 1376264 | tf_op jit(solution)/shard_map/ppermute | solution.py:71
  108.0 21.4 %collective-permute-start.11 = (bf16[128,1792]{1,0:T(8,128)(2,1)S(1)}, bf16[128,1792]{1,0:T(8,128)(2,1)S(1)}, u32[]{:S(2)}, u32[]{:S(2)}) collective-permute-start(bf16[128,1792]{1,0:T(8,128)(2,1)S(1)} %get-tuple-element.14), channel_id=1, source_target_pairs={{0,96},{16,112},{32,0},{48,16},{64,32},{80,48},{96,64},{112,80},{1... | collective-permute-start | bytes 1376264 | tf_op jit(solution)/shard_map/ppermute | solution.py:71
  110.7 18.8 %collective-permute-start.9 = (bf16[128,1792]{1,0:T(8,128)(2,1)S(1)}, bf16[128,1792]{1,0:T(8,128)(2,1)S(1)}, u32[]{:S(2)}, u32[]{:S(2)}) collective-permute-start(bf16[128,1792]{1,0:T(8,128)(2,1)S(1)} %fusion.22), channel_id=1, source_target_pairs={{0,96},{16,112},{32,0},{48,16},{64,32},{80,48},{96,64},{112,80},{1... | collective-permute-start | bytes 1376264 | tf_op jit(solution)/shard_map/ppermute | solution.py:71
  128.7 14.6 %collective-permute-start.5 = (bf16[128,1792]{1,0:T(8,128)(2,1)S(1)}, bf16[128,1792]{1,0:T(8,128)(2,1)S(1)}, u32[]{:S(2)}, u32[]{:S(2)}) collective-permute-start(bf16[128,1792]{1,0:T(8,128)(2,1)S(1)} %fusion.25), channel_id=1, source_target_pairs={{0,32},{16,48},{32,64},{48,80},{64,96},{80,112},{96,0},{112,16},{1... | collective-permute-start | bytes 1376264 | tf_op jit(solution)/shard_map/ppermute | solution.py:71
  128.8 21.7 %collective-permute-start.3 = (bf16[128,1792]{1,0:T(8,128)(2,1)S(1)}, bf16[128,1792]{1,0:T(8,128)(2,1)S(1)}, u32[]{:S(2)}, u32[]{:S(2)}) collective-permute-start(bf16[128,1792]{1,0:T(8,128)(2,1)S(1)} %fusion.28), channel_id=1, source_target_pairs={{0,32},{16,48},{32,64},{48,80},{64,96},{80,112},{96,0},{112,16},{1... | collective-permute-start | bytes 1376264 | tf_op jit(solution)/shard_map/ppermute | solution.py:71
  129.5 21.0 %collective-permute-start.12 = (bf16[128,1792]{1,0:T(8,128)(2,1)S(1)}, bf16[128,1792]{1,0:T(8,128)(2,1)S(1)}, u32[]{:S(2)}, u32[]{:S(2)}) collective-permute-start(bf16[128,1792]{1,0:T(8,128)(2,1)S(1)} %fusion.17), channel_id=1, source_target_pairs={{0,96},{16,112},{32,0},{48,16},{64,32},{80,48},{96,64},{112,80},{1... | collective-permute-start | bytes 1376264 | tf_op jit(solution)/shard_map/ppermute | solution.py:71
  133.0 17.7 %collective-permute-start.10 = (bf16[128,1792]{1,0:T(8,128)(2,1)S(1)}, bf16[128,1792]{1,0:T(8,128)(2,1)S(1)}, u32[]{:S(2)}, u32[]{:S(2)}) collective-permute-start(bf16[128,1792]{1,0:T(8,128)(2,1)S(1)} %fusion.20), channel_id=1, source_target_pairs={{0,96},{16,112},{32,0},{48,16},{64,32},{80,48},{96,64},{112,80},{1... | collective-permute-start | bytes 1376264 | tf_op jit(solution)/shard_map/ppermute | solution.py:71
  150.5 11.1 %collective-permute-start.6 = (bf16[128,1792]{1,0:T(8,128)(2,1)S(1)}, bf16[128,1792]{1,0:T(8,128)(2,1)S(1)}, u32[]{:S(2)}, u32[]{:S(2)}) collective-permute-start(bf16[128,1792]{1,0:T(8,128)(2,1)S(1)} %fusion.24), channel_id=1, source_target_pairs={{0,32},{16,48},{32,64},{48,80},{64,96},{80,112},{96,0},{112,16},{1... | collective-permute-start | bytes 1376264 | tf_op jit(solution)/shard_map/ppermute | solution.py:71
  150.8 11.1 %collective-permute-start.13 = (bf16[128,1792]{1,0:T(8,128)(2,1)S(1)}, bf16[128,1792]{1,0:T(8,128)(2,1)S(1)}, u32[]{:S(2)}, u32[]{:S(2)}) collective-permute-start(bf16[128,1792]{1,0:T(8,128)(2,1)S(1)} %fusion.16), channel_id=1, source_target_pairs={{0,96},{16,112},{32,0},{48,16},{64,32},{80,48},{96,64},{112,80},{1... | collective-permute-start | bytes 1376264 | tf_op jit(solution)/shard_map/ppermute | solution.py:71
  162.6 11.0 %collective-permute-start.14 = (bf16[256,896]{1,0:T(8,128)(2,1)S(1)}, bf16[256,896]{1,0:T(8,128)(2,1)S(1)}, u32[]{:S(2)}, u32[]{:S(2)}) collective-permute-start(bf16[256,896]{1,0:T(8,128)(2,1)S(1)} %get-tuple-element.27), channel_id=1, source_target_pairs={{0,32},{16,48},{32,64},{48,80},{64,96},{80,112},{96,0},{112,16},{1... | collective-permute-start | bytes 1376264 | tf_op jit(solution)/shard_map/ppermute | solution.py:95
  162.7 10.9 %collective-permute-start.17 = (bf16[256,896]{1,0:T(8,128)(2,1)S(1)}, bf16[256,896]{1,0:T(8,128)(2,1)S(1)}, u32[]{:S(2)}, u32[]{:S(2)}) collective-permute-start(bf16[256,896]{1,0:T(8,128)(2,1)S(1)} %get-tuple-element.28), channel_id=1, source_target_pairs={{0,96},{16,112},{32,0},{48,16},{64,32},{80,48},{96,64},{112,80},{1... | collective-permute-start | bytes 1376264 | tf_op jit(solution)/shard_map/ppermute | solution.py:95
  173.6 11.3 %collective-permute-start.15 = (bf16[256,896]{1,0:T(8,128)(2,1)S(1)}, bf16[256,896]{1,0:T(8,128)(2,1)S(1)}, u32[]{:S(2)}, u32[]{:S(2)}) collective-permute-start(bf16[256,896]{1,0:T(8,128)(2,1)S(1)} %collective-permute-done.14), channel_id=1, source_target_pairs={{0,32},{16,48},{32,64},{48,80},{64,96},{80,112},{96,0},{112,16},{1... | collective-permute-start | bytes 1376264 | tf_op jit(solution)/shard_map/ppermute | solution.py:95
  173.6 11.3 %collective-permute-start.18 = (bf16[256,896]{1,0:T(8,128)(2,1)S(1)}, bf16[256,896]{1,0:T(8,128)(2,1)S(1)}, u32[]{:S(2)}, u32[]{:S(2)}) collective-permute-start(bf16[256,896]{1,0:T(8,128)(2,1)S(1)} %collective-permute-done.17), channel_id=1, source_target_pairs={{0,96},{16,112},{32,0},{48,16},{64,32},{80,48},{96,64},{112,80},{1... | collective-permute-start | bytes 1376264 | tf_op jit(solution)/shard_map/ppermute | solution.py:95
  184.9 10.0 %collective-permute-start.16 = (bf16[256,896]{1,0:T(8,128)(2,1)S(1)}, bf16[256,896]{1,0:T(8,128)(2,1)S(1)}, u32[]{:S(2)}, u32[]{:S(2)}) collective-permute-start(bf16[256,896]{1,0:T(8,128)(2,1)S(1)} %collective-permute-done.15), channel_id=1, source_target_pairs={{0,32},{16,48},{32,64},{48,80},{64,96},{80,112},{96,0},{112,16},{1... | collective-permute-start | bytes 1376264 | tf_op jit(solution)/shard_map/ppermute | solution.py:95
  184.9 10.0 %collective-permute-start.19 = (bf16[256,896]{1,0:T(8,128)(2,1)S(1)}, bf16[256,896]{1,0:T(8,128)(2,1)S(1)}, u32[]{:S(2)}, u32[]{:S(2)}) collective-permute-start(bf16[256,896]{1,0:T(8,128)(2,1)S(1)} %collective-permute-done.18), channel_id=1, source_target_pairs={{0,96},{16,112},{32,0},{48,16},{64,32},{80,48},{96,64},{112,80},{1... | collective-permute-start | bytes 1376264 | tf_op jit(solution)/shard_map/ppermute | solution.py:95
  195.0 2.1 copy-start.9
  195.0 2.1 copy-start.4
  197.0 9.5 %collective-permute-start.20 = (bf16[1024,1792]{1,0:T(8,128)(2,1)}, bf16[1024,1792]{1,0:T(8,128)(2,1)}, u32[]{:S(2)}, u32[]{:S(2)}) collective-permute-start(bf16[1024,1792]{1,0:T(8,128)(2,1)} %bitcast.33), channel_id=1, source_target_pairs={{0,16},{16,0},{32,48},{48,32},{64,80},{80,64},{96,112},{112,96},{1... | collective-permute-start | bytes 11010056 | tf_op jit(solution)/shard_map/ppermute | solution.py:100
  198.0 2.0 copy-start.12
Sparse Core Ops, SparseCore 0:
  9.5 54.0 all-gather.1

commit v7 on v6

--- a/solution.py
+++ b/solution.py
@@ -88,12 +88,20 @@
     chunk, width = value.shape
     parts = []
     for direction, cols in ((1, slice(0, width // 2)), (-1, slice(width // 2, width))):
-        held = value[:, cols]
         full = jnp.zeros((n_y, chunk, width // 2), value.dtype)
-        full = lax.dynamic_update_index_in_dim(full, held, y, 0)
-        for step in range(n_y - 1):
-            held = lax.ppermute(held, "row", row_perm(n_row, direction))
-            full = lax.dynamic_update_index_in_dim(full, held, (y - direction * (step + 1)) % n_y, 0)
+        full = lax.dynamic_update_index_in_dim(full, value[:, cols], y, 0)
+        leads = []
+        for sub in range(SUB_RINGS):
+            start = sub * chunk // SUB_RINGS
+            held = value[start:start + chunk // SUB_RINGS, cols]
+            for step in range(n_y - 1):
+                if sub > 0:
+                    held, _ = lax.optimization_barrier((held, leads[step]))
+                held = lax.ppermute(held, "row", row_perm(n_row, direction))
+                if sub == 0:
+                    leads.append(held)
+                place = (y - direction * (step + 1)) % n_y
+                full = lax.dynamic_update_slice(full, held[None], (place, start, 0))
         parts.append(full)
     half = jnp.concatenate(parts, axis=2).reshape(n_y * chunk, width)
     swap = [(i, i ^ 1) for i in range(n_row)]

time: 281 us -> 290 us (1.032)
  starting transfers between devices: 28.8 us -> 38.6 us
    ppermute x6 -> x12, starting transfers between devices: 10.3 us -> 20.1 us  [row_all_gather(): held = lax.ppermute(held, 'row', row_perm(n_row, direction))]
    ppermute x6 -> x12, waiting for transfers between devices: 21.2 us -> 20 us  [row_all_gather(): held = lax.ppermute(held, 'row', row_perm(n_row, direction))]
  transfers between devices with their start and end apart: 22 -> 28, of which waited for: 11 -> 14; matrix products, arithmetic and copies ran while one was open for 17% -> 16% of each run, Pallas kernels for 0% -> 0%
where the time goes in v7:
time: 290 us; the launch traced here: 289 us
  waiting for transfers between devices  109 us (38%)
  blocking collectives  56.7 us (20%)
  starting transfers between devices  38.6 us (13%)
  matrix products  38.5 us (13%)
  local copies, waits for them, and re-layouts  16.6 us (6%)
  other arithmetic  16.2 us (6%)
  between operations  13.8 us (5%)
    all_to_all x1, blocking collectives, on_device(): terms = lax.all_to_all(terms, 'col', 0, 0, tiled=False)  56.7 us
    ppermute x12, waiting for transfers between devices, row_reduce_scatter(): lax.ppermute(acc.astype(jnp.bfloat16), 'row', row_perm(n_row, direction))  44.4 us
    all_gather x1, waiting for transfers between devices, on_device(): gathered = lax.all_gather(tokens, 'col', axis=0, tiled=True)  43.5 us
    ppermute x12, starting transfers between devices, row_all_gather(): held = lax.ppermute(held, 'row', row_perm(n_row, direction))  20.1 us
    ppermute x12, waiting for transfers between devices, row_all_gather(): held = lax.ppermute(held, 'row', row_perm(n_row, direction))  20 us
    ppermute x12, starting transfers between devices, row_reduce_scatter(): lax.ppermute(acc.astype(jnp.bfloat16), 'row', row_perm(n_row, direction))  17.9 us
    dot_general x2, matrix products, row_reduce_scatter(): jnp.dot(send, w, preferred_element_type=jnp.float32).astype(jnp.bfloat16)  14.3 us
    unnamed x28, local copies, waits for them, and re-layouts  13.5 us
  transfers between devices with their start and end apart: 28, of which 14 were waited for; matrix products, arithmetic and copies ran while one was open for 16% of the time, Pallas kernels for 0%

profile of v7, /device:TPU:0, one launch (start us, length us, event | category | flops | bytes accessed | tf_op | source)
XLA Modules:
  0.0 289.0 jit_solution(9134159092676202928)
XLA Ops:
  6.5 0.7 all-gather.2.cloned.1.call-update
  7.3 5.9 %copy.13 = bf16[1024,1792]{0,1:T(8,128)(2,1)} copy(bf16[1024,1792]{1,0:T(8,128)(2,1)} %param.11) | data formatting | bytes 7340032 | tf_op args[1]
  13.2 6.0 %copy.14 = bf16[1024,1792]{0,1:T(8,128)(2,1)} copy(bf16[1024,1792]{1,0:T(8,128)(2,1)} %param.12) | data formatting | bytes 7340032 | tf_op args[2]
  19.3 0.3 fusion.38
  19.7 0.3 fusion.40
  20.1 43.5 %all-gather.2.cloned.1.call-done = bf16[2048,1024]{1,0:T(8,128)(2,1)} async-done(((bf16[128,1024]{1,0:T(8,128)(2,1)}), bf16[2048,1024]{1,0:T(8,128)(2,1)}) %all-gather.2.cloned.1.call-update) | async-done | bytes 4194320 | tf_op jit(solution)/shard_map/all_gather | solution.py:214
  63.6 0.5 broadcast_in_dim.108
  64.1 8.7 %convolution_convert_fusion.2 = bf16[1024,1792]{1,0:T(8,128)(2,1)} fusion(bf16[1024,1792]{0,1:T(8,128)(2,1)} %copy.13, pred[224,8,8,128]{3,2,1,0:T(8,128)(4,1)S(1)} %bitcast.149, bf16[2,1024,1024]{2,1,0:T(8,128)(2,1)} %bitcast.158, s32[]{:T(128)S(6)} %select_n.198), kind=kOutput, calls=%fused_computation.5 | convolution fusion | flops 3761766400 | bytes 11272196 | tf_op jit(solution)/shard_map/dot_general | solution.py:48
  72.8 0.5 broadcast_in_dim.111
  73.4 5.6 %convolution_convert_fusion = bf16[1024,1792]{1,0:T(8,128)(2,1)} fusion(bf16[1024,1792]{0,1:T(8,128)(2,1)S(1)} %copy-done, pred[224,8,8,128]{3,2,1,0:T(8,128)(4,1)S(1)} %bitcast.151, bf16[2,1024,1024]{2,1,0:T(8,128)(2,1)S(1)} %bitcast.160, s32[]{:T(128)S(6)} %select_n.198), kind=kOutput, calls=%fused_computation.3 | convolution fusion | flops 3761766400 | bytes 11272196 | tf_op jit(solution)/shard_map/dot_general | solution.py:48
  79.0 0.5 collective-permute-start.7
  79.5 6.8 %convolution_convert_fusion.3 = bf16[1024,1792]{1,0:T(8,128)(2,1)S(1)} fusion(bf16[1024,1792]{0,1:T(8,128)(2,1)} %copy.13, pred[224,8,8,128]{3,2,1,0:T(8,128)(4,1)S(1)} %bitcast.150, bf16[2,1024,1024]{2,1,0:T(8,128)(2,1)} %bitcast.159, s32[]{:T(128)S(6)} %select_n.193), kind=kOutput, calls=%fused_computation.6 | convolution fusion | flops 3761766400 | bytes 11272196 | tf_op jit(solution)/shard_map/dot_general | solution.py:52
  86.4 4.5 %convolution_convert_fusion.1 = bf16[1024,1792]{1,0:T(8,128)(2,1)S(1)} fusion(bf16[1024,1792]{0,1:T(8,128)(2,1)S(1)} %copy-done.1, pred[224,8,8,128]{3,2,1,0:T(8,128)(4,1)S(1)} %bitcast.152, bf16[2,1024,1024]{2,1,0:T(8,128)(2,1)S(1)} %bitcast.161, s32[]{:T(128)S(6)} %select_n.193), kind=kOutput, calls=%fused_computation.4 | convolution fusion | flops 3761766400 | bytes 11272196 | tf_op jit(solution)/shard_map/dot_general | solution.py:52
  90.9 1.4 convert_add_fusion.7
  92.3 1.6 collective-permute-start.1
  93.9 1.4 convert_add_fusion.3
  95.4 1.8 collective-permute-start.8
  97.2 2.3 convert_add_fusion.6
  99.5 2.3 convert_add_fusion.2
  101.9 4.2 %collective-permute-done.1 = bf16[128,1792]{1,0:T(8,128)(2,1)S(1)} collective-permute-done((bf16[128,1792]{1,0:T(8,128)(2,1)S(1)}, bf16[128,1792]{1,0:T(8,128)(2,1)S(1)}, u32[]{:S(2)}, u32[]{:S(2)}) %collective-permute-start.1) | collective-permute-done | bytes 458784 | tf_op jit(solution)/shard_map/ppermute | solution.py:71
  106.1 0.3 collective-permute-start.4
  106.4 1.6 collective-permute-start.2
  108.0 2.6 collective-permute-start.11
  110.6 1.0 collective-permute-start.9
  111.6 9.0 %collective-permute-done.4 = bf16[128,1792]{1,0:T(8,128)(2,1)S(1)} collective-permute-done((bf16[128,1792]{1,0:T(8,128)(2,1)S(1)}, bf16[128,1792]{1,0:T(8,128)(2,1)S(1)}, u32[]{:S(2)}, u32[]{:S(2)}) %collective-permute-start.4) | collective-permute-done | bytes 458784 | tf_op jit(solution)/shard_map/ppermute | solution.py:71
  120.7 0.1 fusion.25
  120.8 7.9 %collective-permute-done.2 = bf16[128,1792]{1,0:T(8,128)(2,1)S(1)} collective-permute-done((bf16[128,1792]{1,0:T(8,128)(2,1)S(1)}, bf16[128,1792]{1,0:T(8,128)(2,1)S(1)}, u32[]{:S(2)}, u32[]{:S(2)}) %collective-permute-start.2) | collective-permute-done | bytes 458784 | tf_op jit(solution)/shard_map/ppermute | solution.py:71
  128.8 0.6 collective-permute-start.3
  129.4 0.1 fusion.17
  129.5 3.4 %collective-permute-start.12 = (bf16[128,1792]{1,0:T(8,128)(2,1)S(1)}, bf16[128,1792]{1,0:T(8,128)(2,1)S(1)}, u32[]{:S(2)}, u32[]{:S(2)}) collective-permute-start(bf16[128,1792]{1,0:T(8,128)(2,1)S(1)} %fusion.17), channel_id=1, source_target_pairs={{0,96},{16,112},{32,0},{48,16},{64,32},{80,48},{96,64},{112,80},{1... | collective-permute-start | bytes 1376264 | tf_op jit(solution)/shard_map/ppermute | solution.py:71
  132.9 0.1 fusion.20
  133.0 1.4 collective-permute-start.10
  134.5 8.8 %collective-permute-done.5 = bf16[128,1792]{1,0:T(8,128)(2,1)S(1)} collective-permute-done((bf16[128,1792]{1,0:T(8,128)(2,1)S(1)}, bf16[128,1792]{1,0:T(8,128)(2,1)S(1)}, u32[]{:S(2)}, u32[]{:S(2)}) %collective-permute-start.5) | collective-permute-done | bytes 458784 | tf_op jit(solution)/shard_map/ppermute | solution.py:71
  143.3 0.1 fusion.24
  143.4 7.1 %collective-permute-done.3 = bf16[128,1792]{1,0:T(8,128)(2,1)S(1)} collective-permute-done((bf16[128,1792]{1,0:T(8,128)(2,1)S(1)}, bf16[128,1792]{1,0:T(8,128)(2,1)S(1)}, u32[]{:S(2)}, u32[]{:S(2)}) %collective-permute-start.3) | collective-permute-done | bytes 458784 | tf_op jit(solution)/shard_map/ppermute | solution.py:71
  150.6 0.1 collective-permute-done.10
  150.7 3.7 %collective-permute-start.13 = (bf16[128,1792]{1,0:T(8,128)(2,1)S(1)}, bf16[128,1792]{1,0:T(8,128)(2,1)S(1)}, u32[]{:S(2)}, u32[]{:S(2)}) collective-permute-start(bf16[128,1792]{1,0:T(8,128)(2,1)S(1)} %fusion.16), channel_id=1, source_target_pairs={{0,96},{16,112},{32,0},{48,16},{64,32},{80,48},{96,64},{112,80},{1... | collective-permute-start | bytes 1376264 | tf_op jit(solution)/shard_map/ppermute | solution.py:71
  154.4 7.1 %collective-permute-done.6 = bf16[128,1792]{1,0:T(8,128)(2,1)S(1)} collective-permute-done((bf16[128,1792]{1,0:T(8,128)(2,1)S(1)}, bf16[128,1792]{1,0:T(8,128)(2,1)S(1)}, u32[]{:S(2)}, u32[]{:S(2)}) %collective-permute-start.6) | collective-permute-done | bytes 458784 | tf_op jit(solution)/shard_map/ppermute | solution.py:71
  161.6 0.2 fusion.26
  161.8 0.2 fusion.18
  162.0 0.5 fusion.8
  162.7 3.5 %collective-permute-start.20 = (bf16[128,896]{1,0:T(8,128)(2,1)S(1)}, bf16[128,896]{1,0:T(8,128)(2,1)S(1)}, u32[]{:S(2)}, u32[]{:S(2)}) collective-permute-start(bf16[128,896]{1,0:T(8,128)(2,1)S(1)} %get-tuple-element.41), channel_id=1, source_target_pairs={{0,96},{16,112},{32,0},{48,16},{64,32},{80,48},{96,64},{112,80},{1... | collective-permute-start | bytes 688136 | tf_op jit(solution)/shard_map/ppermute | solution.py:100
  166.2 0.1 broadcast.73.clone.1
  166.4 0.1 broadcast.73.clone
  166.6 4.2 %collective-permute-done.14 = bf16[128,896]{1,0:T(8,128)(2,1)S(1)} collective-permute-done((bf16[128,896]{1,0:T(8,128)(2,1)S(1)}, bf16[128,896]{1,0:T(8,128)(2,1)S(1)}, u32[]{:S(2)}, u32[]{:S(2)}) %collective-permute-start.14) | collective-permute-done | bytes 229408 | tf_op jit(solution)/shard_map/ppermute | solution.py:100
  170.8 3.6 %collective-permute-start.23 = (bf16[128,896]{1,0:T(8,128)(2,1)S(1)}, bf16[128,896]{1,0:T(8,128)(2,1)S(1)}, u32[]{:S(2)}, u32[]{:S(2)}) collective-permute-start(bf16[128,896]{1,0:T(8,128)(2,1)S(1)} %get-tuple-element.26), channel_id=1, source_target_pairs={{0,96},{16,112},{32,0},{48,16},{64,32},{80,48},{96,64},{112,80},{1... | collective-permute-start | bytes 688136 | tf_op jit(solution)/shard_map/ppermute | solution.py:100
  174.4 3.2 %collective-permute-start.21 = (bf16[128,896]{1,0:T(8,128)(2,1)S(1)}, bf16[128,896]{1,0:T(8,128)(2,1)S(1)}, u32[]{:S(2)}, u32[]{:S(2)}) collective-permute-start(bf16[128,896]{1,0:T(8,128)(2,1)S(1)} %collective-permute-done.20), channel_id=1, source_target_pairs={{0,96},{16,112},{32,0},{48,16},{64,32},{80,48},{96,64},{112,80},{1... | collective-permute-start | bytes 688136 | tf_op jit(solution)/shard_map/ppermute | solution.py:100
  177.7 0.6 collective-permute-done.17
  178.3 5.8 %collective-permute-done.15 = bf16[128,896]{1,0:T(8,128)(2,1)S(1)} collective-permute-done((bf16[128,896]{1,0:T(8,128)(2,1)S(1)}, bf16[128,896]{1,0:T(8,128)(2,1)S(1)}, u32[]{:S(2)}, u32[]{:S(2)}) %collective-permute-start.15) | collective-permute-done | bytes 229408 | tf_op jit(solution)/shard_map/ppermute | solution.py:100
  184.1 3.2 %collective-permute-start.24 = (bf16[128,896]{1,0:T(8,128)(2,1)S(1)}, bf16[128,896]{1,0:T(8,128)(2,1)S(1)}, u32[]{:S(2)}, u32[]{:S(2)}) collective-permute-start(bf16[128,896]{1,0:T(8,128)(2,1)S(1)} %collective-permute-done.23), channel_id=1, source_target_pairs={{0,96},{16,112},{32,0},{48,16},{64,32},{80,48},{96,64},{112,80},{1... | collective-permute-start | bytes 688136 | tf_op jit(solution)/shard_map/ppermute | solution.py:100
  187.4 3.2 %collective-permute-start.22 = (bf16[128,896]{1,0:T(8,128)(2,1)S(1)}, bf16[128,896]{1,0:T(8,128)(2,1)S(1)}, u32[]{:S(2)}, u32[]{:S(2)}) collective-permute-start(bf16[128,896]{1,0:T(8,128)(2,1)S(1)} %collective-permute-done.21), channel_id=1, source_target_pairs={{0,96},{16,112},{32,0},{48,16},{64,32},{80,48},{96,64},{112,80},{1... | collective-permute-start | bytes 688136 | tf_op jit(solution)/shard_map/ppermute | solution.py:100
  190.7 2.4 collective-permute-done.18
  193.1 3.2 %collective-permute-done.16 = bf16[128,896]{1,0:T(8,128)(2,1)S(1)} collective-permute-done((bf16[128,896]{1,0:T(8,128)(2,1)S(1)}, bf16[128,896]{1,0:T(8,128)(2,1)S(1)}, u32[]{:S(2)}, u32[]{:S(2)}) %collective-permute-start.16) | collective-permute-done | bytes 229408 | tf_op jit(solution)/shard_map/ppermute | solution.py:100
  196.3 3.2 %collective-permute-start.25 = (bf16[128,896]{1,0:T(8,128)(2,1)S(1)}, bf16[128,896]{1,0:T(8,128)(2,1)S(1)}, u32[]{:S(2)}, u32[]{:S(2)}) collective-permute-start(bf16[128,896]{1,0:T(8,128)(2,1)S(1)} %collective-permute-done.24), channel_id=1, source_target_pairs={{0,96},{16,112},{32,0},{48,16},{64,32},{80,48},{96,64},{112,80},{1... | collective-permute-start | bytes 688136 | tf_op jit(solution)/shard_map/ppermute | solution.py:100
  199.7 3.8 %collective-permute-done.19 = bf16[128,896]{1,0:T(8,128)(2,1)S(1)} collective-permute-done((bf16[128,896]{1,0:T(8,128)(2,1)S(1)}, bf16[128,896]{1,0:T(8,128)(2,1)S(1)}, u32[]{:S(2)}, u32[]{:S(2)}) %collective-permute-start.19) | collective-permute-done | bytes 229408 | tf_op jit(solution)/shard_map/ppermute | solution.py:100
  203.6 2.0 pad_maximum_fusion
  205.7 0.3 fusion.36
  206.1 0.5 broadcast_in_dim.127
  206.6 0.5 broadcast_in_dim.107
  207.2 1.5 copy-done.12
  208.7 6.4 %bitcast_dynamic-update-slice_fusion.1 = bf16[2,1024,1024]{2,1,0:T(8,128)(2,1)S(1)} fusion(bf16[2,1024,1024]{2,1,0:T(8,128)(2,1)S(1)} %broadcast_in_dim.107, s32[]{:T(128)S(6)} %select_n.193, bf16[1024,1792]{1,0:T(8,128)(2,1)} %bitcast.39, bf16[1792,1024]{1,0:T(8,128)(2,1)S(1)} %copy-done.12, pred[224,8,8,128]{3,2,1,0:T(8,128)(4,1)S(1)} %bitcast.153), kind=kOutput, calls=%fused_computation.9 | convolution fusion | flops 3760979968 | bytes 11272196 | tf_op jit(solution)/shard_map/dot_general | solution.py:109
  215.1 6.5 %bitcast_dynamic-update-slice_fusion = bf16[2,1024,1024]{2,1,0:T(8,128)(2,1)S(1)} fusion(bf16[2,1024,1024]{2,1,0:T(8,128)(2,1)S(1)} %bitcast_dynamic-update-slice_fusion.1, s32[]{:T(128)S(6)} %select_n.198, bf16[1024,1792]{1,0:T(8,128)(2,1)} %collective-permute-done.26, bf16[1792,1024]{1,0:T(8,128)(2,1)S(1)} %copy-done.12, ...), kind=kOutput, calls=%fused_computation.8 | convolution fusion | flops 3760979968 | bytes 11272196 | tf_op jit(solution)/shard_map/dot_general | solution.py:110
  221.6 56.7 %all_to_all.5 = bf16[16,128,1024]{2,1,0:T(8,128)(2,1)} all-to-all(bf16[16,128,1024]{2,1,0:T(8,128)(2,1)S(1)} %bitcast.144), channel_id=1, replica_groups=mesh['row'=8,'col'=16] {'col'}, dimensions={0} | all-to-all | bytes 8388608 | tf_op jit(solution)/shard_map/all_to_all | solution.py:228
  278.2 3.9 %reduce_sum.12 = bf16[128,1024]{1,0:T(8,128)(2,1)} reduce(bf16[16,128,1024]{2,1,0:T(8,128)(2,1)} %all_to_all.5, bf16[]{:T(256)} %constant.228.clone.1), dimensions={0}, to_apply=%region_3.4 | reduce | flops 1966080 | bytes 4456450 | tf_op jit(solution)/shard_map/reduce_sum | solution.py:229
  (76 shorter events, 1.4 us)
Async XLA Ops:
  6.5 57.0 %all-gather.2.cloned.1.call-start = ((), (), s32[]{:S(2)}) async-start(), calls=%async_computation.1 | async-start | bytes 4456448 | tf_op jit(solution)/shard_map/all_gather | solution.py:214
  13.2 6.0 %copy-start.7 = (s32[14]{0:T(128)S(1)}, s32[14]{0:T(128)}, u32[]{:S(2)}) copy-start(s32[14]{0:T(128)} %param.15) | copy-start | bytes 172
  13.2 6.1 %copy-start.5 = (s32[14,48]{1,0:T(8,128)S(1)}, s32[14,48]{1,0:T(8,128)}, u32[]{:S(2)}) copy-start(s32[14,48]{1,0:T(8,128)} %param.16) | copy-start | bytes 8068
  13.2 6.1 %copy-start.6 = (s32[14,48]{1,0:T(8,128)S(1)}, s32[14,48]{1,0:T(8,128)}, u32[]{:S(2)}) copy-start(s32[14,48]{1,0:T(8,128)} %param.14) | copy-start | bytes 8068
  13.2 6.4 %copy-start.8 = (s32[14]{0:T(128)S(1)}, s32[14]{0:T(128)}, u32[]{:S(2)}) copy-start(s32[14]{0:T(128)} %param.17) | copy-start | bytes 172
  64.1 9.2 %copy-start = (bf16[1024,1792]{0,1:T(8,128)(2,1)S(1)}, bf16[1024,1792]{0,1:T(8,128)(2,1)}, u32[]{:S(2)}) copy-start(bf16[1024,1792]{0,1:T(8,128)(2,1)} %copy.14) | copy-start | bytes 11010052
  64.1 9.2 %copy-start.10 = (bf16[2048,1024]{1,0:T(8,128)(2,1)S(1)}, bf16[2048,1024]{1,0:T(8,128)(2,1)}, u32[]{:S(2)}) copy-start(bf16[2048,1024]{1,0:T(8,128)(2,1)} %all-gather.2.cloned.1.call-done) | copy-start | bytes 12582916
  72.8 18.1 %collective-permute-start = (bf16[1024,1792]{1,0:T(8,128)(2,1)}, bf16[1024,1792]{1,0:T(8,128)(2,1)}, u32[]{:S(2)}, u32[]{:S(2)}) collective-permute-start(bf16[1024,1792]{1,0:T(8,128)(2,1)} %convolution_convert_fusion.2), channel_id=1, source_target_pairs={{0,16},{16,0},{32,48},{48,32},{64,80},{80,64},{96,112},{112,96},{1... | collective-permute-start | bytes 11010056 | tf_op jit(solution)/shard_map/ppermute | solution.py:49
  73.3 5.6 %copy-start.2 = (pred[8,128,14,128]{1,0,3,2:T(8,128)(4,1)}, pred[8,128,14,128]{1,0,3,2:T(8,128)(4,1)S(1)}, u32[]{:S(2)}) copy-start(pred[8,128,14,128]{1,0,3,2:T(8,128)(4,1)S(1)} %broadcast_in_dim.111) | copy-start | bytes 5505028
  79.0 14.9 %collective-permute-start.7 = (bf16[1024,1792]{1,0:T(8,128)(2,1)}, bf16[1024,1792]{1,0:T(8,128)(2,1)}, u32[]{:S(2)}, u32[]{:S(2)}) collective-permute-start(bf16[1024,1792]{1,0:T(8,128)(2,1)} %convolution_convert_fusion), channel_id=1, source_target_pairs={{0,16},{16,0},{32,48},{48,32},{64,80},{80,64},{96,112},{112,96},{1... | collective-permute-start | bytes 11010056 | tf_op jit(solution)/shard_map/ppermute | solution.py:49
  79.5 6.8 %copy-start.1 = (bf16[1024,1792]{0,1:T(8,128)(2,1)S(1)}, bf16[1024,1792]{0,1:T(8,128)(2,1)}, u32[]{:S(2)}) copy-start(bf16[1024,1792]{0,1:T(8,128)(2,1)} %copy.14) | copy-start | bytes 11010052
  79.5 6.8 %copy-start.3 = (pred[8,128,14,128]{1,0,3,2:T(8,128)(4,1)S(1)}, pred[8,128,14,128]{1,0,3,2:T(8,128)(4,1)}, u32[]{:S(2)}) copy-start(pred[8,128,14,128]{1,0,3,2:T(8,128)(4,1)} %copy-done.2) | copy-start | bytes 5505028
  79.5 6.9 %copy-start.11 = (bf16[2048,1024]{1,0:T(8,128)(2,1)S(1)}, bf16[2048,1024]{1,0:T(8,128)(2,1)}, u32[]{:S(2)}) copy-start(bf16[2048,1024]{1,0:T(8,128)(2,1)} %all-gather.2.cloned.1.call-done) | copy-start | bytes 12582916
  92.3 13.7 %collective-permute-start.1 = (bf16[128,1792]{1,0:T(8,128)(2,1)S(1)}, bf16[128,1792]{1,0:T(8,128)(2,1)S(1)}, u32[]{:S(2)}, u32[]{:S(2)}) collective-permute-start(bf16[128,1792]{1,0:T(8,128)(2,1)S(1)} %get-tuple-element.43), channel_id=1, source_target_pairs={{0,32},{16,48},{32,64},{48,80},{64,96},{80,112},{96,0},{112,16},{1... | collective-permute-start | bytes 1376264 | tf_op jit(solution)/shard_map/ppermute | solution.py:71
  95.4 12.6 %collective-permute-start.8 = (bf16[128,1792]{1,0:T(8,128)(2,1)S(1)}, bf16[128,1792]{1,0:T(8,128)(2,1)S(1)}, u32[]{:S(2)}, u32[]{:S(2)}) collective-permute-start(bf16[128,1792]{1,0:T(8,128)(2,1)S(1)} %get-tuple-element.45), channel_id=1, source_target_pairs={{0,96},{16,112},{32,0},{48,16},{64,32},{80,48},{96,64},{112,80},{1... | collective-permute-start | bytes 1376264 | tf_op jit(solution)/shard_map/ppermute | solution.py:71
  106.1 14.6 %collective-permute-start.4 = (bf16[128,1792]{1,0:T(8,128)(2,1)S(1)}, bf16[128,1792]{1,0:T(8,128)(2,1)S(1)}, u32[]{:S(2)}, u32[]{:S(2)}) collective-permute-start(bf16[128,1792]{1,0:T(8,128)(2,1)S(1)} %get-tuple-element.17), channel_id=1, source_target_pairs={{0,32},{16,48},{32,64},{48,80},{64,96},{80,112},{96,0},{112,16},{1... | collective-permute-start | bytes 1376264 | tf_op jit(solution)/shard_map/ppermute | solution.py:71
  106.4 22.3 %collective-permute-start.2 = (bf16[128,1792]{1,0:T(8,128)(2,1)S(1)}, bf16[128,1792]{1,0:T(8,128)(2,1)S(1)}, u32[]{:S(2)}, u32[]{:S(2)}) collective-permute-start(bf16[128,1792]{1,0:T(8,128)(2,1)S(1)} %fusion.30), channel_id=1, source_target_pairs={{0,32},{16,48},{32,64},{48,80},{64,96},{80,112},{96,0},{112,16},{1... | collective-permute-start | bytes 1376264 | tf_op jit(solution)/shard_map/ppermute | solution.py:71
  108.0 21.4 %collective-permute-start.11 = (bf16[128,1792]{1,0:T(8,128)(2,1)S(1)}, bf16[128,1792]{1,0:T(8,128)(2,1)S(1)}, u32[]{:S(2)}, u32[]{:S(2)}) collective-permute-start(bf16[128,1792]{1,0:T(8,128)(2,1)S(1)} %get-tuple-element.20), channel_id=1, source_target_pairs={{0,96},{16,112},{32,0},{48,16},{64,32},{80,48},{96,64},{112,80},{1... | collective-permute-start | bytes 1376264 | tf_op jit(solution)/shard_map/ppermute | solution.py:71
  110.6 18.9 %collective-permute-start.9 = (bf16[128,1792]{1,0:T(8,128)(2,1)S(1)}, bf16[128,1792]{1,0:T(8,128)(2,1)S(1)}, u32[]{:S(2)}, u32[]{:S(2)}) collective-permute-start(bf16[128,1792]{1,0:T(8,128)(2,1)S(1)} %fusion.22), channel_id=1, source_target_pairs={{0,96},{16,112},{32,0},{48,16},{64,32},{80,48},{96,64},{112,80},{1... | collective-permute-start | bytes 1376264 | tf_op jit(solution)/shard_map/ppermute | solution.py:71
  128.7 14.6 %collective-permute-start.5 = (bf16[128,1792]{1,0:T(8,128)(2,1)S(1)}, bf16[128,1792]{1,0:T(8,128)(2,1)S(1)}, u32[]{:S(2)}, u32[]{:S(2)}) collective-permute-start(bf16[128,1792]{1,0:T(8,128)(2,1)S(1)} %fusion.25), channel_id=1, source_target_pairs={{0,32},{16,48},{32,64},{48,80},{64,96},{80,112},{96,0},{112,16},{1... | collective-permute-start | bytes 1376264 | tf_op jit(solution)/shard_map/ppermute | solution.py:71
  128.8 21.7 %collective-permute-start.3 = (bf16[128,1792]{1,0:T(8,128)(2,1)S(1)}, bf16[128,1792]{1,0:T(8,128)(2,1)S(1)}, u32[]{:S(2)}, u32[]{:S(2)}) collective-permute-start(bf16[128,1792]{1,0:T(8,128)(2,1)S(1)} %fusion.28), channel_id=1, source_target_pairs={{0,32},{16,48},{32,64},{48,80},{64,96},{80,112},{96,0},{112,16},{1... | collective-permute-start | bytes 1376264 | tf_op jit(solution)/shard_map/ppermute | solution.py:71
  129.5 21.0 %collective-permute-start.12 = (bf16[128,1792]{1,0:T(8,128)(2,1)S(1)}, bf16[128,1792]{1,0:T(8,128)(2,1)S(1)}, u32[]{:S(2)}, u32[]{:S(2)}) collective-permute-start(bf16[128,1792]{1,0:T(8,128)(2,1)S(1)} %fusion.17), channel_id=1, source_target_pairs={{0,96},{16,112},{32,0},{48,16},{64,32},{80,48},{96,64},{112,80},{1... | collective-permute-start | bytes 1376264 | tf_op jit(solution)/shard_map/ppermute | solution.py:71
  133.0 17.7 %collective-permute-start.10 = (bf16[128,1792]{1,0:T(8,128)(2,1)S(1)}, bf16[128,1792]{1,0:T(8,128)(2,1)S(1)}, u32[]{:S(2)}, u32[]{:S(2)}) collective-permute-start(bf16[128,1792]{1,0:T(8,128)(2,1)S(1)} %fusion.20), channel_id=1, source_target_pairs={{0,96},{16,112},{32,0},{48,16},{64,32},{80,48},{96,64},{112,80},{1... | collective-permute-start | bytes 1376264 | tf_op jit(solution)/shard_map/ppermute | solution.py:71
  150.5 11.1 %collective-permute-start.6 = (bf16[128,1792]{1,0:T(8,128)(2,1)S(1)}, bf16[128,1792]{1,0:T(8,128)(2,1)S(1)}, u32[]{:S(2)}, u32[]{:S(2)}) collective-permute-start(bf16[128,1792]{1,0:T(8,128)(2,1)S(1)} %fusion.24), channel_id=1, source_target_pairs={{0,32},{16,48},{32,64},{48,80},{64,96},{80,112},{96,0},{112,16},{1... | collective-permute-start | bytes 1376264 | tf_op jit(solution)/shard_map/ppermute | solution.py:71
  150.7 11.1 %collective-permute-start.13 = (bf16[128,1792]{1,0:T(8,128)(2,1)S(1)}, bf16[128,1792]{1,0:T(8,128)(2,1)S(1)}, u32[]{:S(2)}, u32[]{:S(2)}) collective-permute-start(bf16[128,1792]{1,0:T(8,128)(2,1)S(1)} %fusion.16), channel_id=1, source_target_pairs={{0,96},{16,112},{32,0},{48,16},{64,32},{80,48},{96,64},{112,80},{1... | collective-permute-start | bytes 1376264 | tf_op jit(solution)/shard_map/ppermute | solution.py:71
  162.6 8.3 %collective-permute-start.14 = (bf16[128,896]{1,0:T(8,128)(2,1)S(1)}, bf16[128,896]{1,0:T(8,128)(2,1)S(1)}, u32[]{:S(2)}, u32[]{:S(2)}) collective-permute-start(bf16[128,896]{1,0:T(8,128)(2,1)S(1)} %get-tuple-element.42), channel_id=1, source_target_pairs={{0,32},{16,48},{32,64},{48,80},{64,96},{80,112},{96,0},{112,16},{1... | collective-permute-start | bytes 688136 | tf_op jit(solution)/shard_map/ppermute | solution.py:100
  162.7 8.2 %collective-permute-start.20 = (bf16[128,896]{1,0:T(8,128)(2,1)S(1)}, bf16[128,896]{1,0:T(8,128)(2,1)S(1)}, u32[]{:S(2)}, u32[]{:S(2)}) collective-permute-start(bf16[128,896]{1,0:T(8,128)(2,1)S(1)} %get-tuple-element.41), channel_id=1, source_target_pairs={{0,96},{16,112},{32,0},{48,16},{64,32},{80,48},{96,64},{112,80},{1... | collective-permute-start | bytes 688136 | tf_op jit(solution)/shard_map/ppermute | solution.py:100
  170.8 7.5 %collective-permute-start.17 = (bf16[128,896]{1,0:T(8,128)(2,1)S(1)}, bf16[128,896]{1,0:T(8,128)(2,1)S(1)}, u32[]{:S(2)}, u32[]{:S(2)}) collective-permute-start(bf16[128,896]{1,0:T(8,128)(2,1)S(1)} %get-tuple-element.23), channel_id=1, source_target_pairs={{0,32},{16,48},{32,64},{48,80},{64,96},{80,112},{96,0},{112,16},{1... | collective-permute-start | bytes 688136 | tf_op jit(solution)/shard_map/ppermute | solution.py:100
  170.8 13.3 %collective-permute-start.23 = (bf16[128,896]{1,0:T(8,128)(2,1)S(1)}, bf16[128,896]{1,0:T(8,128)(2,1)S(1)}, u32[]{:S(2)}, u32[]{:S(2)}) collective-permute-start(bf16[128,896]{1,0:T(8,128)(2,1)S(1)} %get-tuple-element.26), channel_id=1, source_target_pairs={{0,96},{16,112},{32,0},{48,16},{64,32},{80,48},{96,64},{112,80},{1... | collective-permute-start | bytes 688136 | tf_op jit(solution)/shard_map/ppermute | solution.py:100
  174.4 9.7 %collective-permute-start.15 = (bf16[128,896]{1,0:T(8,128)(2,1)S(1)}, bf16[128,896]{1,0:T(8,128)(2,1)S(1)}, u32[]{:S(2)}, u32[]{:S(2)}) collective-permute-start(bf16[128,896]{1,0:T(8,128)(2,1)S(1)} %collective-permute-done.14), channel_id=1, source_target_pairs={{0,32},{16,48},{32,64},{48,80},{64,96},{80,112},{96,0},{112,16},{1... | collective-permute-start | bytes 688136 | tf_op jit(solution)/shard_map/ppermute | solution.py:100
  174.4 9.7 %collective-permute-start.21 = (bf16[128,896]{1,0:T(8,128)(2,1)S(1)}, bf16[128,896]{1,0:T(8,128)(2,1)S(1)}, u32[]{:S(2)}, u32[]{:S(2)}) collective-permute-start(bf16[128,896]{1,0:T(8,128)(2,1)S(1)} %collective-permute-done.20), channel_id=1, source_target_pairs={{0,96},{16,112},{32,0},{48,16},{64,32},{80,48},{96,64},{112,80},{1... | collective-permute-start | bytes 688136 | tf_op jit(solution)/shard_map/ppermute | solution.py:100
  184.1 8.9 %collective-permute-start.18 = (bf16[128,896]{1,0:T(8,128)(2,1)S(1)}, bf16[128,896]{1,0:T(8,128)(2,1)S(1)}, u32[]{:S(2)}, u32[]{:S(2)}) collective-permute-start(bf16[128,896]{1,0:T(8,128)(2,1)S(1)} %collective-permute-done.17), channel_id=1, source_target_pairs={{0,32},{16,48},{32,64},{48,80},{64,96},{80,112},{96,0},{112,16},{1... | collective-permute-start | bytes 688136 | tf_op jit(solution)/shard_map/ppermute | solution.py:100
  184.1 12.1 %collective-permute-start.24 = (bf16[128,896]{1,0:T(8,128)(2,1)S(1)}, bf16[128,896]{1,0:T(8,128)(2,1)S(1)}, u32[]{:S(2)}, u32[]{:S(2)}) collective-permute-start(bf16[128,896]{1,0:T(8,128)(2,1)S(1)} %collective-permute-done.23), channel_id=1, source_target_pairs={{0,96},{16,112},{32,0},{48,16},{64,32},{80,48},{96,64},{112,80},{1... | collective-permute-start | bytes 688136 | tf_op jit(solution)/shard_map/ppermute | solution.py:100
  187.4 8.9 %collective-permute-start.16 = (bf16[128,896]{1,0:T(8,128)(2,1)S(1)}, bf16[128,896]{1,0:T(8,128)(2,1)S(1)}, u32[]{:S(2)}, u32[]{:S(2)}) collective-permute-start(bf16[128,896]{1,0:T(8,128)(2,1)S(1)} %collective-permute-done.15), channel_id=1, source_target_pairs={{0,32},{16,48},{32,64},{48,80},{64,96},{80,112},{96,0},{112,16},{1... | collective-permute-start | bytes 688136 | tf_op jit(solution)/shard_map/ppermute | solution.py:100
  187.4 8.9 %collective-permute-start.22 = (bf16[128,896]{1,0:T(8,128)(2,1)S(1)}, bf16[128,896]{1,0:T(8,128)(2,1)S(1)}, u32[]{:S(2)}, u32[]{:S(2)}) collective-permute-start(bf16[128,896]{1,0:T(8,128)(2,1)S(1)} %collective-permute-done.21), channel_id=1, source_target_pairs={{0,96},{16,112},{32,0},{48,16},{64,32},{80,48},{96,64},{112,80},{1... | collective-permute-start | bytes 688136 | tf_op jit(solution)/shard_map/ppermute | solution.py:100
  196.3 7.2 %collective-permute-start.19 = (bf16[128,896]{1,0:T(8,128)(2,1)S(1)}, bf16[128,896]{1,0:T(8,128)(2,1)S(1)}, u32[]{:S(2)}, u32[]{:S(2)}) collective-permute-start(bf16[128,896]{1,0:T(8,128)(2,1)S(1)} %collective-permute-done.18), channel_id=1, source_target_pairs={{0,32},{16,48},{32,64},{48,80},{64,96},{80,112},{96,0},{112,16},{1... | collective-permute-start | bytes 688136 | tf_op jit(solution)/shard_map/ppermute | solution.py:100
  196.3 7.3 %collective-permute-start.25 = (bf16[128,896]{1,0:T(8,128)(2,1)S(1)}, bf16[128,896]{1,0:T(8,128)(2,1)S(1)}, u32[]{:S(2)}, u32[]{:S(2)}) collective-permute-start(bf16[128,896]{1,0:T(8,128)(2,1)S(1)} %collective-permute-done.24), channel_id=1, source_target_pairs={{0,96},{16,112},{32,0},{48,16},{64,32},{80,48},{96,64},{112,80},{1... | collective-permute-start | bytes 688136 | tf_op jit(solution)/shard_map/ppermute | solution.py:100
  203.6 2.1 copy-start.9
  203.6 2.1 copy-start.4
  205.7 9.5 %collective-permute-start.26 = (bf16[1024,1792]{1,0:T(8,128)(2,1)}, bf16[1024,1792]{1,0:T(8,128)(2,1)}, u32[]{:S(2)}, u32[]{:S(2)}) collective-permute-start(bf16[1024,1792]{1,0:T(8,128)(2,1)} %bitcast.39), channel_id=1, source_target_pairs={{0,16},{16,0},{32,48},{48,32},{64,80},{80,64},{96,112},{112,96},{1... | collective-permute-start | bytes 11010056 | tf_op jit(solution)/shard_map/ppermute | solution.py:108
  206.6 2.0 copy-start.12
Sparse Core Ops, SparseCore 0:
  9.5 54.0 all-gather.1

commit v8 on v6

--- a/solution.py
+++ b/solution.py
@@ -68,6 +68,8 @@
             for step in range(n_y - 1):
                 if sub > 0:
                     acc, _ = lax.optimization_barrier((acc, leads[step]))
+                elif direction < 0:
+                    acc, _ = lax.optimization_barrier((acc, first_leads[step]))
                 received = lax.ppermute(
                     acc.astype(jnp.bfloat16), "row", row_perm(n_row, direction)
                 )
@@ -76,6 +78,7 @@
                 index = (index - direction) % n_y
                 acc = received.astype(jnp.float32) + own(index)[rows_of]
             pieces.append(acc)
+        first_leads = leads
         results.append(jnp.concatenate(pieces, axis=0))
     return results
 

time: 281 us -> 305 us (1.085)
  waiting for transfers between devices: 110 us -> 133 us
  other arithmetic: 16.2 us -> 20.5 us
  starting transfers between devices: 28.8 us -> 24.9 us
    ppermute x12, waiting for transfers between devices: 44.4 us -> 62.7 us  [row_reduce_scatter(): lax.ppermute(acc.astype(jnp.bfloat16), 'row', row_perm(n_row, direction))]
    ppermute x6, waiting for transfers between devices: 21.2 us -> 26.5 us  [row_all_gather(): held = lax.ppermute(held, 'row', row_perm(n_row, direction))]
    ppermute x12, starting transfers between devices: 17.9 us -> 13.9 us  [row_reduce_scatter(): lax.ppermute(acc.astype(jnp.bfloat16), 'row', row_perm(n_row, direction))]
    add x6, other arithmetic: 0.78 us -> 4 us  [row_reduce_scatter(): acc = received.astype(jnp.float32) + own(index)[rows_of]]
  transfers between devices with their start and end apart: 22 -> 22, of which waited for: 11 -> 14; matrix products, arithmetic and copies ran while one was open for 17% -> 17% of each run, Pallas kernels for 0% -> 0%
where the time goes in v8:
time: 305 us; the launch traced here: 304 us
  waiting for transfers between devices  133 us (44%)
  blocking collectives  56.6 us (19%)
  matrix products  38.4 us (13%)
  starting transfers between devices  24.9 us (8%)
  other arithmetic  20.5 us (7%)
  local copies, waits for them, and re-layouts  16.5 us (5%)
  between operations  13.8 us (5%)
    ppermute x12, waiting for transfers between devices, row_reduce_scatter(): lax.ppermute(acc.astype(jnp.bfloat16), 'row', row_perm(n_row, direction))  62.7 us
    all_to_all x1, blocking collectives, on_device(): terms = lax.all_to_all(terms, 'col', 0, 0, tiled=False)  56.6 us
    all_gather x1, waiting for transfers between devices, on_device(): gathered = lax.all_gather(tokens, 'col', axis=0, tiled=True)  43.5 us
    ppermute x6, waiting for transfers between devices, row_all_gather(): held = lax.ppermute(held, 'row', row_perm(n_row, direction))  26.5 us
    dot_general x2, matrix products, row_reduce_scatter(): jnp.dot(send, w, preferred_element_type=jnp.float32).astype(jnp.bfloat16)  14.3 us
    ppermute x12, starting transfers between devices, row_reduce_scatter(): lax.ppermute(acc.astype(jnp.bfloat16), 'row', row_perm(n_row, direction))  13.9 us
    unnamed x28, local copies, waits for them, and re-layouts  13.5 us
    dot_general x2, matrix products, row_reduce_scatter(): jnp.dot(keep, w, preferred_element_type=jnp.float32).astype(jnp.bfloat16)  11.2 us
  transfers between devices with their start and end apart: 22, of which 14 were waited for; matrix products, arithmetic and copies ran while one was open for 17% of the time, Pallas kernels for 0%

profile of v8, /device:TPU:0, one launch (start us, length us, event | category | flops | bytes accessed | tf_op | source)
XLA Modules:
  0.0 304.2 jit_solution(6072407009319257865)
XLA Ops:
  6.5 0.7 all-gather.2.cloned.1.call-update
  7.3 5.9 %copy.13 = bf16[1024,1792]{0,1:T(8,128)(2,1)} copy(bf16[1024,1792]{1,0:T(8,128)(2,1)} %param.11) | data formatting | bytes 7340032 | tf_op args[1]
  13.2 6.0 %copy.14 = bf16[1024,1792]{0,1:T(8,128)(2,1)} copy(bf16[1024,1792]{1,0:T(8,128)(2,1)} %param.12) | data formatting | bytes 7340032 | tf_op args[2]
  19.3 0.3 fusion.33
  19.7 0.3 fusion.35
  20.1 43.5 %all-gather.2.cloned.1.call-done = bf16[2048,1024]{1,0:T(8,128)(2,1)} async-done(((bf16[128,1024]{1,0:T(8,128)(2,1)}), bf16[2048,1024]{1,0:T(8,128)(2,1)}) %all-gather.2.cloned.1.call-update) | async-done | bytes 4194320 | tf_op jit(solution)/shard_map/all_gather | solution.py:209
  63.6 0.5 broadcast_in_dim.90
  64.1 8.7 %convolution_convert_fusion.2 = bf16[1024,1792]{1,0:T(8,128)(2,1)} fusion(bf16[1024,1792]{0,1:T(8,128)(2,1)} %copy.13, pred[224,8,8,128]{3,2,1,0:T(8,128)(4,1)S(1)} %bitcast.129, bf16[2,1024,1024]{2,1,0:T(8,128)(2,1)} %bitcast.138, s32[]{:T(128)S(6)} %select_n.180), kind=kOutput, calls=%fused_computation.5 | convolution fusion | flops 3761766400 | bytes 11272196 | tf_op jit(solution)/shard_map/dot_general | solution.py:48
  72.8 0.5 broadcast_in_dim.93
  73.4 5.6 %convolution_convert_fusion = bf16[1024,1792]{1,0:T(8,128)(2,1)} fusion(bf16[1024,1792]{0,1:T(8,128)(2,1)S(1)} %copy-done, pred[224,8,8,128]{3,2,1,0:T(8,128)(4,1)S(1)} %bitcast.131, bf16[2,1024,1024]{2,1,0:T(8,128)(2,1)S(1)} %bitcast.140, s32[]{:T(128)S(6)} %select_n.180), kind=kOutput, calls=%fused_computation.3 | convolution fusion | flops 3761766400 | bytes 11272196 | tf_op jit(solution)/shard_map/dot_general | solution.py:48
  79.0 0.5 collective-permute-start.7
  79.5 6.8 %convolution_convert_fusion.3 = bf16[1024,1792]{1,0:T(8,128)(2,1)S(1)} fusion(bf16[1024,1792]{0,1:T(8,128)(2,1)} %copy.13, pred[224,8,8,128]{3,2,1,0:T(8,128)(4,1)S(1)} %bitcast.130, bf16[2,1024,1024]{2,1,0:T(8,128)(2,1)} %bitcast.139, s32[]{:T(128)S(6)} %select_n.175), kind=kOutput, calls=%fused_computation.6 | convolution fusion | flops 3761766400 | bytes 11272196 | tf_op jit(solution)/shard_map/dot_general | solution.py:52
  86.4 4.4 %convolution_convert_fusion.1 = bf16[1024,1792]{1,0:T(8,128)(2,1)S(1)} fusion(bf16[1024,1792]{0,1:T(8,128)(2,1)S(1)} %copy-done.1, pred[224,8,8,128]{3,2,1,0:T(8,128)(4,1)S(1)} %bitcast.132, bf16[2,1024,1024]{2,1,0:T(8,128)(2,1)S(1)} %bitcast.141, s32[]{:T(128)S(6)} %select_n.175), kind=kOutput, calls=%fused_computation.4 | convolution fusion | flops 3761766400 | bytes 11272196 | tf_op jit(solution)/shard_map/dot_general | solution.py:52
  90.8 1.4 convert_add_fusion.7
  92.3 1.6 collective-permute-start.1
  93.8 1.4 convert_add_fusion.3
  95.3 10.7 %collective-permute-done.1 = bf16[128,1792]{1,0:T(8,128)(2,1)S(1)} collective-permute-done((bf16[128,1792]{1,0:T(8,128)(2,1)S(1)}, bf16[128,1792]{1,0:T(8,128)(2,1)S(1)}, u32[]{:S(2)}, u32[]{:S(2)}) %collective-permute-start.1) | collective-permute-done | bytes 458784 | tf_op jit(solution)/shard_map/ppermute | solution.py:73
  106.0 1.5 collective-permute-start.8
  107.5 3.6 %convert_add_fusion.4 = (f32[1,256,1792]{2,1,0:T(8,128)}, f32[1,256,1792]{2,1,0:T(8,128)S(1)}, f32[1,256,1792]{2,1,0:T(8,128)S(1)}) fusion(bf16[4,256,1792]{2,1,0:T(8,128)(2,1)} %bitcast.5, s32[]{:T(128)S(6)} %select_n.186, bf16[4,256,1792]{2,1,0:T(8,128)(2,1)S(1)} %bitcast.128, s32[]{:T(128)S(6)} %select_n.184, s32[]{:T(128)S(6)} %select_n.182), kind=kLoop, calls=%fused_computation.27 | loop fusion | flops 4128768 | bytes 11010060 | tf_op jit(solution)/shard_map/add | solution.py:58
  111.1 2.3 convert_add_fusion.2
  113.4 0.6 collective-permute-start.4
  114.0 3.6 %collective-permute-done.8 = bf16[128,1792]{1,0:T(8,128)(2,1)S(1)} collective-permute-done((bf16[128,1792]{1,0:T(8,128)(2,1)S(1)}, bf16[128,1792]{1,0:T(8,128)(2,1)S(1)}, u32[]{:S(2)}, u32[]{:S(2)}) %collective-permute-start.8) | collective-permute-done | bytes 458784 | tf_op jit(solution)/shard_map/ppermute | solution.py:73
  117.6 2.7 collective-permute-start.11
  120.3 0.1 fusion.28
  120.5 8.1 %collective-permute-done.11 = bf16[128,1792]{1,0:T(8,128)(2,1)S(1)} collective-permute-done((bf16[128,1792]{1,0:T(8,128)(2,1)S(1)}, bf16[128,1792]{1,0:T(8,128)(2,1)S(1)}, u32[]{:S(2)}, u32[]{:S(2)}) %collective-permute-start.11) | collective-permute-done | bytes 458784 | tf_op jit(solution)/shard_map/ppermute | solution.py:73
  128.6 0.2 fusion.20
  128.8 7.1 %collective-permute-done.2 = bf16[128,1792]{1,0:T(8,128)(2,1)S(1)} collective-permute-done((bf16[128,1792]{1,0:T(8,128)(2,1)S(1)}, bf16[128,1792]{1,0:T(8,128)(2,1)S(1)}, u32[]{:S(2)}, u32[]{:S(2)}) %collective-permute-start.2) | collective-permute-done | bytes 458784 | tf_op jit(solution)/shard_map/ppermute | solution.py:73
  135.9 0.1 fusion.23
  135.9 2.1 collective-permute-start.5
  138.0 8.5 %collective-permute-done.9 = bf16[128,1792]{1,0:T(8,128)(2,1)S(1)} collective-permute-done((bf16[128,1792]{1,0:T(8,128)(2,1)S(1)}, bf16[128,1792]{1,0:T(8,128)(2,1)S(1)}, u32[]{:S(2)}, u32[]{:S(2)}) %collective-permute-start.9) | collective-permute-done | bytes 458784 | tf_op jit(solution)/shard_map/ppermute | solution.py:73
  146.5 1.3 collective-permute-start.12
  147.8 0.1 fusion.26
  147.9 0.8 collective-permute-start.3
  148.7 7.4 %collective-permute-done.12 = bf16[128,1792]{1,0:T(8,128)(2,1)S(1)} collective-permute-done((bf16[128,1792]{1,0:T(8,128)(2,1)S(1)}, bf16[128,1792]{1,0:T(8,128)(2,1)S(1)}, u32[]{:S(2)}, u32[]{:S(2)}) %collective-permute-start.12) | collective-permute-done | bytes 458784 | tf_op jit(solution)/shard_map/ppermute | solution.py:73
  156.2 1.1 fusion.19
  157.3 1.5 collective-permute-done.3
  158.8 1.2 collective-permute-start.10
  160.0 0.8 fusion.22
  160.9 0.8 collective-permute-start.6
  161.7 7.8 %collective-permute-done.10 = bf16[128,1792]{1,0:T(8,128)(2,1)S(1)} collective-permute-done((bf16[128,1792]{1,0:T(8,128)(2,1)}, bf16[128,1792]{1,0:T(8,128)(2,1)S(1)}, u32[]{:S(2)}, u32[]{:S(2)}) %collective-permute-start.10) | collective-permute-done | bytes 458784 | tf_op jit(solution)/shard_map/ppermute | solution.py:73
  169.5 1.2 collective-permute-start.13
  170.7 0.3 collective-permute-done.6
  171.1 1.6 fusion.24
  172.7 7.6 %collective-permute-done.13 = bf16[128,1792]{1,0:T(8,128)(2,1)S(1)} collective-permute-done((bf16[128,1792]{1,0:T(8,128)(2,1)}, bf16[128,1792]{1,0:T(8,128)(2,1)S(1)}, u32[]{:S(2)}, u32[]{:S(2)}) %collective-permute-start.13) | collective-permute-done | bytes 458784 | tf_op jit(solution)/shard_map/ppermute | solution.py:73
  180.3 0.2 fusion.18
  180.5 0.5 fusion.8
  181.0 0.1 fusion.46
  181.2 3.2 %collective-permute-start.17 = (bf16[256,896]{1,0:T(8,128)(2,1)S(1)}, bf16[256,896]{1,0:T(8,128)(2,1)S(1)}, u32[]{:S(2)}, u32[]{:S(2)}) collective-permute-start(bf16[256,896]{1,0:T(8,128)(2,1)S(1)} %get-tuple-element.38), channel_id=1, source_target_pairs={{0,96},{16,112},{32,0},{48,16},{64,32},{80,48},{96,64},{112,80},{1... | collective-permute-start | bytes 1376264 | tf_op jit(solution)/shard_map/ppermute | solution.py:98
  184.4 0.1 broadcast.73.clone.1
  184.6 0.1 broadcast.73.clone
  184.8 10.7 %collective-permute-done.14 = bf16[256,896]{1,0:T(8,128)(2,1)S(1)} collective-permute-done((bf16[256,896]{1,0:T(8,128)(2,1)S(1)}, bf16[256,896]{1,0:T(8,128)(2,1)S(1)}, u32[]{:S(2)}, u32[]{:S(2)}) %collective-permute-start.14) | collective-permute-done | bytes 458784 | tf_op jit(solution)/shard_map/ppermute | solution.py:98
  195.5 3.5 %collective-permute-start.18 = (bf16[256,896]{1,0:T(8,128)(2,1)S(1)}, bf16[256,896]{1,0:T(8,128)(2,1)S(1)}, u32[]{:S(2)}, u32[]{:S(2)}) collective-permute-start(bf16[256,896]{1,0:T(8,128)(2,1)S(1)} %collective-permute-done.17), channel_id=1, source_target_pairs={{0,96},{16,112},{32,0},{48,16},{64,32},{80,48},{96,64},{112,80},{1... | collective-permute-start | bytes 1376264 | tf_op jit(solution)/shard_map/ppermute | solution.py:98
  199.1 9.9 %collective-permute-done.15 = bf16[256,896]{1,0:T(8,128)(2,1)S(1)} collective-permute-done((bf16[256,896]{1,0:T(8,128)(2,1)S(1)}, bf16[256,896]{1,0:T(8,128)(2,1)S(1)}, u32[]{:S(2)}, u32[]{:S(2)}) %collective-permute-start.15) | collective-permute-done | bytes 458784 | tf_op jit(solution)/shard_map/ppermute | solution.py:98
  209.0 3.7 %collective-permute-start.19 = (bf16[256,896]{1,0:T(8,128)(2,1)S(1)}, bf16[256,896]{1,0:T(8,128)(2,1)S(1)}, u32[]{:S(2)}, u32[]{:S(2)}) collective-permute-start(bf16[256,896]{1,0:T(8,128)(2,1)S(1)} %collective-permute-done.18), channel_id=1, source_target_pairs={{0,96},{16,112},{32,0},{48,16},{64,32},{80,48},{96,64},{112,80},{1... | collective-permute-start | bytes 1376264 | tf_op jit(solution)/shard_map/ppermute | solution.py:98
  212.8 5.9 %collective-permute-done.16 = bf16[256,896]{1,0:T(8,128)(2,1)S(1)} collective-permute-done((bf16[256,896]{1,0:T(8,128)(2,1)S(1)}, bf16[256,896]{1,0:T(8,128)(2,1)S(1)}, u32[]{:S(2)}, u32[]{:S(2)}) %collective-permute-start.16) | collective-permute-done | bytes 458784 | tf_op jit(solution)/shard_map/ppermute | solution.py:98
  218.9 2.0 pad_maximum_fusion
  221.0 0.3 fusion.31
  221.3 0.5 broadcast_in_dim.103
  221.9 0.5 broadcast_in_dim.89
  222.4 1.5 copy-done.12
  223.9 6.4 %bitcast_dynamic-update-slice_fusion.1 = bf16[2,1024,1024]{2,1,0:T(8,128)(2,1)S(1)} fusion(bf16[2,1024,1024]{2,1,0:T(8,128)(2,1)S(1)} %broadcast_in_dim.89, s32[]{:T(128)S(6)} %select_n.175, bf16[1024,1792]{1,0:T(8,128)(2,1)} %bitcast.33, bf16[1792,1024]{1,0:T(8,128)(2,1)S(1)} %copy-done.12, pred[224,8,8,128]{3,2,1,0:T(8,128)(4,1)S(1)} %bitcast.133), kind=kOutput, calls=%fused_computation.9 | convolution fusion | flops 3760979968 | bytes 11272196 | tf_op jit(solution)/shard_map/dot_general | solution.py:104
  230.4 6.5 %bitcast_dynamic-update-slice_fusion = bf16[2,1024,1024]{2,1,0:T(8,128)(2,1)S(1)} fusion(bf16[2,1024,1024]{2,1,0:T(8,128)(2,1)S(1)} %bitcast_dynamic-update-slice_fusion.1, s32[]{:T(128)S(6)} %select_n.180, bf16[1024,1792]{1,0:T(8,128)(2,1)} %collective-permute-done.20, bf16[1792,1024]{1,0:T(8,128)(2,1)S(1)} %copy-done.12, ...), kind=kOutput, calls=%fused_computation.8 | convolution fusion | flops 3760979968 | bytes 11272196 | tf_op jit(solution)/shard_map/dot_general | solution.py:105
  236.8 56.6 %all_to_all.5 = bf16[16,128,1024]{2,1,0:T(8,128)(2,1)} all-to-all(bf16[16,128,1024]{2,1,0:T(8,128)(2,1)S(1)} %bitcast.124), channel_id=1, replica_groups=mesh['row'=8,'col'=16] {'col'}, dimensions={0} | all-to-all | bytes 8388608 | tf_op jit(solution)/shard_map/all_to_all | solution.py:223
  293.4 3.9 %reduce_sum.12 = bf16[128,1024]{1,0:T(8,128)(2,1)} reduce(bf16[16,128,1024]{2,1,0:T(8,128)(2,1)} %all_to_all.5, bf16[]{:T(256)} %constant.226.clone.1), dimensions={0}, to_apply=%region_3.4 | reduce | flops 1966080 | bytes 4456450 | tf_op jit(solution)/shard_map/reduce_sum | solution.py:224
  (56 shorter events, 1.0 us)
Async XLA Ops:
  6.5 57.0 %all-gather.2.cloned.1.call-start = ((), (), s32[]{:S(2)}) async-start(), calls=%async_computation.1 | async-start | bytes 4456448 | tf_op jit(solution)/shard_map/all_gather | solution.py:209
  13.2 6.0 %copy-start.7 = (s32[14]{0:T(128)S(1)}, s32[14]{0:T(128)}, u32[]{:S(2)}) copy-start(s32[14]{0:T(128)} %param.15) | copy-start | bytes 172
  13.2 6.1 %copy-start.5 = (s32[14,48]{1,0:T(8,128)S(1)}, s32[14,48]{1,0:T(8,128)}, u32[]{:S(2)}) copy-start(s32[14,48]{1,0:T(8,128)} %param.16) | copy-start | bytes 8068
  13.2 6.1 %copy-start.6 = (s32[14,48]{1,0:T(8,128)S(1)}, s32[14,48]{1,0:T(8,128)}, u32[]{:S(2)}) copy-start(s32[14,48]{1,0:T(8,128)} %param.14) | copy-start | bytes 8068
  13.2 6.4 %copy-start.8 = (s32[14]{0:T(128)S(1)}, s32[14]{0:T(128)}, u32[]{:S(2)}) copy-start(s32[14]{0:T(128)} %param.17) | copy-start | bytes 172
  64.1 9.3 %copy-start = (bf16[1024,1792]{0,1:T(8,128)(2,1)S(1)}, bf16[1024,1792]{0,1:T(8,128)(2,1)}, u32[]{:S(2)}) copy-start(bf16[1024,1792]{0,1:T(8,128)(2,1)} %copy.14) | copy-start | bytes 11010052
  64.1 9.3 %copy-start.10 = (bf16[2048,1024]{1,0:T(8,128)(2,1)S(1)}, bf16[2048,1024]{1,0:T(8,128)(2,1)}, u32[]{:S(2)}) copy-start(bf16[2048,1024]{1,0:T(8,128)(2,1)} %all-gather.2.cloned.1.call-done) | copy-start | bytes 12582916
  72.8 17.9 %collective-permute-start = (bf16[1024,1792]{1,0:T(8,128)(2,1)}, bf16[1024,1792]{1,0:T(8,128)(2,1)}, u32[]{:S(2)}, u32[]{:S(2)}) collective-permute-start(bf16[1024,1792]{1,0:T(8,128)(2,1)} %convolution_convert_fusion.2), channel_id=1, source_target_pairs={{0,16},{16,0},{32,48},{48,32},{64,80},{80,64},{96,112},{112,96},{1... | collective-permute-start | bytes 11010056 | tf_op jit(solution)/shard_map/ppermute | solution.py:49
  73.4 5.6 %copy-start.2 = (pred[8,128,14,128]{1,0,3,2:T(8,128)(4,1)}, pred[8,128,14,128]{1,0,3,2:T(8,128)(4,1)S(1)}, u32[]{:S(2)}) copy-start(pred[8,128,14,128]{1,0,3,2:T(8,128)(4,1)S(1)} %broadcast_in_dim.93) | copy-start | bytes 5505028
  79.0 14.8 %collective-permute-start.7 = (bf16[1024,1792]{1,0:T(8,128)(2,1)}, bf16[1024,1792]{1,0:T(8,128)(2,1)}, u32[]{:S(2)}, u32[]{:S(2)}) collective-permute-start(bf16[1024,1792]{1,0:T(8,128)(2,1)} %convolution_convert_fusion), channel_id=1, source_target_pairs={{0,16},{16,0},{32,48},{48,32},{64,80},{80,64},{96,112},{112,96},{1... | collective-permute-start | bytes 11010056 | tf_op jit(solution)/shard_map/ppermute | solution.py:49
  79.5 6.8 %copy-start.1 = (bf16[1024,1792]{0,1:T(8,128)(2,1)S(1)}, bf16[1024,1792]{0,1:T(8,128)(2,1)}, u32[]{:S(2)}) copy-start(bf16[1024,1792]{0,1:T(8,128)(2,1)} %copy.14) | copy-start | bytes 11010052
  79.5 6.8 %copy-start.3 = (pred[8,128,14,128]{1,0,3,2:T(8,128)(4,1)S(1)}, pred[8,128,14,128]{1,0,3,2:T(8,128)(4,1)}, u32[]{:S(2)}) copy-start(pred[8,128,14,128]{1,0,3,2:T(8,128)(4,1)} %copy-done.2) | copy-start | bytes 5505028
  79.5 6.9 %copy-start.11 = (bf16[2048,1024]{1,0:T(8,128)(2,1)S(1)}, bf16[2048,1024]{1,0:T(8,128)(2,1)}, u32[]{:S(2)}) copy-start(bf16[2048,1024]{1,0:T(8,128)(2,1)} %all-gather.2.cloned.1.call-done) | copy-start | bytes 12582916
  92.3 13.7 %collective-permute-start.1 = (bf16[128,1792]{1,0:T(8,128)(2,1)S(1)}, bf16[128,1792]{1,0:T(8,128)(2,1)S(1)}, u32[]{:S(2)}, u32[]{:S(2)}) collective-permute-start(bf16[128,1792]{1,0:T(8,128)(2,1)S(1)} %get-tuple-element.40), channel_id=1, source_target_pairs={{0,32},{16,48},{32,64},{48,80},{64,96},{80,112},{96,0},{112,16},{1... | collective-permute-start | bytes 1376264 | tf_op jit(solution)/shard_map/ppermute | solution.py:73
  106.0 11.6 %collective-permute-start.8 = (bf16[128,1792]{1,0:T(8,128)(2,1)S(1)}, bf16[128,1792]{1,0:T(8,128)(2,1)S(1)}, u32[]{:S(2)}, u32[]{:S(2)}) collective-permute-start(bf16[128,1792]{1,0:T(8,128)(2,1)S(1)} %get-tuple-element.17), channel_id=1, source_target_pairs={{0,96},{16,112},{32,0},{48,16},{64,32},{80,48},{96,64},{112,80},{1... | collective-permute-start | bytes 1376264 | tf_op jit(solution)/shard_map/ppermute | solution.py:73
  113.4 22.4 %collective-permute-start.4 = (bf16[128,1792]{1,0:T(8,128)(2,1)S(1)}, bf16[128,1792]{1,0:T(8,128)(2,1)S(1)}, u32[]{:S(2)}, u32[]{:S(2)}) collective-permute-start(bf16[128,1792]{1,0:T(8,128)(2,1)S(1)} %get-tuple-element.14), channel_id=1, source_target_pairs={{0,32},{16,48},{32,64},{48,80},{64,96},{80,112},{96,0},{112,16},{1... | collective-permute-start | bytes 1376264 | tf_op jit(solution)/shard_map/ppermute | solution.py:73
  117.6 11.0 %collective-permute-start.11 = (bf16[128,1792]{1,0:T(8,128)(2,1)S(1)}, bf16[128,1792]{1,0:T(8,128)(2,1)S(1)}, u32[]{:S(2)}, u32[]{:S(2)}) collective-permute-start(bf16[128,1792]{1,0:T(8,128)(2,1)S(1)} %get-tuple-element.20), channel_id=1, source_target_pairs={{0,96},{16,112},{32,0},{48,16},{64,32},{80,48},{96,64},{112,80},{1... | collective-permute-start | bytes 1376264 | tf_op jit(solution)/shard_map/ppermute | solution.py:73
  120.4 15.4 %collective-permute-start.2 = (bf16[128,1792]{1,0:T(8,128)(2,1)S(1)}, bf16[128,1792]{1,0:T(8,128)(2,1)S(1)}, u32[]{:S(2)}, u32[]{:S(2)}) collective-permute-start(bf16[128,1792]{1,0:T(8,128)(2,1)S(1)} %fusion.28), channel_id=1, source_target_pairs={{0,32},{16,48},{32,64},{48,80},{64,96},{80,112},{96,0},{112,16},{1... | collective-permute-start | bytes 1376264 | tf_op jit(solution)/shard_map/ppermute | solution.py:73
  135.9 10.7 %collective-permute-start.9 = (bf16[128,1792]{1,0:T(8,128)(2,1)S(1)}, bf16[128,1792]{1,0:T(8,128)(2,1)S(1)}, u32[]{:S(2)}, u32[]{:S(2)}) collective-permute-start(bf16[128,1792]{1,0:T(8,128)(2,1)S(1)} %get-tuple-element.18), channel_id=1, source_target_pairs={{0,96},{16,112},{32,0},{48,16},{64,32},{80,48},{96,64},{112,80},{1... | collective-permute-start | bytes 1376264 | tf_op jit(solution)/shard_map/ppermute | solution.py:73
  135.9 24.1 %collective-permute-start.5 = (bf16[128,1792]{1,0:T(8,128)(2,1)S(1)}, bf16[128,1792]{1,0:T(8,128)(2,1)S(1)}, u32[]{:S(2)}, u32[]{:S(2)}) collective-permute-start(bf16[128,1792]{1,0:T(8,128)(2,1)S(1)} %fusion.23), channel_id=1, source_target_pairs={{0,32},{16,48},{32,64},{48,80},{64,96},{80,112},{96,0},{112,16},{1... | collective-permute-start | bytes 1376264 | tf_op jit(solution)/shard_map/ppermute | solution.py:73
  146.5 9.6 %collective-permute-start.12 = (bf16[128,1792]{1,0:T(8,128)(2,1)S(1)}, bf16[128,1792]{1,0:T(8,128)(2,1)S(1)}, u32[]{:S(2)}, u32[]{:S(2)}) collective-permute-start(bf16[128,1792]{1,0:T(8,128)(2,1)S(1)} %get-tuple-element.21), channel_id=1, source_target_pairs={{0,96},{16,112},{32,0},{48,16},{64,32},{80,48},{96,64},{112,80},{1... | collective-permute-start | bytes 1376264 | tf_op jit(solution)/shard_map/ppermute | solution.py:73
  147.9 10.9 %collective-permute-start.3 = (bf16[128,1792]{1,0:T(8,128)(2,1)S(1)}, bf16[128,1792]{1,0:T(8,128)(2,1)S(1)}, u32[]{:S(2)}, u32[]{:S(2)}) collective-permute-start(bf16[128,1792]{1,0:T(8,128)(2,1)S(1)} %fusion.26), channel_id=1, source_target_pairs={{0,32},{16,48},{32,64},{48,80},{64,96},{80,112},{96,0},{112,16},{1... | collective-permute-start | bytes 1376264 | tf_op jit(solution)/shard_map/ppermute | solution.py:73
  158.8 10.7 %collective-permute-start.10 = (bf16[128,1792]{1,0:T(8,128)(2,1)}, bf16[128,1792]{1,0:T(8,128)(2,1)S(1)}, u32[]{:S(2)}, u32[]{:S(2)}) collective-permute-start(bf16[128,1792]{1,0:T(8,128)(2,1)} %get-tuple-element.19), channel_id=1, source_target_pairs={{0,96},{16,112},{32,0},{48,16},{64,32},{80,48},{96,64},{112,80},{1... | collective-permute-start | bytes 1376264 | tf_op jit(solution)/shard_map/ppermute | solution.py:73
  160.9 10.2 %collective-permute-start.6 = (bf16[128,1792]{1,0:T(8,128)(2,1)}, bf16[128,1792]{1,0:T(8,128)(2,1)S(1)}, u32[]{:S(2)}, u32[]{:S(2)}) collective-permute-start(bf16[128,1792]{1,0:T(8,128)(2,1)} %fusion.22), channel_id=1, source_target_pairs={{0,32},{16,48},{32,64},{48,80},{64,96},{80,112},{96,0},{112,16},{1... | collective-permute-start | bytes 1376264 | tf_op jit(solution)/shard_map/ppermute | solution.py:73
  169.5 10.8 %collective-permute-start.13 = (bf16[128,1792]{1,0:T(8,128)(2,1)}, bf16[128,1792]{1,0:T(8,128)(2,1)S(1)}, u32[]{:S(2)}, u32[]{:S(2)}) collective-permute-start(bf16[128,1792]{1,0:T(8,128)(2,1)} %get-tuple-element.22), channel_id=1, source_target_pairs={{0,96},{16,112},{32,0},{48,16},{64,32},{80,48},{96,64},{112,80},{1... | collective-permute-start | bytes 1376264 | tf_op jit(solution)/shard_map/ppermute | solution.py:73
  181.1 14.4 %collective-permute-start.14 = (bf16[256,896]{1,0:T(8,128)(2,1)S(1)}, bf16[256,896]{1,0:T(8,128)(2,1)S(1)}, u32[]{:S(2)}, u32[]{:S(2)}) collective-permute-start(bf16[256,896]{1,0:T(8,128)(2,1)S(1)} %get-tuple-element.37), channel_id=1, source_target_pairs={{0,32},{16,48},{32,64},{48,80},{64,96},{80,112},{96,0},{112,16},{1... | collective-permute-start | bytes 1376264 | tf_op jit(solution)/shard_map/ppermute | solution.py:98
  181.2 14.4 %collective-permute-start.17 = (bf16[256,896]{1,0:T(8,128)(2,1)S(1)}, bf16[256,896]{1,0:T(8,128)(2,1)S(1)}, u32[]{:S(2)}, u32[]{:S(2)}) collective-permute-start(bf16[256,896]{1,0:T(8,128)(2,1)S(1)} %get-tuple-element.38), channel_id=1, source_target_pairs={{0,96},{16,112},{32,0},{48,16},{64,32},{80,48},{96,64},{112,80},{1... | collective-permute-start | bytes 1376264 | tf_op jit(solution)/shard_map/ppermute | solution.py:98
  195.5 13.5 %collective-permute-start.15 = (bf16[256,896]{1,0:T(8,128)(2,1)S(1)}, bf16[256,896]{1,0:T(8,128)(2,1)S(1)}, u32[]{:S(2)}, u32[]{:S(2)}) collective-permute-start(bf16[256,896]{1,0:T(8,128)(2,1)S(1)} %collective-permute-done.14), channel_id=1, source_target_pairs={{0,32},{16,48},{32,64},{48,80},{64,96},{80,112},{96,0},{112,16},{1... | collective-permute-start | bytes 1376264 | tf_op jit(solution)/shard_map/ppermute | solution.py:98
  195.5 13.5 %collective-permute-start.18 = (bf16[256,896]{1,0:T(8,128)(2,1)S(1)}, bf16[256,896]{1,0:T(8,128)(2,1)S(1)}, u32[]{:S(2)}, u32[]{:S(2)}) collective-permute-start(bf16[256,896]{1,0:T(8,128)(2,1)S(1)} %collective-permute-done.17), channel_id=1, source_target_pairs={{0,96},{16,112},{32,0},{48,16},{64,32},{80,48},{96,64},{112,80},{1... | collective-permute-start | bytes 1376264 | tf_op jit(solution)/shard_map/ppermute | solution.py:98
  209.0 9.7 %collective-permute-start.16 = (bf16[256,896]{1,0:T(8,128)(2,1)S(1)}, bf16[256,896]{1,0:T(8,128)(2,1)S(1)}, u32[]{:S(2)}, u32[]{:S(2)}) collective-permute-start(bf16[256,896]{1,0:T(8,128)(2,1)S(1)} %collective-permute-done.15), channel_id=1, source_target_pairs={{0,32},{16,48},{32,64},{48,80},{64,96},{80,112},{96,0},{112,16},{1... | collective-permute-start | bytes 1376264 | tf_op jit(solution)/shard_map/ppermute | solution.py:98
  209.0 9.7 %collective-permute-start.19 = (bf16[256,896]{1,0:T(8,128)(2,1)S(1)}, bf16[256,896]{1,0:T(8,128)(2,1)S(1)}, u32[]{:S(2)}, u32[]{:S(2)}) collective-permute-start(bf16[256,896]{1,0:T(8,128)(2,1)S(1)} %collective-permute-done.18), channel_id=1, source_target_pairs={{0,96},{16,112},{32,0},{48,16},{64,32},{80,48},{96,64},{112,80},{1... | collective-permute-start | bytes 1376264 | tf_op jit(solution)/shard_map/ppermute | solution.py:98
  218.8 2.1 copy-start.9
  218.8 2.1 copy-start.4
  220.9 9.5 %collective-permute-start.20 = (bf16[1024,1792]{1,0:T(8,128)(2,1)}, bf16[1024,1792]{1,0:T(8,128)(2,1)}, u32[]{:S(2)}, u32[]{:S(2)}) collective-permute-start(bf16[1024,1792]{1,0:T(8,128)(2,1)} %bitcast.33), channel_id=1, source_target_pairs={{0,16},{16,0},{32,48},{48,32},{64,80},{80,64},{96,112},{112,96},{1... | collective-permute-start | bytes 11010056 | tf_op jit(solution)/shard_map/ppermute | solution.py:103
  221.9 2.0 copy-start.12
Sparse Core Ops, SparseCore 0:
  9.5 54.0 all-gather.1
